TPU v7x, 512 devices: a whole 4x4x16 slice. The times are simulated.
512 devices in a mesh: tile: 64 (over x, z_lo, core), loop: 8 (over y, z_hi).
Axes of the slice: x: 4, y: 4, z: 16 (z_hi: 2, z_lo: 8; z = z_hi * 8 + z_lo), core: 2. Of those that a mesh axis runs over, the one named last changes fastest.
Arguments:
- star_slot: int32 [64, 128, 128], P('tile', 'loop'), may hold values from 0 to 255
- star_block: int32 [64, 128], P('tile', 'loop'), may hold values from 0 to 1, as said below
- exposure: int32 [64, 128, 128], P('tile', 'loop'), may hold values from 0 to 511
- superpixel: int32 [64, 128, 128], P('tile', 'loop'), may hold values from 0 to 2047
- magnitude: float32 [64, 128, 128], P('tile', 'loop'), may hold values from -7 to 7
- weight: float32 [64, 128, 128], P('tile', 'loop'), may hold values from 0.25 to 4
Outputs:
- star_mags: float32 [262144], P(('tile', 'loop'))
- zero_points: float32 [4096], P('loop')
- flat_field: float32 [512, 256], P('tile')
Inputs may be any that keep to these rules, and one draw needn't show every extreme that they name: `star_block`: observation blocks of one device at positions 2 * o to 2 * o + 1 of its 16 blocks observe stars of the star shard held by loop index o of the same tile.
All inputs are finite; a program needn't handle non-finite values.
Results may differ from a plain program's by a relative error of at most 0.00022.
Values sent between devices are 32-bit elements; how exact they have to be, the bound alone decides.
No kernel may reach another device: no remote copies, remote signals or barrier semaphores. Data moves between devices by JAX's collectives and lax.ppermute only.
A program may use at most 64 MiB of HBM per device.

v0:
```python
import functools

import jax
import jax.numpy as jnp
from jax import lax
from jax.sharding import Mesh
from jax.sharding import PartitionSpec as P

FC = 256
ROWS_DEV = 8
SBLK_DEV = 2
EXP_DEV = 512
STAR_BLK = 256
ITERS = 2
LOOP = ("loop_0", "loop_1")
TILE = ("tile_0", "tile_1", "tile_2")
TILE_LOOP = ("tile_0", "tile_1", "tile_2", "loop_0", "loop_1")


SMOOTH = 2.0
RIDGE = 0.5


def sent_to_all(array, axis):
    peers = lax.axis_size(axis)
    return lax.all_to_all(
        jnp.broadcast_to(array[None], (peers, *array.shape)), axis, 0, 0, tiled=True
    )


def over_copies(array, axis):
    return sent_to_all(array, axis).sum(axis=0)


def in_blocks(array, dim, peers):
    before, after = (array.shape[:dim], array.shape[dim + 1 :])
    return jnp.moveaxis(array.reshape(*before, peers, -1, *after), dim, 0)


def summed_on_arrival(array, axis, dim):
    peers = lax.axis_size(axis)
    pieces = lax.all_to_all(in_blocks(array, dim, peers), axis, 0, 0, tiled=True)
    return jnp.sum(pieces, axis=0)


def laid_out(pieces, dim):
    dims = list(pieces.shape[1:])
    dims[dim] *= pieces.shape[0]
    return jnp.moveaxis(pieces, 0, dim).reshape(dims)


def gathered_copies(array, axis, dim):
    pieces = sent_to_all(array, axis)
    return laid_out(pieces, dim)


def extended(array, sides, width):
    for axis, dim in sides:
        peers, length = (lax.axis_size(axis), array.shape[dim])
        up = [(i, (i + 1) % peers) for i in range(peers - 1)]
        down = [(j, i) for i, j in up]
        last = lax.slice_in_dim(array, length - width, length, axis=dim)
        leading = lax.slice_in_dim(array, 0, width, axis=dim)
        before = lax.ppermute(last, axis, up)
        after = lax.ppermute(leading, axis, down)
        array = jnp.concatenate([before, array, after], axis=dim)
    return array


def by_axis(array, axes):
    return functools.reduce(lax.psum, axes, array)


def scatter_add(values, targets, total):
    return jax.ops.segment_sum(values.reshape(-1), targets.reshape(-1), num_segments=total)


def combine(vector, other, factor):
    return jax.tree.map(lambda values, others: values + factor * others, vector, other)


def on_device(star_slot, star_block, exposure, superpixel, magnitude, weight):
    loop_size = lax.axis_size(LOOP)
    loop_rank = lax.axis_index(LOOP)
    tile_rank = lax.axis_index(TILE)
    stars_dev = SBLK_DEV * STAR_BLK
    pixels = ROWS_DEV * FC
    star_local = (star_block[0][:, None] * STAR_BLK + star_slot[0]).reshape(loop_size, -1)
    expo_ids = exposure[0].reshape(loop_size, -1)
    pixel_ids = superpixel[0].reshape(loop_size, -1)
    weights = weight[0].reshape(loop_size, -1)
    magnitudes = magnitude[0].reshape(loop_size, -1)
    spread = star_local + lax.broadcasted_iota(jnp.int32, star_local.shape, 0) * stars_dev

    def exposure_total(parts):
        return jax.tree.map(lambda part: over_copies(part, TILE), parts)

    def flat_total(parts):
        return jax.tree.map(lambda part: over_copies(part, LOOP), parts)

    weighted = weights * magnitudes
    rhs_stars, count_stars = (
        summed_on_arrival(scatter_add(weighted, spread, loop_size * stars_dev), LOOP, 0),
        summed_on_arrival(scatter_add(weights, spread, loop_size * stars_dev), LOOP, 0),
    )
    rhs_expo, count_expo = exposure_total(
        (scatter_add(weighted, expo_ids, EXP_DEV), scatter_add(weights, expo_ids, EXP_DEV))
    )
    rhs_flat, count_flat = flat_total(
        (scatter_add(weighted, pixel_ids, pixels), scatter_add(weights, pixel_ids, pixels))
    )
    right_side = (rhs_stars, rhs_expo, rhs_flat.reshape(ROWS_DEV, FC))
    diagonal = (
        count_stars + RIDGE,
        count_expo + RIDGE,
        count_flat.reshape(ROWS_DEV, FC) + (4.0 * SMOOTH + RIDGE),
    )

    def operate(vector):
        star_dir, expo_dir, flat_dir = vector
        flat_line = flat_dir.reshape(-1)
        piece = gathered_copies(star_dir, LOOP, 0)
        shard_count = piece.shape[0] // stars_dev
        nearby = star_local
        nearby = nearby + lax.broadcasted_iota(jnp.int32, nearby.shape, 0) * stars_dev
        weighted_fit = weights * (piece[nearby] + expo_dir[expo_ids] + flat_line[pixel_ids])
        partial_value = scatter_add(weighted_fit, nearby, shard_count * stars_dev)
        partial_value, expo_sum, flat_sum = (
            partial_value,
            scatter_add(weighted_fit, expo_ids, EXP_DEV),
            scatter_add(weighted_fit, pixel_ids, pixels),
        )
        star_sum = summed_on_arrival(partial_value, LOOP, 0)
        (expo_sum,) = exposure_total((expo_sum,))
        (flat_sum,) = flat_total((flat_sum,))
        padded = extended(flat_dir, ((TILE, 0),), 1)
        columns = jnp.pad(flat_dir, ((0, 0), (1, 1)))
        beside = padded[2:] + padded[:-2] + columns[:, 2:] + columns[:, :-2]
        return (
            star_sum + RIDGE * star_dir,
            expo_sum + RIDGE * expo_dir,
            flat_sum.reshape(ROWS_DEV, FC) + SMOOTH * (4.0 * flat_dir - beside) + RIDGE * flat_dir,
        )

    def inner_local(first_vec, second_vec):
        star_part = jnp.sum(first_vec[0] * second_vec[0])
        expo_part = jnp.where(tile_rank == 0, jnp.sum(first_vec[1] * second_vec[1]), 0.0)
        flat_part = jnp.where(loop_rank == 0, jnp.sum(first_vec[2] * second_vec[2]), 0.0)
        return star_part + expo_part + flat_part

    def divide(vector):
        return jax.tree.map(lambda values, scales: values / scales, vector, diagonal)

    solution = jax.tree.map(jnp.zeros_like, right_side)
    residual = right_side

    def paired(current, precon, image):
        return (
            by_axis(inner_local(current, precon), TILE_LOOP),
            by_axis(inner_local(image, precon), TILE_LOOP),
        )

    precon = divide(residual)
    image = operate(precon)
    norm_now, curvature = paired(residual, precon, image)
    step_size = norm_now / curvature
    direction, along = (precon, image)
    for iteration in range(ITERS):
        solution = combine(solution, direction, step_size)
        residual = combine(residual, along, -step_size)
        if iteration + 1 < ITERS:
            precon = divide(residual)
            image = operate(precon)
            norm_next, curvature = paired(residual, precon, image)
            ratio = norm_next / norm_now
            step_size = norm_next / (curvature - ratio * norm_next / step_size)
            direction = combine(precon, direction, ratio)
            along = combine(image, along, ratio)
            norm_now = norm_next
    return (solution[0], solution[1], solution[2])


def solution(mesh):
    split = Mesh(
        mesh.devices.reshape(4, 8, 2, 4, 2), ("tile_0", "tile_1", "tile_2", "loop_0", "loop_1")
    )
    placed = (
        P(TILE, LOOP, None),
        P(TILE, LOOP),
        P(TILE, LOOP, None),
        P(TILE, LOOP, None),
        P(TILE, LOOP, None),
        P(TILE, LOOP, None),
    )
    return jax.shard_map(
        on_device,
        mesh=split,
        in_specs=placed,
        out_specs=(P(TILE_LOOP), P(LOOP), P(TILE, None)),
        check_vma=False,
    )
```

profile of v0, /device:TPU:1, one launch (start us, length us, event | category | flops | bytes accessed | tf_op | source)
XLA Modules:
  0.0 629.4 jit_solution(2819419280737360786)
XLA Ops:
  2.2 15.3 %scatter_custom_fusion = f32[4096]{0:T(1024)} fusion(s32[2048]{0:T(1024)S(1)} %bitcast.63, f32[2048]{0:T(1024)S(1)} %bitcast_multiply_fusion, f32[]{:T(128)} %constant.16.clone.1), kind=kCustom, calls=%fused_computation.64 | custom fusion | flops 2048 | bytes 16388 | tf_op jit(solution)/shard_map/scatter-add | solution.py:75
  17.4 18.3 %all-to-all-start = ((f32[8,1,512]{2,1,0:T(1,128)}), f32[8,1,512]{2,1,0:T(1,128)S(1)}, u32[]{:S(2)}, u32[]{:S(2)}) async-start(f32[8,1,512]{2,1,0:T(1,128)} %bitcast.5), calls=%async_computation | async-start | bytes 32768 | tf_op jit(solution)/shard_map/all_to_all | solution.py:42
  35.7 15.3 %scatter_custom_fusion.1 = f32[4096]{0:T(1024)} fusion(s32[2048]{0:T(1024)S(1)} %bitcast.64, f32[2048]{0:T(1024)S(1)} %bitcast.46, f32[]{:T(128)} %constant.16.clone.1), kind=kCustom, calls=%fused_computation.62 | custom fusion | flops 2048 | bytes 16388 | tf_op jit(solution)/shard_map/scatter-add | solution.py:75
  50.9 13.9 %all-to-all-start.1 = ((f32[8,1,512]{2,1,0:T(1,128)}), f32[8,1,512]{2,1,0:T(1,128)S(1)}, u32[]{:S(2)}, u32[]{:S(2)}) async-start(f32[8,1,512]{2,1,0:T(1,128)} %bitcast.6), calls=%async_computation.1 | async-start | bytes 32768 | tf_op jit(solution)/shard_map/all_to_all | solution.py:42
  64.8 13.7 %all-to-all-done.1 = f32[8,1,512]{2,1,0:T(1,128)S(1)} async-done(((f32[8,1,512]{2,1,0:T(1,128)}), f32[8,1,512]{2,1,0:T(1,128)S(1)}, u32[]{:S(2)}, u32[]{:S(2)}) %all-to-all-start.1) | async-done | bytes 16416 | tf_op jit(solution)/shard_map/all_to_all | solution.py:42
  135.3 14.7 %scatter_custom_fusion.2 = f32[512]{0:T(512)S(1)} fusion(s32[2048]{0:T(1024)S(1)} %bitcast.59, f32[2048]{0:T(1024)S(1)} %bitcast_multiply_fusion, f32[]{:T(128)} %constant.16.clone.1), kind=kCustom, calls=%fused_computation.105 | custom fusion | flops 2048 | bytes 2052 | tf_op jit(solution)/shard_map/scatter-add | solution.py:75
  162.5 14.7 %scatter_custom_fusion.3 = f32[512]{0:T(512)S(1)} fusion(s32[2048]{0:T(1024)S(1)} %bitcast.60, f32[2048]{0:T(1024)S(1)} %bitcast.48, f32[]{:T(128)} %constant.16.clone.1), kind=kCustom, calls=%fused_computation.103 | custom fusion | flops 2048 | bytes 2052 | tf_op jit(solution)/shard_map/scatter-add | solution.py:75
  177.9 13.1 %all-to-all-start.3 = ((f32[64,1,512]{2,1,0:T(1,128)}), f32[64,1,512]{2,1,0:T(1,128)S(1)}, u32[]{:S(2)}, u32[]{:S(2)}) async-start(f32[64,1,512]{2,1,0:T(1,128)} %broadcast_in_dim.21), calls=%async_computation.3 | async-start | bytes 262144 | tf_op jit(solution)/shard_map/all_to_all | solution.py:26
  191.0 11.8 %gather_fusion = f32[2048]{0:T(1024)S(1)} fusion(f32[4096]{0:T(1024)S(1)} %bitcast.43, s32[2048]{0:T(1024)S(1)} %broadcast_clamp_fusion.2), kind=kCustom, calls=%fused_computation | custom fusion | bytes 24576 | tf_op jit(solution)/shard_map/gather | solution.py:126
  215.6 13.2 %gather_fusion.1 = f32[2048]{0:T(1024)S(1)} fusion(f32[512]{0:T(512)S(1)} %add_divide_fusion.1, s32[2048]{0:T(1024)S(1)} %broadcast_clamp_fusion.1), kind=kCustom, calls=%fused_computation.1 | custom fusion | bytes 24576 | tf_op jit(solution)/shard_map/gather | solution.py:126
  228.8 15.3 %scatter_custom_fusion.6 = f32[4096]{0:T(1024)} fusion(s32[2048]{0:T(1024)S(1)} %bitcast.65, f32[2048]{0:T(1024)S(1)} %add_multiply_fusion.1, f32[]{:T(128)} %constant.16.clone.1), kind=kCustom, calls=%fused_computation.60 | custom fusion | flops 2048 | bytes 16388 | tf_op jit(solution)/shard_map/scatter-add | solution.py:75
  244.1 14.1 %all-to-all-start.7 = ((f32[8,1,512]{2,1,0:T(1,128)}), f32[8,1,512]{2,1,0:T(1,128)S(1)}, u32[]{:S(2)}, u32[]{:S(2)}) async-start(f32[8,1,512]{2,1,0:T(1,128)} %bitcast.11), calls=%async_computation.7 | async-start | bytes 32768 | tf_op jit(solution)/shard_map/all_to_all | solution.py:42
  284.2 14.7 %scatter_custom_fusion.7 = f32[512]{0:T(512)S(1)} fusion(s32[2048]{0:T(1024)S(1)} %bitcast.61, f32[2048]{0:T(1024)S(1)} %add_multiply_fusion.1, f32[]{:T(128)} %constant.16.clone.1), kind=kCustom, calls=%fused_computation.101 | custom fusion | flops 2048 | bytes 2052 | tf_op jit(solution)/shard_map/scatter-add | solution.py:75
  299.6 14.2 %all-to-all-start.8 = ((f32[64,1,512]{2,1,0:T(1,128)}), f32[64,1,512]{2,1,0:T(1,128)S(1)}, u32[]{:S(2)}, u32[]{:S(2)}) async-start(f32[64,1,512]{2,1,0:T(1,128)} %broadcast_in_dim.25), calls=%async_computation.8 | async-start | bytes 262144 | tf_op jit(solution)/shard_map/all_to_all | solution.py:26
  340.8 30.1 %all-reduce.3 = (f32[]{:T(128)}, f32[]{:T(128)}) all-reduce(f32[]{:T(128)} %get-tuple-element.23, f32[]{:T(128)} %get-tuple-element.24), channel_id=1, replica_groups=mesh['tile_0'=4,'tile_1'=8,'tile_2'=2,'loop_0'=4,'loop_1'=2] {'tile_1'}, use_global_device_ids=true, to_apply=%region_16.0 | all-reduce | flops 2 | bytes 16 | tf_op jit(solution)/shard_map/psum | solution.py:71
  390.2 13.1 %all-reduce.9 = (f32[]{:T(128)}, f32[]{:T(128)}) all-reduce(f32[]{:T(128)} %get-tuple-element.19, f32[]{:T(128)} %get-tuple-element.20), channel_id=1, replica_groups=mesh['tile_0'=4,'tile_1'=8,'tile_2'=2,'loop_0'=4,'loop_1'=2] {'loop_1'}, use_global_device_ids=true, to_apply=%region_19.20 | all-reduce | flops 2 | bytes 16 | tf_op jit(solution)/shard_map/psum | solution.py:71
  416.8 13.2 %gather_fusion.4 = f32[2048]{0:T(1024)S(1)} fusion(f32[512]{0:T(512)S(1)} %get-tuple-element.33, s32[2048]{0:T(1024)S(1)} %broadcast_clamp_fusion.1), kind=kCustom, calls=%fused_computation.4 | custom fusion | bytes 24576 | tf_op jit(solution)/shard_map/gather | solution.py:126
  430.0 11.8 %gather_fusion.5 = f32[2048]{0:T(1024)S(1)} fusion(f32[2048]{0:T(1024)S(1)} %bitcast.42, s32[2048]{0:T(1024)S(1)} %broadcast_clamp_fusion), kind=kCustom, calls=%fused_computation.5 | custom fusion | bytes 24576 | tf_op jit(solution)/shard_map/gather | solution.py:126
  441.8 11.8 %gather_fusion.3 = f32[2048]{0:T(1024)S(1)} fusion(f32[4096]{0:T(1024)S(1)} %bitcast.44, s32[2048]{0:T(1024)S(1)} %broadcast_clamp_fusion.2), kind=kCustom, calls=%fused_computation.3 | custom fusion | bytes 24576 | tf_op jit(solution)/shard_map/gather | solution.py:126
  453.6 15.3 %scatter_custom_fusion.9 = f32[4096]{0:T(1024)} fusion(s32[2048]{0:T(1024)S(1)} %bitcast.66, f32[2048]{0:T(1024)S(1)} %add_multiply_fusion, f32[]{:T(128)} %constant.16.clone.1), kind=kCustom, calls=%fused_computation.58 | custom fusion | flops 2048 | bytes 16388 | tf_op jit(solution)/shard_map/scatter-add | solution.py:75
  468.9 13.9 %all-to-all-start.11 = ((f32[8,1,512]{2,1,0:T(1,128)}), f32[8,1,512]{2,1,0:T(1,128)S(1)}, u32[]{:S(2)}, u32[]{:S(2)}) async-start(f32[8,1,512]{2,1,0:T(1,128)} %bitcast.13), calls=%async_computation.11 | async-start | bytes 32768 | tf_op jit(solution)/shard_map/all_to_all | solution.py:42
  508.7 14.7 %scatter_custom_fusion.10 = f32[512]{0:T(512)S(1)} fusion(s32[2048]{0:T(1024)S(1)} %bitcast.62, f32[2048]{0:T(1024)S(1)} %add_multiply_fusion, f32[]{:T(128)} %constant.16.clone.1), kind=kCustom, calls=%fused_computation.99 | custom fusion | flops 2048 | bytes 2052 | tf_op jit(solution)/shard_map/scatter-add | solution.py:75
  561.2 29.6 %all-reduce.2 = (f32[]{:T(128)}, f32[]{:T(128)}) all-reduce(f32[]{:T(128)} %get-tuple-element.21, f32[]{:T(128)} %get-tuple-element.22), channel_id=1, replica_groups=mesh['tile_0'=4,'tile_1'=8,'tile_2'=2,'loop_0'=4,'loop_1'=2] {'tile_1'}, use_global_device_ids=true, to_apply=%region_38.39 | all-reduce | flops 2 | bytes 16 | tf_op jit(solution)/shard_map/psum | solution.py:71
  610.6 13.1 %all-reduce.8 = (f32[]{:T(128)}, f32[]{:T(128)}) all-reduce(f32[]{:T(128)} %get-tuple-element.17, f32[]{:T(128)} %get-tuple-element.18), channel_id=1, replica_groups=mesh['tile_0'=4,'tile_1'=8,'tile_2'=2,'loop_0'=4,'loop_1'=2] {'loop_1'}, use_global_device_ids=true, to_apply=%region_41.42 | all-reduce | flops 2 | bytes 16 | tf_op jit(solution)/shard_map/psum | solution.py:71
  (119 shorter events, 246.2 us)
Async XLA Ops:
  0.6 0.7 copy-start.5
  0.7 0.7 copy-start
  0.7 0.7 copy-start.2
  1.4 0.7 copy-start.1
  17.4 33.5 %all-to-all-start = ((f32[8,1,512]{2,1,0:T(1,128)}), f32[8,1,512]{2,1,0:T(1,128)S(1)}, u32[]{:S(2)}, u32[]{:S(2)}) async-start(f32[8,1,512]{2,1,0:T(1,128)} %bitcast.5), calls=%async_computation | async-start | bytes 32768 | tf_op jit(solution)/shard_map/all_to_all | solution.py:42
  50.9 27.6 %all-to-all-start.1 = ((f32[8,1,512]{2,1,0:T(1,128)}), f32[8,1,512]{2,1,0:T(1,128)S(1)}, u32[]{:S(2)}, u32[]{:S(2)}) async-start(f32[8,1,512]{2,1,0:T(1,128)} %bitcast.6), calls=%async_computation.1 | async-start | bytes 32768 | tf_op jit(solution)/shard_map/all_to_all | solution.py:42
  79.2 3.5 copy-start.3
  79.2 17.2 %all-to-all-start.6 = ((f32[8,1,512]{2,1,0:T(1,128)}), f32[8,1,512]{2,1,0:T(1,128)S(1)}, u32[]{:S(2)}, u32[]{:S(2)}) async-start(f32[8,1,512]{2,1,0:T(1,128)} %broadcast_in_dim.24), calls=%async_computation.6 | async-start | bytes 32768 | tf_op jit(solution)/shard_map/all_to_all | solution.py:26
  97.1 25.5 %all-to-all-start.4 = ((f32[8,1,2048]{2,1,0:T(1,128)}), f32[8,1,2048]{2,1,0:T(1,128)S(1)}, u32[]{:S(2)}, u32[]{:S(2)}) async-start(f32[8,1,2048]{2,1,0:T(1,128)} %broadcast_in_dim.22), calls=%async_computation.4 | async-start | bytes 131072 | tf_op jit(solution)/shard_map/all_to_all | solution.py:26
  123.2 26.8 %all-to-all-start.5 = ((f32[8,1,2048]{2,1,0:T(1,128)}), f32[8,1,2048]{2,1,0:T(1,128)S(1)}, u32[]{:S(2)}, u32[]{:S(2)}) async-start(f32[8,1,2048]{2,1,0:T(1,128)} %broadcast_in_dim.23), calls=%async_computation.5 | async-start | bytes 131072 | tf_op jit(solution)/shard_map/all_to_all | solution.py:26
  134.6 0.7 copy-start.4
  150.7 26.5 %all-to-all-start.2 = ((f32[64,1,512]{2,1,0:T(1,128)}), f32[64,1,512]{2,1,0:T(1,128)S(1)}, u32[]{:S(2)}, u32[]{:S(2)}) async-start(f32[64,1,512]{2,1,0:T(1,128)} %broadcast_in_dim.20), calls=%async_computation.2 | async-start | bytes 262144 | tf_op jit(solution)/shard_map/all_to_all | solution.py:26
  177.9 37.5 %all-to-all-start.3 = ((f32[64,1,512]{2,1,0:T(1,128)}), f32[64,1,512]{2,1,0:T(1,128)S(1)}, u32[]{:S(2)}, u32[]{:S(2)}) async-start(f32[64,1,512]{2,1,0:T(1,128)} %broadcast_in_dim.21), calls=%async_computation.3 | async-start | bytes 262144 | tf_op jit(solution)/shard_map/all_to_all | solution.py:26
  244.1 27.9 %all-to-all-start.7 = ((f32[8,1,512]{2,1,0:T(1,128)}), f32[8,1,512]{2,1,0:T(1,128)S(1)}, u32[]{:S(2)}, u32[]{:S(2)}) async-start(f32[8,1,512]{2,1,0:T(1,128)} %bitcast.11), calls=%async_computation.7 | async-start | bytes 32768 | tf_op jit(solution)/shard_map/all_to_all | solution.py:42
  272.6 26.2 %all-to-all-start.9 = ((f32[8,1,2048]{2,1,0:T(1,128)}), f32[8,1,2048]{2,1,0:T(1,128)S(1)}, u32[]{:S(2)}, u32[]{:S(2)}) async-start(f32[8,1,2048]{2,1,0:T(1,128)} %broadcast_in_dim.26), calls=%async_computation.9 | async-start | bytes 131072 | tf_op jit(solution)/shard_map/all_to_all | solution.py:26
  299.6 28.8 %all-to-all-start.8 = ((f32[64,1,512]{2,1,0:T(1,128)}), f32[64,1,512]{2,1,0:T(1,128)S(1)}, u32[]{:S(2)}, u32[]{:S(2)}) async-start(f32[64,1,512]{2,1,0:T(1,128)} %broadcast_in_dim.25), calls=%async_computation.8 | async-start | bytes 262144 | tf_op jit(solution)/shard_map/all_to_all | solution.py:26
  313.8 6.9 %collective-permute-start = (f32[1,256]{1,0:T(1,128)S(1)}, f32[1,256]{1,0:T(1,128)S(1)}, u32[]{:S(2)}, u32[]{:S(2)}) collective-permute-start(f32[1,256]{1,0:T(1,128)S(1)} %get-tuple-element.43), channel_id=1, source_target_pairs={{8,0},{16,8},{24,16},{32,24},{40,32},{48,40},{56,48},{64,56},{72,6... | collective-permute-start | bytes 3080 | tf_op jit(solution)/shard_map/ppermute | solution.py:65
  316.2 4.6 collective-permute-start.1
  405.3 36.5 %all-to-all-start.10 = ((f32[8,1,512]{2,1,0:T(1,128)}), f32[8,1,512]{2,1,0:T(1,128)S(1)}, u32[]{:S(2)}, u32[]{:S(2)}) async-start(f32[8,1,512]{2,1,0:T(1,128)} %broadcast_in_dim.27), calls=%async_computation.10 | async-start | bytes 32768 | tf_op jit(solution)/shard_map/all_to_all | solution.py:26
  468.9 27.6 %all-to-all-start.11 = ((f32[8,1,512]{2,1,0:T(1,128)}), f32[8,1,512]{2,1,0:T(1,128)S(1)}, u32[]{:S(2)}, u32[]{:S(2)}) async-start(f32[8,1,512]{2,1,0:T(1,128)} %bitcast.13), calls=%async_computation.11 | async-start | bytes 32768 | tf_op jit(solution)/shard_map/all_to_all | solution.py:42
  497.2 26.2 %all-to-all-start.13 = ((f32[8,1,2048]{2,1,0:T(1,128)}), f32[8,1,2048]{2,1,0:T(1,128)S(1)}, u32[]{:S(2)}, u32[]{:S(2)}) async-start(f32[8,1,2048]{2,1,0:T(1,128)} %broadcast_in_dim.29), calls=%async_computation.13 | async-start | bytes 131072 | tf_op jit(solution)/shard_map/all_to_all | solution.py:26
  524.1 24.1 %all-to-all-start.12 = ((f32[64,1,512]{2,1,0:T(1,128)}), f32[64,1,512]{2,1,0:T(1,128)S(1)}, u32[]{:S(2)}, u32[]{:S(2)}) async-start(f32[64,1,512]{2,1,0:T(1,128)} %broadcast_in_dim.28), calls=%async_computation.12 | async-start | bytes 262144 | tf_op jit(solution)/shard_map/all_to_all | solution.py:26
  533.6 6.3 %collective-permute-start.2 = (f32[1,256]{1,0:T(1,128)S(1)}, f32[1,256]{1,0:T(1,128)S(1)}, u32[]{:S(2)}, u32[]{:S(2)}) collective-permute-start(f32[1,256]{1,0:T(1,128)S(1)} %get-tuple-element.41), channel_id=1, source_target_pairs={{8,0},{16,8},{24,16},{32,24},{40,32},{48,40},{56,48},{64,56},{72,6... | collective-permute-start | bytes 3080 | tf_op jit(solution)/shard_map/ppermute | solution.py:65
  536.0 4.0 collective-permute-start.3
where the time goes:
time: 633 us; the launch traced here: 629 us
  starting transfers between devices  181 us (29%)
  other arithmetic  172 us (27%)
  blocking collectives  144 us (23%)
  local copies, waits for them, and re-layouts  82.5 us (13%)
  waiting for transfers between devices  36.3 us (6%)
  between operations  14.7 us (2%)
    scatter-add x12, other arithmetic, scatter_add(): jax.ops.segment_sum(values.reshape(-1), targets.reshape(-1), num_segments...  165 us
    psum x10, blocking collectives, by_axis(): return functools.reduce(lax.psum, axes, array)  144 us
    all_to_all x10, starting transfers between devices, sent_to_all(): lax.all_to_all(jnp.broadcast_to(array[None], (peers, *array.shape)), axis...  109 us
    all_to_all x4, starting transfers between devices, summed_on_arrival(): lax.all_to_all(in_blocks(array, dim, peers), axis, 0, 0, tiled=True)  60.1 us
    gather x2, local copies, waits for them, and re-layouts, operate(): expo_dir[expo_ids]  26.4 us
    gather x2, local copies, waits for them, and re-layouts, operate(): piece[nearby] + expo_dir[expo_ids] + flat_line[pixel_ids]  23.6 us
    gather x2, local copies, waits for them, and re-layouts, operate(): flat_line[pixel_ids]  23.6 us
    all_to_all x4, waiting for transfers between devices, summed_on_arrival(): lax.all_to_all(in_blocks(array, dim, peers), axis, 0, 0, tiled=True)  18.7 us
  transfers between devices with their start and end apart: 18, of which 7 were waited for; matrix products, arithmetic and copies ran while one was open for 27% of the time, Pallas kernels for 0%

commit v1 on v0

v1 whole, which is shorter than its diff:
```python
import jax
import jax.numpy as jnp
from jax import lax
from jax.experimental import pallas as pl
from jax.experimental.pallas import tpu as pltpu
from jax.sharding import Mesh
from jax.sharding import PartitionSpec as P

SMOOTH = 2.0
RIDGE = 0.5
LO = 128
NX, NZ, NC, NY, NH = 4, 8, 2, 4, 2
ALL = ("x", "zl", "c", "y", "zh")
F32 = jnp.float32
I32 = jnp.int32
BF16 = jnp.bfloat16
NT = (((1,), (1,)), ((), ()))
NN = (((1,), (0,)), ((), ()))


def split3(v):
    first = v.astype(BF16).astype(F32)
    rest = v - first
    second = rest.astype(BF16).astype(F32)
    return first, second, rest - second


def pad16(rows):
    count = sum(row.shape[0] for row in rows)
    if count % 16:
        rows = rows + [jnp.zeros((16 - count % 16, rows[0].shape[1]), F32)]
    return jnp.concatenate(rows, axis=0).astype(BF16)


def onehot(lo):
    n = lo.shape[1]
    return jnp.where(lax.broadcasted_iota(I32, (LO, n), 0) == lo, 1.0, 0.0).astype(BF16)


def scatter(values, hi, high, hot):
    mask = lax.broadcasted_iota(I32, (high, hi.shape[1]), 0) == hi
    rows = [jnp.where(mask, part, 0.0) for v in values for part in split3(v)]
    sums = lax.dot_general(pad16(rows), hot, NT, preferred_element_type=F32)
    return [
        sums[3 * high * i : 3 * high * i + high]
        + sums[3 * high * i + high : 3 * high * i + 2 * high]
        + sums[3 * high * i + 2 * high : 3 * high * (i + 1)]
        for i in range(len(values))
    ]


def gather(table, hi, hot):
    high = table.shape[0]
    parts = lax.dot_general(pad16(list(split3(table))), hot, NN, preferred_element_type=F32)
    found = parts[:high] + parts[high : 2 * high] + parts[2 * high : 3 * high]
    mask = lax.broadcasted_iota(I32, found.shape, 0) == hi
    return jnp.sum(jnp.where(mask, found, 0.0), axis=0, keepdims=True)


def row_iota(shape):
    return lax.broadcasted_iota(I32, shape, 0)


def pack_kernel(block_ref, slot_ref, expo_ref, pix_ref, mag_ref, w_ref, out_ref):
    rows = row_iota((8, LO))
    for r in range(16):
        star = slot_ref[r : r + 1, :] + (block_ref[0, r] * 256 + ((r // 2) % 2) * 512)
        pix = pix_ref[r : r + 1, :]
        pix = (((pix >> 7) & 1) * 8 + (pix >> 8)) * LO + (pix & 127)
        w = w_ref[r : r + 1, :]
        fields = (
            star.astype(F32),
            pix.astype(F32),
            expo_ref[r : r + 1, :].astype(F32),
            w,
            w * mag_ref[r : r + 1, :],
        )
        tile = jnp.zeros((8, LO), F32)
        for f, field in enumerate(fields):
            tile = jnp.where(rows == f, field, tile)
        out_ref[r // 4, :, (r % 4) * LO : (r % 4 + 1) * LO] = tile


def expo_kernel(obs_ref, out_ref):
    x = jnp.concatenate([obs_ref[k] for k in range(4)], axis=1)
    e = x[2:3].astype(I32)
    weighted, count = scatter([x[4:5], x[3:4]], e >> 7, 8, onehot(e & 127))
    both = jnp.where(row_iota((8, LO)) < 4, weighted, pltpu.roll(count, 4, 0))
    for peer in range(16):
        out_ref[peer] = both


def fields_of(obs_ref, k):
    x = jnp.concatenate([obs_ref[g, k] for g in range(8)], axis=1)
    ids = x.astype(I32)
    return ids[0:1], ids[1:2], ids[2:3], x[3:4], x[4:5]


def own_fields(obs_ref, y, k):
    x = jnp.concatenate([obs_ref[2 * y + rel, k] for rel in range(2)], axis=1)
    ids = x.astype(I32)
    return ids[0:1], ids[1:2], ids[2:3], x[3:4]


def tile_kernel(
    pos_ref, obs_ref, g0s_ref, ds_ref, cs_ref, g0f_ref, df_ref, cf_ref, ru_ref, top_ref, bot_ref,
    hot_s, hot_p, fit_ref,
):
    g0f_ref[...] = jnp.zeros((16, LO), F32)
    df_ref[...] = jnp.zeros((16, LO), F32)

    def sums(k, carry):
        s, p, e, w, wm = fields_of(obs_ref, k)
        hs = onehot(s & 127)
        hp = onehot(p & 127)
        hot_s[k] = hs
        hot_p[k] = hp
        weighted, count = scatter([wm, w], s >> 7, 8, hs)
        diag = count + RIDGE
        g0s_ref[k] = weighted / diag
        ds_ref[k] = diag
        weighted, count = scatter([wm, w], p >> 7, 16, hp)
        g0f_ref[...] += weighted
        df_ref[...] += count
        return carry

    lax.fori_loop(0, 4, sums, 0)
    diag = df_ref[...] + (4.0 * SMOOTH + RIDGE)
    g0f = g0f_ref[...] / diag
    df_ref[...] = diag
    g0f_ref[...] = g0f
    top_ref[...] = jnp.concatenate([g0f[0:1], g0f[8:9]], axis=0)
    bot_ref[...] = jnp.concatenate([g0f[7:8], g0f[15:16]], axis=0)
    cf_ref[...] = jnp.zeros((16, LO), F32)

    def couple(k, carry):
        s, p, e, w, wm = fields_of(obs_ref, k)
        hs = hot_s[k]
        hp = hot_p[k]
        from_star = gather(g0s_ref[k], s >> 7, hs)
        from_flat = gather(g0f_ref[...], p >> 7, hp)
        (cs_ref[k],) = scatter([w * from_flat], s >> 7, 8, hs)
        (added,) = scatter([w * from_star], p >> 7, 16, hp)
        cf_ref[...] += added
        fit_ref[k] = w * (from_star + from_flat)
        return carry

    lax.fori_loop(0, 4, couple, 0)
    y = pos_ref[0]
    total = jnp.zeros((8, LO), F32)
    for k in range(4):
        s, p, e, w = own_fields(obs_ref, y, k)
        hi = (e >> 7) + (lax.broadcasted_iota(I32, e.shape, 1) >> 9) * 4
        fit = fit_ref[k, :, pl.ds(pl.multiple_of(y * 1024, 1024), 1024)]
        (added,) = scatter([fit], hi, 8, onehot(e & 127))
        total += added
    ru_ref[...] = total


def pair_rows(first, second):
    low = row_iota((8, LO)) < 4
    return jnp.where(low, first, pltpu.roll(second, 4, 0)), jnp.where(
        low, pltpu.roll(first, 4, 0), second
    )


def beside(flat, above, below):
    left, right = flat[:8], flat[8:]
    rows = row_iota((8, LO))
    lanes = lax.broadcasted_iota(I32, (8, LO), 1)
    out = []
    left_up, right_up = pltpu.roll(left, 1, 1), pltpu.roll(right, 1, 1)
    left_down, right_down = pltpu.roll(left, 127, 1), pltpu.roll(right, 127, 1)
    sides = (
        jnp.where(lanes == 0, 0.0, left_up) + jnp.where(lanes == 127, right_down, left_down),
        jnp.where(lanes == 0, left_up, right_up) + jnp.where(lanes == 127, 0.0, right_down),
    )
    for i, half in enumerate((left, right)):
        upper = jnp.where(rows == 0, above[i : i + 1], pltpu.roll(half, 1, 0))
        lower = jnp.where(rows == 7, below[i : i + 1], pltpu.roll(half, 7, 0))
        out.append(sides[i] + upper + lower)
    return jnp.concatenate(out, axis=0)


def expo_apply_kernel(
    obs_ref, expo_ref, g0f_ref, cs_ref, cf_ref, ds_ref, df_ref, above_ref, below_ref,
    cs_out, ys_out, cf_out, yf_out, g0z_out, dz_out, top_out,
):
    for y in range(4):
        part = expo_ref[y]
        for xc in range(1, 8):
            part = part + expo_ref[xc * 4 + y]
        weighted, count = pair_rows(part[:8], part[8:])
        diag = count + RIDGE
        g0z_out[y] = weighted / diag
        dz_out[y] = diag
    table = jnp.concatenate([g0z_out[y] for y in range(4)], axis=0)
    cf_out[...] = cf_ref[...]

    def apply(k, carry):
        s, p, e, w, wm = fields_of(obs_ref, k)
        hi = (e >> 7) + (lax.broadcasted_iota(I32, e.shape, 1) >> 9) * 4
        fit = w * gather(table, hi, onehot(e & 127))
        (added,) = scatter([fit], s >> 7, 8, onehot(s & 127))
        total = cs_ref[k] + added
        cs_out[k] = total
        ys_out[k] = total / ds_ref[k]
        (added,) = scatter([fit], p >> 7, 16, onehot(p & 127))
        cf_out[...] += added
        return carry

    lax.fori_loop(0, 4, apply, 0)
    cf = cf_out[...] - SMOOTH * beside(g0f_ref[...], above_ref[...], below_ref[...])
    cf_out[...] = cf
    yf = cf / df_ref[...]
    yf_out[...] = yf
    top_out[...] = jnp.concatenate([yf[0:1], yf[8:9]], axis=0)


def fold8(a):
    total = a[0:8]
    for i in range(8, a.shape[0], 8):
        total = total + a[i : i + 8]
    return jnp.sum(total, axis=0, keepdims=True)


def fold_lanes(a):
    total = a[:, 0:LO]
    for i in range(LO, a.shape[1], LO):
        total = total + a[:, i : i + LO]
    return total


def last_kernel(
    pos_ref, obs_ref, g0s_ref, ds_ref, cs_ref, ys_ref, g0f_ref, df_ref, cf_ref, yf_ref, ru_ref, out_ref
):
    y = pos_ref[0]
    total = jnp.zeros((8, LO), F32)
    cross = jnp.zeros((1, LO), F32)
    yf = yf_ref[...]
    for k in range(4):
        s, p, e, w = own_fields(obs_ref, y, k)
        hi = (e >> 7) + (lax.broadcasted_iota(I32, e.shape, 1) >> 9) * 4
        from_star = gather(ys_ref[k], s >> 7, onehot(s & 127))
        from_flat = gather(yf, p >> 7, onehot(p & 127))
        (added,) = scatter([w * (from_star + from_flat)], hi, 8, onehot(e & 127))
        total += added
        cross += fold_lanes(w * from_star * from_flat)
    out_ref[0:8] = jnp.where(row_iota((8, LO)) < 4, ru_ref[...], pltpu.roll(total, 4, 0))
    out_ref[8:16] = jnp.where(row_iota((8, LO)) < 4, pltpu.roll(ru_ref[...], 4, 0), total)
    g0s = jnp.concatenate([g0s_ref[k] for k in range(4)], axis=0)
    ds = jnp.concatenate([ds_ref[k] for k in range(4)], axis=0)
    cs = jnp.concatenate([cs_ref[k] for k in range(4)], axis=0)
    ys = jnp.concatenate([ys_ref[k] for k in range(4)], axis=0)
    g0f, df, cf = g0f_ref[...], df_ref[...], cf_ref[...]
    none = jnp.zeros((2, LO), F32)
    rho = 0.25 * (fold8(g0s * g0s * ds) + fold8(g0f * g0f * df))
    beta = 0.25 * (fold8(g0s * cs) + fold8(g0f * cf))
    eta = 0.25 * (fold8(cs * ys) + fold8(cf * yf))
    delta = 2.0 * cross - (0.25 * SMOOTH) * fold8(yf * beside(yf, none, none))
    out_ref[16:24] = jnp.concatenate([rho, beta, eta, delta, jnp.zeros((4, LO), F32)], axis=0)


def whole(a):
    return jnp.sum(jnp.sum(a, axis=0, keepdims=True), axis=1, keepdims=True)


def finish_kernel(
    pos_ref, sums_ref, g0z_ref, dz_ref, g0s_ref, ys_ref, g0f_ref, yf_ref, star_out, zero_out, flat_out
):
    y, zh = pos_ref[0], pos_ref[1]
    scal = sums_ref[0, 16:24]
    for peer in range(1, 32):
        scal = scal + sums_ref[peer, 16:24]
    z_rho = jnp.zeros((8, LO), F32)
    z_beta, z_eta, z_delta = z_rho, z_rho, z_rho
    z_own = z_rho
    for i in range(4):
        part = sums_ref[i, 0:16]
        for xc in range(1, 8):
            part = part + sums_ref[xc * 4 + i, 0:16]
        cz, qz = pair_rows(part[:8], part[8:])
        g0z, dz = g0z_ref[i], dz_ref[i]
        yz = cz / dz
        z_rho += g0z * g0z * dz
        z_beta += g0z * cz
        z_eta += cz * yz
        z_delta += qz * yz
        z_own = jnp.where(i == y, yz, z_own)
    rho0 = whole(z_rho) + whole(scal[0:1])
    beta = whole(z_beta) + whole(scal[1:2])
    eta = whole(z_eta) + whole(scal[2:3])
    delta = 2.0 * whole(z_delta) + whole(scal[3:4])
    curv0 = rho0 + beta
    step0 = rho0 / curv0
    left = beta / curv0
    rho1 = left * left * rho0 - 2.0 * step0 * left * beta + step0 * step0 * eta
    curv_g = (
        left * left * curv0
        - 2.0 * step0 * left * (beta + eta)
        + step0 * step0 * (eta + delta)
    )
    ratio = rho1 / rho0
    mixed = left * curv0 - step0 * (beta + eta)
    curv1 = curv_g + 2.0 * ratio * mixed + ratio * ratio * curv0
    step1 = rho1 / curv1
    along_g = step0 + step1 * (left + ratio)
    along_y = -step1 * step0
    star = along_g * g0s_ref[y] + along_y * ys_ref[y]
    star_out[...] = jnp.where(zh == 0, star, pltpu.roll(star, 4, 0))[0:4]
    zero_out[...] = (along_g * g0z_ref[y] + along_y * z_own)[0:4]
    flat = along_g * g0f_ref[...] + along_y * yf_ref[...]
    flat_out[:, 0:LO] = flat[:8]
    flat_out[:, LO : 2 * LO] = flat[8:]


VMEM = pl.BlockSpec(memory_space=pltpu.VMEM)
SMEM = pl.BlockSpec(memory_space=pltpu.SMEM)


def call(kernel, name, shapes, args, smem=0, scratch=(), flops=0):
    out = [jax.ShapeDtypeStruct(shape, F32) for shape in shapes]
    many = len(out) > 1
    return pl.pallas_call(
        kernel,
        name=name,
        out_shape=tuple(out) if many else out[0],
        in_specs=[SMEM] * smem + [VMEM] * (len(args) - smem),
        out_specs=tuple([VMEM] * len(out)) if many else VMEM,
        scratch_shapes=list(scratch),
        cost_estimate=pl.CostEstimate(flops=flops, bytes_accessed=1 << 20, transcendentals=0),
    )(*args)


def exchange(blocks, axes):
    return lax.all_to_all(blocks, axes, 0, 0, tiled=True)


def flat_pairs():
    def place(tile, y, zh):
        x, rest = divmod(tile, NZ * NC)
        zl, c = divmod(rest, NC)
        return (((x * NZ + zl) * NC + c) * NY + y) * NH + zh

    up = []
    for tile in range(NX * NZ * NC - 1):
        far = (tile + 1) % (NZ * NC) == 0
        for y in range(NY):
            for zh in range(NH):
                up.append((place(tile, y, zh), place(tile + 1, y, 1 - zh if far else zh)))
    return up, [(j, i) for i, j in up]


def on_device(star_slot, star_block, exposure, superpixel, magnitude, weight):
    y = lax.axis_index("y")
    zh = lax.axis_index("zh")
    pos = jnp.stack([y, zh]).astype(I32)
    up, down = flat_pairs()
    obs = call(
        pack_kernel, "pack", [(4, 8, 512)],
        (star_block, star_slot[0], exposure[0], superpixel[0], magnitude[0], weight[0]), smem=1,
    )
    partner = lax.ppermute(obs, "zh", [(0, 1), (1, 0)])
    expo = exchange(call(expo_kernel, "expo", [(16, 8, LO)], (obs,)), ("zl", "zh"))
    expo = expo.reshape(NZ, NH, 8, LO).sum(axis=0)
    expo = jnp.where(zh == 0, expo, expo[::-1]).reshape(16, LO)
    both = jnp.stack([obs, partner])
    tile_obs = exchange(jnp.broadcast_to(both[None], (NY, *both.shape)), "y")
    tile_obs = tile_obs.reshape(8, 4, 8, 512)
    expo, tile_obs = lax.optimization_barrier((expo, tile_obs))
    expo = exchange(jnp.broadcast_to(expo[None], (32, 16, LO)), ("x", "c", "y"))
    g0s, ds, cs, g0f, df, cf, ru, top, bot = call(
        tile_kernel, "tile",
        [(4, 8, LO)] * 3 + [(16, LO)] * 3 + [(8, LO)] + [(2, LO)] * 2,
        (pos, tile_obs), smem=1,
        scratch=[pltpu.VMEM((4, LO, 4096), BF16)] * 2 + [pltpu.VMEM((4, 1, 4096), F32)],
        flops=1 << 30,
    )
    above = lax.ppermute(bot, ALL, up)
    below = lax.ppermute(top, ALL, down)
    cs, ys, cf, yf, g0z, dz, first = call(
        expo_apply_kernel, "apply",
        [(4, 8, LO)] * 2 + [(16, LO)] * 2 + [(4, 8, LO)] * 2 + [(2, LO)],
        (tile_obs, expo, g0f, cs, cf, ds, df, above, below),
        flops=1 << 30,
    )
    next_first = lax.ppermute(first, ALL, down)
    payload = call(
        last_kernel, "last", [(24, LO)],
        (pos, tile_obs, g0s, ds, cs, ys, g0f, df, cf, yf, ru), smem=1,
        flops=1 << 28,
    )
    edge = -(0.5 * SMOOTH) * (yf[7] * next_first[0] + yf[15] * next_first[1])
    payload = payload + jnp.where(
        lax.broadcasted_iota(I32, (24, LO), 0) == 19, edge[None], 0.0
    )
    sums = exchange(jnp.broadcast_to(payload[None], (NZ, 24, LO)), "zl").sum(axis=0)
    sums = exchange(jnp.broadcast_to(sums[None], (32, 24, LO)), ("x", "c", "y"))
    star, zero, flat = call(
        finish_kernel, "finish", [(4, LO), (4, LO), (8, 2 * LO)],
        (pos, sums, g0z, dz, g0s, ys, g0f, yf), smem=1,
    )
    return star.reshape(-1), zero.reshape(-1), flat


def solution(mesh):
    split = Mesh(mesh.devices.reshape(NX, NZ, NC, NY, NH), ALL)
    tile, loop = ("x", "zl", "c"), ("y", "zh")
    placed = (
        P(tile, loop, None),
        P(tile, loop),
        P(tile, loop, None),
        P(tile, loop, None),
        P(tile, loop, None),
        P(tile, loop, None),
    )
    return jax.shard_map(
        on_device,
        mesh=split,
        in_specs=placed,
        out_specs=(P(ALL), P(loop), P(tile, None)),
        check_vma=False,
    )
```

time: 633 us -> 139 us (0.22)
  other arithmetic: 172 us -> 2.17 us
  starting transfers between devices: 181 us -> 46.2 us
  blocking collectives: 144 us -> 44.7 us
  local copies, waits for them, and re-layouts: 82.5 us -> 3.74 us
  Pallas kernels: 0 us -> 25.8 us
  waiting for transfers between devices: 36.3 us -> 14.8 us
  between operations: 14.7 us -> 0.77 us
    scatter-add x12 -> x0, other arithmetic: 165 us -> none  [scatter_add(): jax.ops.segment_sum(values.reshape(-1), targets.reshape(-1), num_segments...]
    psum x10 -> x0, blocking collectives: 144 us -> none  [by_axis(): return functools.reduce(lax.psum, axes, array)]
    all_to_all x14 -> x3, starting transfers between devices: 169 us -> 27.3 us  [exchange(): return lax.all_to_all(blocks, axes, 0, 0, tiled=True)]
    gather x6 -> x0, local copies, waits for them, and re-layouts: 73.5 us -> none  [the longest x2 26.4 us: operate(): expo_dir[expo_ids]]
    all_to_all x0 -> x2, blocking collectives: none -> 44.7 us  [exchange(): return lax.all_to_all(blocks, axes, 0, 0, tiled=True)]
    all_to_all x14 -> x3, waiting for transfers between devices: 36.3 us -> 8.21 us  [exchange(): return lax.all_to_all(blocks, axes, 0, 0, tiled=True)]
    pallas_call x0 -> x6, Pallas kernels: none -> 25.8 us  [call(): pl.pallas_call(kernel, name=name, out_shape=tuple(out) if many else out[0...]
    ppermute x4, starting transfers between devices: 11.2 us -> 18.9 us  [the longest x1 12 us: on_device(): partner = lax.ppermute(obs, 'zh', [(0, 1), (1, 0)])]
  transfers between devices with their start and end apart: 18 -> 7, of which waited for: 7 -> 4; matrix products, arithmetic and copies ran while one was open for 27% -> 1% of each run, Pallas kernels for 0% -> 10%
where the time goes in v1:
time: 139 us; the launch traced here: 138 us
  starting transfers between devices  46.2 us (33%)
  blocking collectives  44.7 us (32%)
  Pallas kernels  25.8 us (19%)
  waiting for transfers between devices  14.8 us (11%)
  local copies, waits for them, and re-layouts  3.74 us (3%)
  other arithmetic  2.17 us (2%)
    all_to_all x2, blocking collectives, exchange(): return lax.all_to_all(blocks, axes, 0, 0, tiled=True)  44.7 us
    all_to_all x3, starting transfers between devices, exchange(): return lax.all_to_all(blocks, axes, 0, 0, tiled=True)  27.3 us
    pallas_call x6, Pallas kernels, call(): pl.pallas_call(kernel, name=name, out_shape=tuple(out) if many else out[0...  25.8 us
    ppermute x1, starting transfers between devices, on_device(): partner = lax.ppermute(obs, 'zh', [(0, 1), (1, 0)])  12 us
    all_to_all x3, waiting for transfers between devices, exchange(): return lax.all_to_all(blocks, axes, 0, 0, tiled=True)  8.21 us
    ppermute x1, waiting for transfers between devices, on_device(): partner = lax.ppermute(obs, 'zh', [(0, 1), (1, 0)])  3.39 us
    ppermute x1, starting transfers between devices, on_device(): above = lax.ppermute(bot, ALL, up)  3.07 us
    ppermute x1, waiting for transfers between devices, on_device(): below = lax.ppermute(top, ALL, down)  2.93 us
  transfers between devices with their start and end apart: 7, of which 4 were waited for; matrix products, arithmetic and copies ran while one was open for 1% of the time, Pallas kernels for 10%

profile of v1, /device:TPU:1, one launch (start us, length us, event | category | flops | bytes accessed | tf_op | source)
XLA Modules:
  0.0 138.1 jit_solution(7214956932238292105)
XLA Ops:
  0.6 1.5 %pack.1.obs_ref = f32[4,8,512]{2,1,0:T(8,128)} custom-call(s32[1,16]{1,0:T(1,128)} %block_ref.1, s32[16,128]{1,0:T(8,128)} %bitcast.23, s32[16,128]{1,0:T(8,128)} %bitcast.24, s32[16,128]{1,0:T(8,128)} %bitcast.25, f32[16,128]{1,0:T(8,128)} %bitcast.26, f32[16,128]{1,0:T(8,128)} %bitcast.27), custom_call_target="tpu_custom_call" | custom-call | bytes 1048576 | tf_op jit(solution)/shard_map/pack/pallas_call | solution.py:324
  2.1 1.8 %expo.1 = f32[16,8,128]{2,1,0:T(8,128)} custom-call(f32[4,8,512]{2,1,0:T(8,128)} %pack.1.obs_ref), custom_call_target="tpu_custom_call" | custom-call | bytes 1048576 | tf_op jit(solution)/shard_map/expo/pallas_call | solution.py:324
  3.9 15.9 %all-to-all-start = ((f32[16,8,128]{2,1,0:T(8,128)}), f32[16,8,128]{2,1,0:T(8,128)S(1)}, u32[]{:S(2)}, u32[]{:S(2)}) async-start(f32[16,8,128]{2,1,0:T(8,128)} %expo.1), calls=%async_computation | async-start | bytes 131072 | tf_op jit(solution)/shard_map/all_to_all | solution.py:336
  19.8 12.0 %collective-permute-start = (f32[4,8,512]{2,1,0:T(8,128)S(1)}, f32[4,8,512]{2,1,0:T(8,128)S(1)}, u32[]{:S(2)}, u32[]{:S(2)}) collective-permute-start(f32[4,8,512]{2,1,0:T(8,128)S(1)} %copy-done), channel_id=1, source_target_pairs={{0,1},{1,0},{2,3},{3,2},{4,5},{5,4},{6,7},{7,6},{8,9},{9,8},{10,11... | collective-permute-start | bytes 196616 | tf_op jit(solution)/shard_map/ppermute | solution.py:363
  31.8 3.4 %collective-permute-done = f32[4,8,512]{2,1,0:T(8,128)S(1)} collective-permute-done((f32[4,8,512]{2,1,0:T(8,128)S(1)}, f32[4,8,512]{2,1,0:T(8,128)S(1)}, u32[]{:S(2)}, u32[]{:S(2)}) %collective-permute-start) | collective-permute-done | bytes 65568 | tf_op jit(solution)/shard_map/ppermute | solution.py:363
  35.2 0.9 broadcast_in_dim.22
  36.0 4.2 %all-to-all-start.1 = ((f32[4,2,4,8,512]{4,3,2,1,0:T(8,128)}), f32[4,2,4,8,512]{4,3,2,1,0:T(8,128)S(1)}, u32[]{:S(2)}, u32[]{:S(2)}) async-start(f32[4,2,4,8,512]{4,3,2,1,0:T(8,128)} %broadcast_in_dim.22), calls=%async_computation.1 | async-start | bytes 1048576 | tf_op jit(solution)/shard_map/all_to_all | solution.py:336
  40.2 8.2 %all-to-all-done.1 = f32[4,2,4,8,512]{4,3,2,1,0:T(8,128)S(1)} async-done(((f32[4,2,4,8,512]{4,3,2,1,0:T(8,128)}), f32[4,2,4,8,512]{4,3,2,1,0:T(8,128)S(1)}, u32[]{:S(2)}, u32[]{:S(2)}) %all-to-all-start.1) | async-done | bytes 524320 | tf_op jit(solution)/shard_map/all_to_all | solution.py:336
  48.4 0.8 broadcast_in_dim.23
  49.2 7.3 %all-to-all-start.2 = ((f32[32,16,128]{2,1,0:T(8,128)}), f32[32,16,128]{2,1,0:T(8,128)S(1)}, u32[]{:S(2)}, u32[]{:S(2)}) async-start(f32[32,16,128]{2,1,0:T(8,128)} %broadcast_in_dim.23), calls=%async_computation.2 | async-start | bytes 524288 | tf_op jit(solution)/shard_map/all_to_all | solution.py:336
  57.1 11.6 %tile.1 = (f32[4,8,128]{2,1,0:T(8,128)}, f32[4,8,128]{2,1,0:T(8,128)}, f32[4,8,128]{2,1,0:T(8,128)}, f32[16,128]{1,0:T(8,128)}, f32[16,128]{1,0:T(8,128)}, /*ind...) custom-call(s32[2]{0:T(128)} %pad_add_fusion.pos_ref, f32[8,4,8,512]{3,2,1,0:T(8,128)} %bitcast.18), custom_call_target="tpu_custom_call" | custom-call | flops 1073741824 | bytes 1048576 | tf_op jit(solution)/shard_map/tile/pallas_call | solution.py:324
  68.7 0.7 copy-done.7
  69.4 3.1 %collective-permute-start.1 = (f32[2,128]{1,0:T(2,128)S(1)}, f32[2,128]{1,0:T(2,128)S(1)}, u32[]{:S(2)}, u32[]{:S(2)}) collective-permute-start(f32[2,128]{1,0:T(2,128)S(1)} %copy-done.7), channel_id=1, source_target_pairs={{0,8},{1,9},{2,10},{3,11},{4,12},{5,13},{6,14},{7,15},{8,16},{9,17... | collective-permute-start | bytes 3080 | tf_op jit(solution)/shard_map/ppermute | solution.py:379
  72.5 1.9 %collective-permute-start.2 = (f32[2,128]{1,0:T(2,128)S(1)}, f32[2,128]{1,0:T(2,128)S(1)}, u32[]{:S(2)}, u32[]{:S(2)}) collective-permute-start(f32[2,128]{1,0:T(2,128)S(1)} %copy-done.6), channel_id=1, source_target_pairs={{8,0},{9,1},{10,2},{11,3},{12,4},{13,5},{14,6},{15,7},{16,8},{17,9... | collective-permute-start | bytes 3080 | tf_op jit(solution)/shard_map/ppermute | solution.py:380
  74.4 2.9 %collective-permute-done.2.below_ref = f32[2,128]{1,0:T(2,128)S(1)} collective-permute-done((f32[2,128]{1,0:T(2,128)S(1)}, f32[2,128]{1,0:T(2,128)S(1)}, u32[]{:S(2)}, u32[]{:S(2)}) %collective-permute-start.2) | collective-permute-done | bytes 1056 | tf_op jit(solution)/shard_map/ppermute | solution.py:380
  78.1 6.4 %apply.1 = (f32[4,8,128]{2,1,0:T(8,128)}, f32[4,8,128]{2,1,0:T(8,128)}, f32[16,128]{1,0:T(8,128)}, f32[16,128]{1,0:T(8,128)}, f32[4,8,128]{2,1,0:T(8,128)}, /*index=5*/f32[4,8,128]{2,1,0:T(8,128)}, f32[2,128]{1,0:T(2,128)}) custom-call(f32[8,4,8,512]{3,2,1,0:T(8,128)} %bitcast.19, f32[32,16,128]{2,1,0:T(8,128)} %copy-done.2, ...), custom_call_target="tpu_custom_call" | custom-call | flops 1073741824 | bytes 1048576 | tf_op jit(solution)/shard_map/apply/pallas_call | solution.py:324
  84.5 0.7 copy-done.5
  85.2 1.9 %collective-permute-start.3 = (f32[2,128]{1,0:T(2,128)S(1)}, f32[2,128]{1,0:T(2,128)S(1)}, u32[]{:S(2)}, u32[]{:S(2)}) collective-permute-start(f32[2,128]{1,0:T(2,128)S(1)} %copy-done.5), channel_id=1, source_target_pairs={{8,0},{9,1},{10,2},{11,3},{12,4},{13,5},{14,6},{15,7},{16,8},{17,9... | collective-permute-start | bytes 3080 | tf_op jit(solution)/shard_map/ppermute | solution.py:387
  87.1 2.7 %last.1 = f32[24,128]{1,0:T(8,128)} custom-call(s32[2]{0:T(128)} %pad_add_fusion.pos_ref, f32[8,4,8,512]{3,2,1,0:T(8,128)} %bitcast.20, f32[4,8,128]{2,1,0:T(8,128)} %get-tuple-element.25.g0s_ref, f32[4,8,128]{2,1,0:T(8,128)} %get-tuple-element.26.ds_ref, f32[4,8,128]{2,1,0:T(8,128)} %get-tuple-element.34.cs_ref, f32[4,8,128]{2,1,0:T(8,128)} %get-tuple-element.35.ys_ref, ...), custom_call_target="tpu_custom_call" | custom-call | flops 268435456 | bytes 1048576 | tf_op jit(solution)/shard_map/last/pallas_call | solution.py:324
  90.0 0.7 multiply_bitcast_fusion
  90.7 0.8 select_add_fusion
  91.5 28.1 %all_to_all.25 = f32[8,24,128]{2,1,0:T(8,128)S(1)} all-to-all(f32[8,24,128]{2,1,0:T(8,128)S(1)} %broadcast_in_dim.44), channel_id=1, replica_groups=mesh['x'=4,'zl'=8,'c'=2,'y'=4,'zh'=2] {'zl'}, dimensions={0} | all-to-all | bytes 196608 | tf_op jit(solution)/shard_map/all_to_all | solution.py:336
  119.6 16.7 %all_to_all.26.sums_ref = f32[32,24,128]{2,1,0:T(8,128)} all-to-all(f32[32,24,128]{2,1,0:T(8,128)S(1)} %broadcast_in_dim.45), channel_id=1, replica_groups=mesh['x'=4,'zl'=8,'c'=2,'y'=4,'zh'=2] {'x','c','y'}, dimensions={0} | all-to-all | bytes 786432 | tf_op jit(solution)/shard_map/all_to_all | solution.py:336
  136.3 1.9 %finish.1 = (f32[4,128]{1,0:T(4,128)}, f32[4,128]{1,0:T(4,128)}, f32[8,256]{1,0:T(8,128)}) custom-call(s32[2]{0:T(128)} %pad_add_fusion.pos_ref, f32[32,24,128]{2,1,0:T(8,128)} %all_to_all.26.sums_ref, f32[4,8,128]{2,1,0:T(8,128)} %get-tuple-element.40.g0z_ref, f32[4,8,128]{2,1,0:T(8,128)} %get-tuple-element.41.dz_ref, ...), custom_call_target="tpu_custom_call" | custom-call | bytes 1048576 | tf_op jit(solution)/shard_map/finish/pallas_call | solution.py:324
  (26 shorter events, 1.7 us)
Async XLA Ops:
  3.9 15.9 %copy-start = (f32[4,8,512]{2,1,0:T(8,128)S(1)}, f32[4,8,512]{2,1,0:T(8,128)}, u32[]{:S(2)}) copy-start(f32[4,8,512]{2,1,0:T(8,128)} %pack.1.obs_ref) | copy-start | bytes 196612
  3.9 31.3 %all-to-all-start = ((f32[16,8,128]{2,1,0:T(8,128)}), f32[16,8,128]{2,1,0:T(8,128)S(1)}, u32[]{:S(2)}, u32[]{:S(2)}) async-start(f32[16,8,128]{2,1,0:T(8,128)} %expo.1), calls=%async_computation | async-start | bytes 131072 | tf_op jit(solution)/shard_map/all_to_all | solution.py:336
  19.8 15.4 %collective-permute-start = (f32[4,8,512]{2,1,0:T(8,128)S(1)}, f32[4,8,512]{2,1,0:T(8,128)S(1)}, u32[]{:S(2)}, u32[]{:S(2)}) collective-permute-start(f32[4,8,512]{2,1,0:T(8,128)S(1)} %copy-done), channel_id=1, source_target_pairs={{0,1},{1,0},{2,3},{3,2},{4,5},{5,4},{6,7},{7,6},{8,9},{9,8},{10,11... | collective-permute-start | bytes 196616 | tf_op jit(solution)/shard_map/ppermute | solution.py:363
  36.0 12.4 %all-to-all-start.1 = ((f32[4,2,4,8,512]{4,3,2,1,0:T(8,128)}), f32[4,2,4,8,512]{4,3,2,1,0:T(8,128)S(1)}, u32[]{:S(2)}, u32[]{:S(2)}) async-start(f32[4,2,4,8,512]{4,3,2,1,0:T(8,128)} %broadcast_in_dim.22), calls=%async_computation.1 | async-start | bytes 1048576 | tf_op jit(solution)/shard_map/all_to_all | solution.py:336
  48.4 8.7 %copy-start.1 = (f32[4,2,4,8,512]{4,3,2,1,0:T(8,128)}, f32[4,2,4,8,512]{4,3,2,1,0:T(8,128)S(1)}, u32[]{:S(2)}) copy-start(f32[4,2,4,8,512]{4,3,2,1,0:T(8,128)S(1)} %all-to-all-done.1) | copy-start | bytes 1572868
  49.2 28.2 %all-to-all-start.2 = ((f32[32,16,128]{2,1,0:T(8,128)}), f32[32,16,128]{2,1,0:T(8,128)S(1)}, u32[]{:S(2)}, u32[]{:S(2)}) async-start(f32[32,16,128]{2,1,0:T(8,128)} %broadcast_in_dim.23), calls=%async_computation.2 | async-start | bytes 524288 | tf_op jit(solution)/shard_map/all_to_all | solution.py:336
  68.7 0.7 copy-start.7
  69.4 3.1 %copy-start.6 = (f32[2,128]{1,0:T(2,128)S(1)}, f32[2,128]{1,0:T(2,128)}, u32[]{:S(2)}) copy-start(f32[2,128]{1,0:T(2,128)} %get-tuple-element.33) | copy-start | bytes 3076
  69.4 5.0 %collective-permute-start.1 = (f32[2,128]{1,0:T(2,128)S(1)}, f32[2,128]{1,0:T(2,128)S(1)}, u32[]{:S(2)}, u32[]{:S(2)}) collective-permute-start(f32[2,128]{1,0:T(2,128)S(1)} %copy-done.7), channel_id=1, source_target_pairs={{0,8},{1,9},{2,10},{3,11},{4,12},{5,13},{6,14},{7,15},{8,16},{9,17... | collective-permute-start | bytes 3080 | tf_op jit(solution)/shard_map/ppermute | solution.py:379
  72.5 4.9 %collective-permute-start.2 = (f32[2,128]{1,0:T(2,128)S(1)}, f32[2,128]{1,0:T(2,128)S(1)}, u32[]{:S(2)}, u32[]{:S(2)}) collective-permute-start(f32[2,128]{1,0:T(2,128)S(1)} %copy-done.6), channel_id=1, source_target_pairs={{8,0},{9,1},{10,2},{11,3},{12,4},{13,5},{14,6},{15,7},{16,8},{17,9... | collective-permute-start | bytes 3080 | tf_op jit(solution)/shard_map/ppermute | solution.py:380
  74.4 3.0 %copy-start.3 = (f32[2,128]{1,0:T(2,128)}, f32[2,128]{1,0:T(2,128)S(1)}, u32[]{:S(2)}) copy-start(f32[2,128]{1,0:T(2,128)S(1)} %collective-permute-done.1.above_ref) | copy-start | bytes 3076
  77.4 0.6 copy-start.4
  77.4 0.7 copy-start.2
  84.5 0.7 copy-start.5
  85.2 4.9 %collective-permute-start.3 = (f32[2,128]{1,0:T(2,128)S(1)}, f32[2,128]{1,0:T(2,128)S(1)}, u32[]{:S(2)}, u32[]{:S(2)}) collective-permute-start(f32[2,128]{1,0:T(2,128)S(1)} %copy-done.5), channel_id=1, source_target_pairs={{8,0},{9,1},{10,2},{11,3},{12,4},{13,5},{14,6},{15,7},{16,8},{17,9... | collective-permute-start | bytes 3080 | tf_op jit(solution)/shard_map/ppermute | solution.py:387

commit v2 on v1

--- a/solution.py
+++ b/solution.py
@@ -19,41 +19,74 @@
 
 
 def split3(v):
-    first = v.astype(BF16).astype(F32)
-    rest = v - first
-    second = rest.astype(BF16).astype(F32)
-    return first, second, rest - second
-
-
-def pad16(rows):
-    count = sum(row.shape[0] for row in rows)
-    if count % 16:
-        rows = rows + [jnp.zeros((16 - count % 16, rows[0].shape[1]), F32)]
-    return jnp.concatenate(rows, axis=0).astype(BF16)
+    first = v.astype(BF16)
+    rest = v - first.astype(F32)
+    second = rest.astype(BF16)
+    return first, second, (rest - second.astype(F32)).astype(BF16)
+
+
+def bf_iota(shape, wrap=None):
+    rows = lax.broadcasted_iota(I32, shape, 0)
+    if wrap:
+        rows = rows & (wrap - 1)
+    return rows.astype(F32).astype(BF16)
 
 
 def onehot(lo):
-    n = lo.shape[1]
-    return jnp.where(lax.broadcasted_iota(I32, (LO, n), 0) == lo, 1.0, 0.0).astype(BF16)
+    rows = bf_iota((LO, LO))
+    one, zero = jnp.ones((), BF16), jnp.zeros((), BF16)
+    tiles = [
+        jnp.where(rows == jnp.broadcast_to(lo[:, i : i + LO], (LO, LO)), one, zero)
+        for i in range(0, lo.shape[1], LO)
+    ]
+    return jnp.concatenate(tiles, axis=1)
+
+
+def spread(parts, hi, high):
+    n = hi.shape[1]
+    shape = (16, n)
+    zero = jnp.zeros((), BF16)
+    mask = bf_iota((16, LO), high)
+    mask = jnp.concatenate(
+        [mask == jnp.broadcast_to(hi[:, i : i + LO], (16, LO)) for i in range(0, n, LO)], axis=1
+    )
+    if high == 16:
+        return [jnp.where(mask, jnp.broadcast_to(part, shape), zero) for part in parts]
+    if len(parts) % 2:
+        parts = list(parts) + [jnp.zeros_like(parts[0])]
+    low = lax.broadcasted_iota(I32, (16, n), 0) < 8
+    return [
+        jnp.where(
+            mask,
+            jnp.where(low, jnp.broadcast_to(a.astype(F32), shape), jnp.broadcast_to(b.astype(F32), shape)).astype(BF16),
+            zero,
+        )
+        for a, b in zip(parts[::2], parts[1::2])
+    ]
 
 
 def scatter(values, hi, high, hot):
-    mask = lax.broadcasted_iota(I32, (high, hi.shape[1]), 0) == hi
-    rows = [jnp.where(mask, part, 0.0) for v in values for part in split3(v)]
-    sums = lax.dot_general(pad16(rows), hot, NT, preferred_element_type=F32)
-    return [
-        sums[3 * high * i : 3 * high * i + high]
-        + sums[3 * high * i + high : 3 * high * i + 2 * high]
-        + sums[3 * high * i + 2 * high : 3 * high * (i + 1)]
-        for i in range(len(values))
-    ]
+    parts = [part for value in values for part in value]
+    rows = jnp.concatenate(spread(parts, hi, high), axis=0)
+    sums = lax.dot_general(rows, hot, NT, preferred_element_type=F32)
+    out = []
+    for i in range(len(values)):
+        at = 3 * high * i
+        out.append(
+            sums[at : at + high] + sums[at + high : at + 2 * high] + sums[at + 2 * high : at + 3 * high]
+        )
+    return out
 
 
 def gather(table, hi, hot):
     high = table.shape[0]
-    parts = lax.dot_general(pad16(list(split3(table))), hot, NN, preferred_element_type=F32)
+    parts = [part.astype(F32) for part in split3(table)]
+    if 3 * high % 16:
+        parts.append(jnp.zeros((high, LO), F32))
+    parts = jnp.concatenate(parts, axis=0).astype(BF16)
+    parts = lax.dot_general(parts, hot, NN, preferred_element_type=F32)
     found = parts[:high] + parts[high : 2 * high] + parts[2 * high : 3 * high]
-    mask = lax.broadcasted_iota(I32, found.shape, 0) == hi
+    mask = lax.broadcasted_iota(I32, found.shape, 0).astype(F32) == hi
     return jnp.sum(jnp.where(mask, found, 0.0), axis=0, keepdims=True)
 
 
@@ -66,60 +99,74 @@
     for r in range(16):
         star = slot_ref[r : r + 1, :] + (block_ref[0, r] * 256 + ((r // 2) % 2) * 512)
         pix = pix_ref[r : r + 1, :]
-        pix = (((pix >> 7) & 1) * 8 + (pix >> 8)) * LO + (pix & 127)
+        expo = expo_ref[r : r + 1, :]
         w = w_ref[r : r + 1, :]
-        fields = (
-            star.astype(F32),
-            pix.astype(F32),
-            expo_ref[r : r + 1, :].astype(F32),
-            w,
-            w * mag_ref[r : r + 1, :],
-        )
-        tile = jnp.zeros((8, LO), F32)
-        for f, field in enumerate(fields):
+        ids = (star & 127, star >> 7, pix & 127, ((pix >> 7) & 1) * 8 + (pix >> 8), expo & 127, expo >> 7)
+        tile = jnp.zeros((8, LO), I32)
+        for f, field in enumerate(ids):
             tile = jnp.where(rows == f, field, tile)
+        tile = jnp.where(rows == 6, w, tile.astype(F32))
+        tile = jnp.where(rows == 7, w * mag_ref[r : r + 1, :], tile)
         out_ref[r // 4, :, (r % 4) * LO : (r % 4 + 1) * LO] = tile
+
+
+S_LO, S_HI, P_LO, P_HI, E_LO, E_HI, W, WM = range(8)
+
+
+def row(x, f):
+    return x[f : f + 1]
 
 
 def expo_kernel(obs_ref, out_ref):
     x = jnp.concatenate([obs_ref[k] for k in range(4)], axis=1)
-    e = x[2:3].astype(I32)
-    weighted, count = scatter([x[4:5], x[3:4]], e >> 7, 8, onehot(e & 127))
+    parts = split3(x)
+    weighted, count = scatter(
+        [[row(part, WM) for part in parts], [row(part, W) for part in parts]],
+        row(parts[0], E_HI), 8, onehot(row(parts[0], E_LO)),
+    )
     both = jnp.where(row_iota((8, LO)) < 4, weighted, pltpu.roll(count, 4, 0))
     for peer in range(16):
         out_ref[peer] = both
 
 
 def fields_of(obs_ref, k):
-    x = jnp.concatenate([obs_ref[g, k] for g in range(8)], axis=1)
-    ids = x.astype(I32)
-    return ids[0:1], ids[1:2], ids[2:3], x[3:4], x[4:5]
+    return jnp.concatenate([obs_ref[g, k] for g in range(8)], axis=1)
 
 
 def own_fields(obs_ref, y, k):
-    x = jnp.concatenate([obs_ref[2 * y + rel, k] for rel in range(2)], axis=1)
-    ids = x.astype(I32)
-    return ids[0:1], ids[1:2], ids[2:3], x[3:4]
+    return jnp.concatenate([obs_ref[2 * y + rel, k] for rel in range(2)], axis=1)
+
+
+def expo_hi(x):
+    hi = row(x, E_HI)
+    shift = (lax.broadcasted_iota(I32, hi.shape, 1) >> 9) & 1
+    return hi + 4.0 * shift.astype(F32)
+
+
+def two_rows(first, second):
+    return jnp.where(row_iota((8, first.shape[1])) == 0, first, second)
 
 
 def tile_kernel(
-    pos_ref, obs_ref, g0s_ref, ds_ref, cs_ref, g0f_ref, df_ref, cf_ref, ru_ref, top_ref, bot_ref,
+    obs_ref, g0s_ref, ds_ref, cs_ref, g0f_ref, df_ref, cf_ref, ru_ref, hop_ref, chip_ref,
     hot_s, hot_p, fit_ref,
 ):
     g0f_ref[...] = jnp.zeros((16, LO), F32)
     df_ref[...] = jnp.zeros((16, LO), F32)
 
     def sums(k, carry):
-        s, p, e, w, wm = fields_of(obs_ref, k)
-        hs = onehot(s & 127)
-        hp = onehot(p & 127)
+        x = fields_of(obs_ref, k)
+        parts = split3(x)
+        hs = onehot(row(parts[0], S_LO))
+        hp = onehot(row(parts[0], P_LO))
         hot_s[k] = hs
         hot_p[k] = hp
-        weighted, count = scatter([wm, w], s >> 7, 8, hs)
+        values = [[row(part, WM) for part in parts], [row(part, W) for part in parts]]
+        weighted, count = scatter(values, row(parts[0], S_HI), 8, hs)
         diag = count + RIDGE
         g0s_ref[k] = weighted / diag
         ds_ref[k] = diag
-        weighted, count = scatter([wm, w], p >> 7, 16, hp)
+        weighted, count = scatter(values, row(parts[0], P_HI), 16, hp)
         g0f_ref[...] += weighted
         df_ref[...] += count
         return carry
@@ -129,31 +176,41 @@
     g0f = g0f_ref[...] / diag
     df_ref[...] = diag
     g0f_ref[...] = g0f
-    top_ref[...] = jnp.concatenate([g0f[0:1], g0f[8:9]], axis=0)
-    bot_ref[...] = jnp.concatenate([g0f[7:8], g0f[15:16]], axis=0)
+    odd = lax.axis_index("c") == 1
+    top = jnp.concatenate([g0f[0:1], g0f[8:9]], axis=0)
+    bot = jnp.concatenate([g0f[7:8], g0f[15:16]], axis=0)
+    hop_ref[...] = jnp.where(odd, bot, top)
+    chip_ref[...] = jnp.where(odd, top, bot)
     cf_ref[...] = jnp.zeros((16, LO), F32)
 
     def couple(k, carry):
-        s, p, e, w, wm = fields_of(obs_ref, k)
+        x = fields_of(obs_ref, k)
+        ids = x.astype(BF16)
         hs = hot_s[k]
         hp = hot_p[k]
-        from_star = gather(g0s_ref[k], s >> 7, hs)
-        from_flat = gather(g0f_ref[...], p >> 7, hp)
-        (cs_ref[k],) = scatter([w * from_flat], s >> 7, 8, hs)
-        (added,) = scatter([w * from_star], p >> 7, 16, hp)
+        from_star = gather(g0s_ref[k], row(x, S_HI), hs)
+        from_flat = gather(g0f_ref[...], row(x, P_HI), hp)
+        fit = two_rows(from_star, from_flat) * row(x, W)
+        parts = split3(fit)
+        (cs_ref[k],) = scatter([[row(part, 1) for part in parts]], row(ids, S_HI), 8, hs)
+        (added,) = scatter([[row(part, 0) for part in parts]], row(ids, P_HI), 16, hp)
         cf_ref[...] += added
-        fit_ref[k] = w * (from_star + from_flat)
+        fit_ref[k] = fit
         return carry
 
     lax.fori_loop(0, 4, couple, 0)
-    y = pos_ref[0]
+    y = lax.axis_index("y")
     total = jnp.zeros((8, LO), F32)
     for k in range(4):
-        s, p, e, w = own_fields(obs_ref, y, k)
-        hi = (e >> 7) + (lax.broadcasted_iota(I32, e.shape, 1) >> 9) * 4
+        x = own_fields(obs_ref, y, k)
         fit = fit_ref[k, :, pl.ds(pl.multiple_of(y * 1024, 1024), 1024)]
-        (added,) = scatter([fit], hi, 8, onehot(e & 127))
-        total += added
+        parts = split3(fit)
+        hi = expo_hi(x).astype(BF16)
+        star_part, flat_part = scatter(
+            [[row(part, 0) for part in parts], [row(part, 1) for part in parts]],
+            hi, 8, onehot(row(x, E_LO).astype(BF16)),
+        )
+        total += star_part + flat_part
     ru_ref[...] = total
 
 
@@ -183,7 +240,7 @@
 
 
 def expo_apply_kernel(
-    obs_ref, expo_ref, g0f_ref, cs_ref, cf_ref, ds_ref, df_ref, above_ref, below_ref,
+    obs_ref, expo_ref, g0f_ref, cs_ref, cf_ref, ds_ref, df_ref, hop_ref, chip_ref,
     cs_out, ys_out, cf_out, yf_out, g0z_out, dz_out, top_out,
 ):
     for y in range(4):
@@ -194,23 +251,31 @@
         diag = count + RIDGE
         g0z_out[y] = weighted / diag
         dz_out[y] = diag
-    table = jnp.concatenate([g0z_out[y] for y in range(4)], axis=0)
     cf_out[...] = cf_ref[...]
 
     def apply(k, carry):
-        s, p, e, w, wm = fields_of(obs_ref, k)
-        hi = (e >> 7) + (lax.broadcasted_iota(I32, e.shape, 1) >> 9) * 4
-        fit = w * gather(table, hi, onehot(e & 127))
-        (added,) = scatter([fit], s >> 7, 8, onehot(s & 127))
+        x = fields_of(obs_ref, k)
+        ids = x.astype(BF16)
+        hot = onehot(row(ids, E_LO))
+        hi = expo_hi(x)
+        found = [
+            gather(g0z_out[y], hi[:, 1024 * y : 1024 * (y + 1)], hot[:, 1024 * y : 1024 * (y + 1)])
+            for y in range(4)
+        ]
+        parts = split3(row(x, W) * jnp.concatenate(found, axis=1))
+        (added,) = scatter([parts], row(ids, S_HI), 8, onehot(row(ids, S_LO)))
         total = cs_ref[k] + added
         cs_out[k] = total
         ys_out[k] = total / ds_ref[k]
-        (added,) = scatter([fit], p >> 7, 16, onehot(p & 127))
+        (added,) = scatter([parts], row(ids, P_HI), 16, onehot(row(ids, P_LO)))
         cf_out[...] += added
         return carry
 
     lax.fori_loop(0, 4, apply, 0)
-    cf = cf_out[...] - SMOOTH * beside(g0f_ref[...], above_ref[...], below_ref[...])
+    odd = lax.axis_index("c") == 1
+    above = jnp.where(odd, chip_ref[...], hop_ref[...])
+    below = jnp.where(odd, hop_ref[...], chip_ref[...])
+    cf = cf_out[...] - SMOOTH * beside(g0f_ref[...], above, below)
     cf_out[...] = cf
     yf = cf / df_ref[...]
     yf_out[...] = yf
@@ -232,18 +297,20 @@
 
 
 def last_kernel(
-    pos_ref, obs_ref, g0s_ref, ds_ref, cs_ref, ys_ref, g0f_ref, df_ref, cf_ref, yf_ref, ru_ref, out_ref
+    obs_ref, g0s_ref, ds_ref, cs_ref, ys_ref, g0f_ref, df_ref, cf_ref, yf_ref, ru_ref, out_ref
 ):
-    y = pos_ref[0]
+    y = lax.axis_index("y")
     total = jnp.zeros((8, LO), F32)
     cross = jnp.zeros((1, LO), F32)
     yf = yf_ref[...]
     for k in range(4):
-        s, p, e, w = own_fields(obs_ref, y, k)
-        hi = (e >> 7) + (lax.broadcasted_iota(I32, e.shape, 1) >> 9) * 4
-        from_star = gather(ys_ref[k], s >> 7, onehot(s & 127))
-        from_flat = gather(yf, p >> 7, onehot(p & 127))
-        (added,) = scatter([w * (from_star + from_flat)], hi, 8, onehot(e & 127))
+        x = own_fields(obs_ref, y, k)
+        ids = x.astype(BF16)
+        w = row(x, W)
+        from_star = gather(ys_ref[k], row(x, S_HI), onehot(row(ids, S_LO)))
+        from_flat = gather(yf, row(x, P_HI), onehot(row(ids, P_LO)))
+        parts = split3(w * (from_star + from_flat))
+        (added,) = scatter([parts], expo_hi(x).astype(BF16), 8, onehot(row(ids, E_LO)))
         total += added
         cross += fold_lanes(w * from_star * from_flat)
     out_ref[0:8] = jnp.where(row_iota((8, LO)) < 4, ru_ref[...], pltpu.roll(total, 4, 0))
@@ -261,14 +328,23 @@
     out_ref[16:24] = jnp.concatenate([rho, beta, eta, delta, jnp.zeros((4, LO), F32)], axis=0)
 
 
+def edge_kernel(payload_ref, yf_ref, next_ref, out_ref):
+    edge = yf_ref[7:8] * next_ref[0:1] + yf_ref[15:16] * next_ref[1:2]
+    edge = jnp.where(row_iota((8, LO)) == 3, -(0.5 * SMOOTH) * edge, 0.0)
+    scal = payload_ref[16:24] + edge
+    for peer in range(8):
+        out_ref[peer, 0:16] = payload_ref[0:16]
+        out_ref[peer, 16:24] = scal
+
+
 def whole(a):
     return jnp.sum(jnp.sum(a, axis=0, keepdims=True), axis=1, keepdims=True)
 
 
 def finish_kernel(
-    pos_ref, sums_ref, g0z_ref, dz_ref, g0s_ref, ys_ref, g0f_ref, yf_ref, star_out, zero_out, flat_out
+    sums_ref, g0z_ref, dz_ref, g0s_ref, ys_ref, g0f_ref, yf_ref, star_out, zero_out, flat_out
 ):
-    y, zh = pos_ref[0], pos_ref[1]
+    y, zh = lax.axis_index("y"), lax.axis_index("zh")
     scal = sums_ref[0, 16:24]
     for peer in range(1, 32):
         scal = scal + sums_ref[peer, 16:24]
@@ -342,20 +418,20 @@
         zl, c = divmod(rest, NC)
         return (((x * NZ + zl) * NC + c) * NY + y) * NH + zh
 
-    up = []
+    chip, hop, down = [], [], []
     for tile in range(NX * NZ * NC - 1):
         far = (tile + 1) % (NZ * NC) == 0
         for y in range(NY):
             for zh in range(NH):
-                up.append((place(tile, y, zh), place(tile + 1, y, 1 - zh if far else zh)))
-    return up, [(j, i) for i, j in up]
+                here, there = place(tile, y, zh), place(tile + 1, y, 1 - zh if far else zh)
+                (hop if tile % 2 else chip).extend([(here, there), (there, here)])
+                down.append((there, here))
+    return chip, hop, down
 
 
 def on_device(star_slot, star_block, exposure, superpixel, magnitude, weight):
-    y = lax.axis_index("y")
     zh = lax.axis_index("zh")
-    pos = jnp.stack([y, zh]).astype(I32)
-    up, down = flat_pairs()
+    chip, hop, down = flat_pairs()
     obs = call(
         pack_kernel, "pack", [(4, 8, 512)],
         (star_block, star_slot[0], exposure[0], superpixel[0], magnitude[0], weight[0]), smem=1,
@@ -365,40 +441,38 @@
     expo = expo.reshape(NZ, NH, 8, LO).sum(axis=0)
     expo = jnp.where(zh == 0, expo, expo[::-1]).reshape(16, LO)
     both = jnp.stack([obs, partner])
+    expo, both = lax.optimization_barrier((expo, both))
     tile_obs = exchange(jnp.broadcast_to(both[None], (NY, *both.shape)), "y")
     tile_obs = tile_obs.reshape(8, 4, 8, 512)
     expo, tile_obs = lax.optimization_barrier((expo, tile_obs))
     expo = exchange(jnp.broadcast_to(expo[None], (32, 16, LO)), ("x", "c", "y"))
-    g0s, ds, cs, g0f, df, cf, ru, top, bot = call(
+    g0s, ds, cs, g0f, df, cf, ru, hop_row, chip_row = call(
         tile_kernel, "tile",
         [(4, 8, LO)] * 3 + [(16, LO)] * 3 + [(8, LO)] + [(2, LO)] * 2,
-        (pos, tile_obs), smem=1,
-        scratch=[pltpu.VMEM((4, LO, 4096), BF16)] * 2 + [pltpu.VMEM((4, 1, 4096), F32)],
+        (tile_obs,),
+        scratch=[pltpu.VMEM((4, LO, 4096), BF16)] * 2 + [pltpu.VMEM((4, 8, 4096), F32)],
         flops=1 << 30,
     )
-    above = lax.ppermute(bot, ALL, up)
-    below = lax.ppermute(top, ALL, down)
+    by_hop = lax.ppermute(hop_row, ALL, hop)
+    by_chip = lax.ppermute(chip_row, ALL, chip)
     cs, ys, cf, yf, g0z, dz, first = call(
         expo_apply_kernel, "apply",
         [(4, 8, LO)] * 2 + [(16, LO)] * 2 + [(4, 8, LO)] * 2 + [(2, LO)],
-        (tile_obs, expo, g0f, cs, cf, ds, df, above, below),
+        (tile_obs, expo, g0f, cs, cf, ds, df, by_hop, by_chip),
         flops=1 << 30,
     )
     next_first = lax.ppermute(first, ALL, down)
     payload = call(
         last_kernel, "last", [(24, LO)],
-        (pos, tile_obs, g0s, ds, cs, ys, g0f, df, cf, yf, ru), smem=1,
+        (tile_obs, g0s, ds, cs, ys, g0f, df, cf, yf, ru),
         flops=1 << 28,
     )
-    edge = -(0.5 * SMOOTH) * (yf[7] * next_first[0] + yf[15] * next_first[1])
-    payload = payload + jnp.where(
-        lax.broadcasted_iota(I32, (24, LO), 0) == 19, edge[None], 0.0
-    )
-    sums = exchange(jnp.broadcast_to(payload[None], (NZ, 24, LO)), "zl").sum(axis=0)
+    payload = call(edge_kernel, "edge", [(NZ, 24, LO)], (payload, yf, next_first))
+    sums = exchange(payload, "zl").sum(axis=0)
     sums = exchange(jnp.broadcast_to(sums[None], (32, 24, LO)), ("x", "c", "y"))
     star, zero, flat = call(
         finish_kernel, "finish", [(4, LO), (4, LO), (8, 2 * LO)],
-        (pos, sums, g0z, dz, g0s, ys, g0f, yf), smem=1,
+        (sums, g0z, dz, g0s, ys, g0f, yf),
     )
     return star.reshape(-1), zero.reshape(-1), flat
 

time: 139 us -> 132 us (0.950)
  blocking collectives: 44.7 us -> 54.6 us
  waiting for transfers between devices: 14.8 us -> 5.49 us
  starting transfers between devices: 46.2 us -> 41.9 us
  other arithmetic: 2.17 us -> 0.04 us
    all_to_all x2 -> x3, blocking collectives: 44.7 us -> 54.6 us  [exchange(): return lax.all_to_all(blocks, axes, 0, 0, tiled=True)]
    all_to_all x3 -> x2, waiting for transfers between devices: 8.21 us -> 0.01 us  [exchange(): return lax.all_to_all(blocks, axes, 0, 0, tiled=True)]
    all_to_all x3 -> x2, starting transfers between devices: 27.3 us -> 22.8 us  [exchange(): return lax.all_to_all(blocks, axes, 0, 0, tiled=True)]
    ppermute x2, waiting for transfers between devices: 2.93 us -> 1.11 us  [the longest x1 1.1 us: on_device(): by_chip = lax.ppermute(chip_row, ALL, chip)]
    pallas_call x6 -> x7, Pallas kernels: 25.8 us -> 25.1 us  [call(): pl.pallas_call(kernel, name=name, out_shape=tuple(out) if many else out[0...]
  transfers between devices with their start and end apart: 7 -> 6, of which waited for: 4 -> 3; matrix products, arithmetic and copies ran while one was open for 1% -> 0% of each run, Pallas kernels for 10% -> 10%
where the time goes in v2:
time: 132 us; the launch traced here: 131 us
  blocking collectives  54.6 us (41%)
  starting transfers between devices  41.9 us (32%)
  Pallas kernels  25.1 us (19%)
  waiting for transfers between devices  5.49 us (4%)
  local copies, waits for them, and re-layouts  3.38 us (3%)
    all_to_all x3, blocking collectives, exchange(): return lax.all_to_all(blocks, axes, 0, 0, tiled=True)  54.6 us
    pallas_call x7, Pallas kernels, call(): pl.pallas_call(kernel, name=name, out_shape=tuple(out) if many else out[0...  25.1 us
    all_to_all x2, starting transfers between devices, exchange(): return lax.all_to_all(blocks, axes, 0, 0, tiled=True)  22.8 us
    ppermute x1, starting transfers between devices, on_device(): partner = lax.ppermute(obs, 'zh', [(0, 1), (1, 0)])  12 us
    ppermute x1, waiting for transfers between devices, on_device(): partner = lax.ppermute(obs, 'zh', [(0, 1), (1, 0)])  3.39 us
    ppermute x1, starting transfers between devices, on_device(): by_hop = lax.ppermute(hop_row, ALL, hop)  3.06 us
  transfers between devices with their start and end apart: 6, of which 3 were waited for; matrix products, arithmetic and copies ran while one was open for 0% of the time, Pallas kernels for 10%

profile of v2, /device:TPU:1, one launch (start us, length us, event | category | flops | bytes accessed | tf_op | source)
XLA Modules:
  0.0 131.3 jit_solution(10549150744702274215)
XLA Ops:
  0.6 1.5 %pack.1.obs_ref = f32[4,8,512]{2,1,0:T(8,128)} custom-call(s32[1,16]{1,0:T(1,128)} %block_ref.1, s32[16,128]{1,0:T(8,128)} %bitcast.19, s32[16,128]{1,0:T(8,128)} %bitcast.20, s32[16,128]{1,0:T(8,128)} %bitcast.21, f32[16,128]{1,0:T(8,128)} %bitcast.22, f32[16,128]{1,0:T(8,128)} %bitcast.23), custom_call_target="tpu_custom_call" | custom-call | bytes 1048576 | tf_op jit(solution)/shard_map/pack/pallas_call | solution.py:400
  2.1 1.8 %expo.1 = f32[16,8,128]{2,1,0:T(8,128)} custom-call(f32[4,8,512]{2,1,0:T(8,128)} %pack.1.obs_ref), custom_call_target="tpu_custom_call" | custom-call | bytes 1048576 | tf_op jit(solution)/shard_map/expo/pallas_call | solution.py:400
  3.9 15.9 %all-to-all-start = ((f32[16,8,128]{2,1,0:T(8,128)}), f32[16,8,128]{2,1,0:T(8,128)S(1)}, u32[]{:S(2)}, u32[]{:S(2)}) async-start(f32[16,8,128]{2,1,0:T(8,128)} %expo.1), calls=%async_computation | async-start | bytes 131072 | tf_op jit(solution)/shard_map/all_to_all | solution.py:412
  19.8 12.0 %collective-permute-start = (f32[4,8,512]{2,1,0:T(8,128)S(1)}, f32[4,8,512]{2,1,0:T(8,128)S(1)}, u32[]{:S(2)}, u32[]{:S(2)}) collective-permute-start(f32[4,8,512]{2,1,0:T(8,128)S(1)} %copy-done), channel_id=1, source_target_pairs={{0,1},{1,0},{2,3},{3,2},{4,5},{5,4},{6,7},{7,6},{8,9},{9,8},{10,11... | collective-permute-start | bytes 196616 | tf_op jit(solution)/shard_map/ppermute | solution.py:439
  31.8 3.4 %collective-permute-done = f32[4,8,512]{2,1,0:T(8,128)S(1)} collective-permute-done((f32[4,8,512]{2,1,0:T(8,128)S(1)}, f32[4,8,512]{2,1,0:T(8,128)S(1)}, u32[]{:S(2)}, u32[]{:S(2)}) %collective-permute-start) | collective-permute-done | bytes 65568 | tf_op jit(solution)/shard_map/ppermute | solution.py:439
  35.3 12.6 %all_to_all.25 = f32[4,2,4,8,512]{4,3,2,1,0:T(8,128)} all-to-all(f32[4,2,4,8,512]{4,3,2,1,0:T(8,128)S(1)} %broadcast_in_dim.6), channel_id=1, replica_groups=mesh['x'=4,'zl'=8,'c'=2,'y'=4,'zh'=2] {'y'}, dimensions={0} | all-to-all | bytes 1048576 | tf_op jit(solution)/shard_map/all_to_all | solution.py:412
  47.9 0.7 broadcast_in_dim.7
  48.6 7.0 %all-to-all-start.2 = ((f32[32,16,128]{2,1,0:T(8,128)}), f32[32,16,128]{2,1,0:T(8,128)S(1)}, u32[]{:S(2)}, u32[]{:S(2)}) async-start(f32[32,16,128]{2,1,0:T(8,128)} %broadcast_in_dim.7), calls=%async_computation.2 | async-start | bytes 524288 | tf_op jit(solution)/shard_map/all_to_all | solution.py:412
  55.6 10.1 %tile.1 = (f32[4,8,128]{2,1,0:T(8,128)}, f32[4,8,128]{2,1,0:T(8,128)}, f32[4,8,128]{2,1,0:T(8,128)}, f32[16,128]{1,0:T(8,128)}, f32[16,128]{1,0:T(8,128)}, /*ind...) custom-call(f32[8,4,8,512]{3,2,1,0:T(8,128)} %bitcast.14), custom_call_target="tpu_custom_call" | custom-call | flops 1073741824 | bytes 1048576 | tf_op jit(solution)/shard_map/tile/pallas_call | solution.py:400
  65.7 0.7 copy-done.7
  66.4 3.1 %collective-permute-start.1 = (f32[2,128]{1,0:T(2,128)S(1)}, f32[2,128]{1,0:T(2,128)S(1)}, u32[]{:S(2)}, u32[]{:S(2)}) collective-permute-start(f32[2,128]{1,0:T(2,128)S(1)} %copy-done.7), channel_id=1, source_target_pairs={{8,16},{16,8},{9,17},{17,9},{10,18},{18,10},{11,19},{19,11},{12,20... | collective-permute-start | bytes 3080 | tf_op jit(solution)/shard_map/ppermute | solution.py:456
  69.5 1.9 %collective-permute-start.2 = (f32[2,128]{1,0:T(2,128)S(1)}, f32[2,128]{1,0:T(2,128)S(1)}, u32[]{:S(2)}, u32[]{:S(2)}) collective-permute-start(f32[2,128]{1,0:T(2,128)S(1)} %copy-done.6), channel_id=1, source_target_pairs={{0,8},{8,0},{1,9},{9,1},{2,10},{10,2},{3,11},{11,3},{4,12},{12,4},... | collective-permute-start | bytes 3080 | tf_op jit(solution)/shard_map/ppermute | solution.py:457
  71.4 1.1 collective-permute-done.2.chip_ref
  72.5 0.5 copy-done.4
  73.2 5.8 %apply.1 = (f32[4,8,128]{2,1,0:T(8,128)}, f32[4,8,128]{2,1,0:T(8,128)}, f32[16,128]{1,0:T(8,128)}, f32[16,128]{1,0:T(8,128)}, f32[4,8,128]{2,1,0:T(8,128)}, /*index=5*/f32[4,8,128]{2,1,0:T(8,128)}, f32[2,128]{1,0:T(2,128)}) custom-call(f32[8,4,8,512]{3,2,1,0:T(8,128)} %bitcast.15, f32[32,16,128]{2,1,0:T(8,128)} %copy-done.1, ...), custom_call_target="tpu_custom_call" | custom-call | flops 1073741824 | bytes 1048576 | tf_op jit(solution)/shard_map/apply/pallas_call | solution.py:400
  79.1 0.6 copy-done.5
  79.7 2.1 %collective-permute-start.3 = (f32[2,128]{1,0:T(2,128)S(1)}, f32[2,128]{1,0:T(2,128)S(1)}, u32[]{:S(2)}, u32[]{:S(2)}) collective-permute-start(f32[2,128]{1,0:T(2,128)S(1)} %copy-done.5), channel_id=1, source_target_pairs={{8,0},{9,1},{10,2},{11,3},{12,4},{13,5},{14,6},{15,7},{16,8},{17,9... | collective-permute-start | bytes 3080 | tf_op jit(solution)/shard_map/ppermute | solution.py:464
  81.8 2.7 %last.1.payload_ref = f32[24,128]{1,0:T(8,128)} custom-call(f32[8,4,8,512]{3,2,1,0:T(8,128)} %bitcast.16, f32[4,8,128]{2,1,0:T(8,128)} %get-tuple-element.29.g0s_ref, f32[4,8,128]{2,1,0:T(8,128)} %get-tuple-element.30.ds_ref, f32[4,8,128]{2,1,0:T(8,128)} %get-tuple-element.38.cs_ref, f32[4,8,128]{2,1,0:T(8,128)} %get-tuple-element.39.ys_ref, ...), custom_call_target="tpu_custom_call" | custom-call | flops 268435456 | bytes 1048576 | tf_op jit(solution)/shard_map/last/pallas_call | solution.py:400
  84.5 1.0 collective-permute-done.3.next_ref
  85.5 0.6 copy-done.2
  86.0 1.4 %edge.1 = f32[8,24,128]{2,1,0:T(8,128)} custom-call(f32[24,128]{1,0:T(8,128)} %last.1.payload_ref, f32[16,128]{1,0:T(8,128)} %get-tuple-element.41.yf_ref, f32[2,128]{1,0:T(2,128)} %copy-done.2), custom_call_target="tpu_custom_call" | custom-call | bytes 1048576 | tf_op jit(solution)/shard_map/edge/pallas_call | solution.py:400
  87.4 25.4 %all_to_all.26 = f32[8,24,128]{2,1,0:T(8,128)S(1)} all-to-all(f32[8,24,128]{2,1,0:T(8,128)} %edge.1), channel_id=1, replica_groups=mesh['x'=4,'zl'=8,'c'=2,'y'=4,'zh'=2] {'zl'}, dimensions={0} | all-to-all | bytes 196608 | tf_op jit(solution)/shard_map/all_to_all | solution.py:412
  112.8 16.7 %all_to_all.27.sums_ref = f32[32,24,128]{2,1,0:T(8,128)} all-to-all(f32[32,24,128]{2,1,0:T(8,128)S(1)} %broadcast_in_dim.8), channel_id=1, replica_groups=mesh['x'=4,'zl'=8,'c'=2,'y'=4,'zh'=2] {'x','c','y'}, dimensions={0} | all-to-all | bytes 786432 | tf_op jit(solution)/shard_map/all_to_all | solution.py:412
  129.5 1.8 %finish.1 = (f32[4,128]{1,0:T(4,128)}, f32[4,128]{1,0:T(4,128)}, f32[8,256]{1,0:T(8,128)}) custom-call(f32[32,24,128]{2,1,0:T(8,128)} %all_to_all.27.sums_ref, f32[4,8,128]{2,1,0:T(8,128)} %get-tuple-element.44.g0z_ref, f32[4,8,128]{2,1,0:T(8,128)} %get-tuple-element.45.dz_ref, f32[4,8,128]{2,1,0:T(8,128)} %get-tuple-element.29.g0s_ref, ...), custom_call_target="tpu_custom_call" | custom-call | bytes 1048576 | tf_op jit(solution)/shard_map/finish/pallas_call | solution.py:400
  (21 shorter events, 0.3 us)
Async XLA Ops:
  3.9 15.9 %copy-start = (f32[4,8,512]{2,1,0:T(8,128)S(1)}, f32[4,8,512]{2,1,0:T(8,128)}, u32[]{:S(2)}) copy-start(f32[4,8,512]{2,1,0:T(8,128)} %pack.1.obs_ref) | copy-start | bytes 196612
  3.9 31.3 %all-to-all-start = ((f32[16,8,128]{2,1,0:T(8,128)}), f32[16,8,128]{2,1,0:T(8,128)S(1)}, u32[]{:S(2)}, u32[]{:S(2)}) async-start(f32[16,8,128]{2,1,0:T(8,128)} %expo.1), calls=%async_computation | async-start | bytes 131072 | tf_op jit(solution)/shard_map/all_to_all | solution.py:412
  19.8 15.4 %collective-permute-start = (f32[4,8,512]{2,1,0:T(8,128)S(1)}, f32[4,8,512]{2,1,0:T(8,128)S(1)}, u32[]{:S(2)}, u32[]{:S(2)}) collective-permute-start(f32[4,8,512]{2,1,0:T(8,128)S(1)} %copy-done), channel_id=1, source_target_pairs={{0,1},{1,0},{2,3},{3,2},{4,5},{5,4},{6,7},{7,6},{8,9},{9,8},{10,11... | collective-permute-start | bytes 196616 | tf_op jit(solution)/shard_map/ppermute | solution.py:439
  48.6 23.9 %all-to-all-start.2 = ((f32[32,16,128]{2,1,0:T(8,128)}), f32[32,16,128]{2,1,0:T(8,128)S(1)}, u32[]{:S(2)}, u32[]{:S(2)}) async-start(f32[32,16,128]{2,1,0:T(8,128)} %broadcast_in_dim.7), calls=%async_computation.2 | async-start | bytes 524288 | tf_op jit(solution)/shard_map/all_to_all | solution.py:412
  65.7 0.7 copy-start.7
  66.4 3.1 %copy-start.6 = (f32[2,128]{1,0:T(2,128)S(1)}, f32[2,128]{1,0:T(2,128)}, u32[]{:S(2)}) copy-start(f32[2,128]{1,0:T(2,128)} %get-tuple-element.37) | copy-start | bytes 3076
  66.4 5.0 %collective-permute-start.1 = (f32[2,128]{1,0:T(2,128)S(1)}, f32[2,128]{1,0:T(2,128)S(1)}, u32[]{:S(2)}, u32[]{:S(2)}) collective-permute-start(f32[2,128]{1,0:T(2,128)S(1)} %copy-done.7), channel_id=1, source_target_pairs={{8,16},{16,8},{9,17},{17,9},{10,18},{18,10},{11,19},{19,11},{12,20... | collective-permute-start | bytes 3080 | tf_op jit(solution)/shard_map/ppermute | solution.py:456
  69.5 3.1 %collective-permute-start.2 = (f32[2,128]{1,0:T(2,128)S(1)}, f32[2,128]{1,0:T(2,128)S(1)}, u32[]{:S(2)}, u32[]{:S(2)}) collective-permute-start(f32[2,128]{1,0:T(2,128)S(1)} %copy-done.6), channel_id=1, source_target_pairs={{0,8},{8,0},{1,9},{9,1},{2,10},{10,2},{3,11},{11,3},{4,12},{12,4},... | collective-permute-start | bytes 3080 | tf_op jit(solution)/shard_map/ppermute | solution.py:457
  71.4 1.1 copy-start.3
  72.5 0.6 copy-start.4
  72.5 0.7 copy-start.1
  79.1 0.6 copy-start.5
  79.7 5.8 %collective-permute-start.3 = (f32[2,128]{1,0:T(2,128)S(1)}, f32[2,128]{1,0:T(2,128)S(1)}, u32[]{:S(2)}, u32[]{:S(2)}) collective-permute-start(f32[2,128]{1,0:T(2,128)S(1)} %copy-done.5), channel_id=1, source_target_pairs={{8,0},{9,1},{10,2},{11,3},{12,4},{13,5},{14,6},{15,7},{16,8},{17,9... | collective-permute-start | bytes 3080 | tf_op jit(solution)/shard_map/ppermute | solution.py:464
  85.5 0.6 copy-start.2

commit v3 on v2

v3 whole, which is shorter than its diff:
```python
import jax
import jax.numpy as jnp
from jax import lax
from jax.experimental import pallas as pl
from jax.experimental.pallas import tpu as pltpu
from jax.sharding import Mesh
from jax.sharding import PartitionSpec as P

SMOOTH = 2.0
RIDGE = 0.5
LO, HALF, HI = 128, 64, 16
NX, NZ, NC, NY, NH = 4, 8, 2, 4, 2
ALL = ("x", "zl", "c", "y", "zh")
PLANE = ("x", "c", "y")
F32 = jnp.float32
I32 = jnp.int32
BF16 = jnp.bfloat16
NT = (((1,), (1,)), ((), ()))
NN = (((1,), (0,)), ((), ()))
S_LO, S_HI, P_LO, P_HI, E_LO, E_HI, W, WM = range(8)
STAR, FLAT = 3, 7


def split3(v):
    first = v.astype(BF16)
    rest = v - first.astype(F32)
    second = rest.astype(BF16)
    return first, second, (rest - second.astype(F32)).astype(BF16)


def row(x, f):
    return x[f : f + 1]


def row_iota(shape):
    return lax.broadcasted_iota(I32, shape, 0)


def lane_tiles(n):
    return [slice(i, i + LO) for i in range(0, n, LO)]


def is_row(ids, count):
    rows = row_iota((count, LO)).astype(F32).astype(ids.dtype)
    return [rows == jnp.broadcast_to(ids[:, at], (count, LO)) for at in lane_tiles(ids.shape[1])]


def onehot(lo, size):
    one, zero = jnp.ones((), BF16), jnp.zeros((), BF16)
    return jnp.concatenate([jnp.where(same, one, zero) for same in is_row(lo, size)], axis=1)


def scatter(values, hi, hot):
    masks = is_row(hi, HI)
    zero = jnp.zeros((), BF16)
    rows = jnp.concatenate(
        [
            jnp.concatenate(
                [
                    jnp.where(mask, jnp.broadcast_to(part[:, at], (HI, LO)), zero)
                    for mask, at in zip(masks, lane_tiles(hi.shape[1]))
                ],
                axis=1,
            )
            for value in values
            for part in value
        ],
        axis=0,
    )
    sums = lax.dot_general(rows, hot, NT, preferred_element_type=F32)
    sums = [sums[at : at + HI] for at in range(0, sums.shape[0], HI)]
    return [sums[i] + sums[i + 1] + sums[i + 2] for i in range(0, len(sums), 3)]


def picked(table, hi, hot):
    parts = jnp.concatenate([part.astype(F32) for part in split3(table)], axis=0).astype(BF16)
    parts = lax.dot_general(parts, hot, NN, preferred_element_type=F32)
    found = parts[:HI] + parts[HI : 2 * HI] + parts[2 * HI :]
    found = jnp.where(row_iota(found.shape).astype(F32) == hi, found, 0.0)
    return found[:8] + found[8:]


def folded(a, *shifts):
    for shift in shifts:
        a = a + pltpu.roll(a, shift, 0)
    return a


def gather(table, hi, hot):
    return folded(picked(table, hi, hot), 4, 2, 1)


def gather_both(first, second):
    a, b = folded(picked(*first), 4), folded(picked(*second), 4)
    return folded(jnp.where(row_iota(a.shape) & 7 < 4, a, b), 2, 1)


def pack_kernel(block_ref, slot_ref, expo_ref, pix_ref, mag_ref, w_ref, out_ref):
    rows = row_iota((8, LO))
    for r in range(16):
        star = slot_ref[r : r + 1, :] + (block_ref[0, r] * 256 + ((r // 2) % 2) * 512)
        pix = pix_ref[r : r + 1, :]
        expo = expo_ref[r : r + 1, :]
        w = w_ref[r : r + 1, :]
        ids = (
            star & 63,
            ((star >> 6) & 1) * 8 + (star >> 7),
            pix & 127,
            ((pix >> 7) & 1) * 8 + (pix >> 8),
            expo & 63,
            ((expo >> 6) & 1) * 4 + (expo >> 7),
        )
        tile = jnp.zeros((8, LO), I32)
        for f, field in enumerate(ids):
            tile = jnp.where(rows == f, field, tile)
        tile = jnp.where(rows == W, w, tile.astype(F32))
        tile = jnp.where(rows == WM, w * mag_ref[r : r + 1, :], tile)
        out_ref[r // 4, :, (r % 4) * LO : (r % 4 + 1) * LO] = tile


def expo_kernel(obs_ref, out_ref):
    x = jnp.concatenate([obs_ref[k] for k in range(4)], axis=1)
    parts = split3(x)
    weighted, count = scatter(
        [[row(part, WM) for part in parts], [row(part, W) for part in parts]],
        row(parts[0], E_HI),
        onehot(row(parts[0], E_LO), HALF),
    )
    both = jnp.concatenate([weighted[:8], count[:8]], axis=1)
    for peer in range(NZ * NH):
        out_ref[peer] = both


def fields_of(obs_ref, k):
    return jnp.concatenate([obs_ref[g, k] for g in range(8)], axis=1)


def own_fields(obs_ref, y, k):
    return jnp.concatenate([obs_ref[2 * y + rel, k] for rel in range(2)], axis=1)


def expo_hi(x):
    hi = row(x, E_HI)
    rel = (lax.broadcasted_iota(I32, hi.shape, 1) >> 9) & 1
    return hi + 8.0 * rel.astype(F32)


def by_rel(pair):
    return jnp.concatenate([pair[:8], pair[8:]], axis=1)


def sums_kernel(obs_ref, g0s_ref, ds_ref, g0f_ref, df_ref, hop_ref, chip_ref):
    g0f_ref[...] = jnp.zeros((HI, LO), F32)
    df_ref[...] = jnp.zeros((HI, LO), F32)

    def sums(k, carry):
        parts = split3(fields_of(obs_ref, k))
        values = [[row(part, WM) for part in parts], [row(part, W) for part in parts]]
        weighted, count = scatter(values, row(parts[0], S_HI), onehot(row(parts[0], S_LO), HALF))
        diag = count + RIDGE
        g0s_ref[k] = weighted / diag
        ds_ref[k] = diag
        weighted, count = scatter(values, row(parts[0], P_HI), onehot(row(parts[0], P_LO), LO))
        g0f_ref[...] += weighted
        df_ref[...] += count
        return carry

    lax.fori_loop(0, 4, sums, 0)
    diag = df_ref[...] + (4.0 * SMOOTH + RIDGE)
    g0f = g0f_ref[...] / diag
    df_ref[...] = diag
    g0f_ref[...] = g0f
    odd = lax.axis_index("c") == 1
    top = jnp.concatenate([g0f[0:1], g0f[8:9]], axis=0)
    bot = jnp.concatenate([g0f[7:8], g0f[15:16]], axis=0)
    hop_ref[...] = jnp.where(odd, bot, top)
    chip_ref[...] = jnp.where(odd, top, bot)


def couple_kernel(obs_ref, g0s_ref, g0f_ref, cs_ref, cf_ref, ru_ref, fit_ref):
    cf_ref[...] = jnp.zeros((HI, LO), F32)

    def couple(k, carry):
        x = fields_of(obs_ref, k)
        ids = x.astype(BF16)
        hs = onehot(row(ids, S_LO), HALF)
        hp = onehot(row(ids, P_LO), LO)
        fit = row(x, W) * gather_both(
            (g0s_ref[k], row(x, S_HI), hs), (g0f_ref[...], row(x, P_HI), hp)
        )
        parts = split3(fit)
        (cs_ref[k],) = scatter([[row(part, FLAT) for part in parts]], row(ids, S_HI), hs)
        (added,) = scatter([[row(part, STAR) for part in parts]], row(ids, P_HI), hp)
        cf_ref[...] += added
        fit_ref[k] = fit
        return carry

    lax.fori_loop(0, 4, couple, 0)
    y = lax.axis_index("y")
    total = jnp.zeros((HI, HALF), F32)
    for k in range(4):
        x = own_fields(obs_ref, y, k)
        fit = fit_ref[k, :, pl.ds(pl.multiple_of(y * 1024, 1024), 1024)]
        (added,) = scatter(
            [split3(row(fit, STAR) + row(fit, FLAT))],
            expo_hi(x).astype(BF16),
            onehot(row(x, E_LO).astype(BF16), HALF),
        )
        total += added
    ru_ref[...] = total


def beside(flat, above, below):
    left, right = flat[:8], flat[8:]
    rows = row_iota((8, LO))
    lanes = lax.broadcasted_iota(I32, (8, LO), 1)
    out = []
    left_up, right_up = pltpu.roll(left, 1, 1), pltpu.roll(right, 1, 1)
    left_down, right_down = pltpu.roll(left, 127, 1), pltpu.roll(right, 127, 1)
    sides = (
        jnp.where(lanes == 0, 0.0, left_up) + jnp.where(lanes == 127, right_down, left_down),
        jnp.where(lanes == 0, left_up, right_up) + jnp.where(lanes == 127, 0.0, right_down),
    )
    for i, half in enumerate((left, right)):
        upper = jnp.where(rows == 0, above[i : i + 1], pltpu.roll(half, 1, 0))
        lower = jnp.where(rows == 7, below[i : i + 1], pltpu.roll(half, 7, 0))
        out.append(sides[i] + upper + lower)
    return jnp.concatenate(out, axis=0)


def expo_apply_kernel(
    obs_ref, expo_ref, g0f_ref, cf_ref, df_ref, hop_ref, chip_ref,
    fit_ref, cf_out, yf_out, g0z_out, dz_out, top_out,
):
    for y in range(4):
        part = expo_ref[y]
        for xc in range(1, 8):
            part = part + expo_ref[xc * 4 + y]
        diag = part[:, HALF:] + RIDGE
        g0z_out[y] = part[:, :HALF] / diag
        dz_out[y] = diag
    cf_out[...] = cf_ref[...]

    def apply(k, carry):
        x = fields_of(obs_ref, k)
        ids = x.astype(BF16)
        hot = onehot(row(ids, E_LO), HALF)
        hi = expo_hi(x)
        found = [
            gather(g0z_out[y], hi[:, 1024 * y : 1024 * (y + 1)], hot[:, 1024 * y : 1024 * (y + 1)])
            for y in range(4)
        ]
        fit = row(x, W) * jnp.concatenate(found, axis=1)
        fit_ref[k] = fit
        parts = [row(part, 0) for part in split3(fit)]
        (added,) = scatter([parts], row(ids, P_HI), onehot(row(ids, P_LO), LO))
        cf_out[...] += added
        return carry

    lax.fori_loop(0, 4, apply, 0)
    odd = lax.axis_index("c") == 1
    above = jnp.where(odd, chip_ref[...], hop_ref[...])
    below = jnp.where(odd, hop_ref[...], chip_ref[...])
    cf = cf_out[...] - SMOOTH * beside(g0f_ref[...], above, below)
    cf_out[...] = cf
    yf = cf / df_ref[...]
    yf_out[...] = yf
    top_out[...] = jnp.concatenate([yf[0:1], yf[8:9]], axis=0)


def fold8(a):
    total = a[0:8]
    for i in range(8, a.shape[0], 8):
        total = total + a[i : i + 8]
    total = jnp.sum(total, axis=0, keepdims=True)
    if total.shape[1] < LO:
        total = jnp.concatenate([total, jnp.zeros((1, LO - total.shape[1]), F32)], axis=1)
    return total


def fold_lanes(a):
    total = a[:, 0:LO]
    for i in range(LO, a.shape[1], LO):
        total = total + a[:, i : i + LO]
    return total


def last_kernel(
    obs_ref, fit_ref, g0s_ref, ds_ref, cs_ref, g0f_ref, df_ref, cf_ref, yf_ref, ru_ref, ys_ref, out_ref
):
    star = jnp.zeros((3, LO), F32)
    rho, beta, eta = row(star, 0), row(star, 1), row(star, 2)

    def finish_star(k, sums):
        ids = fields_of(obs_ref, k).astype(BF16)
        parts = [row(part, 0) for part in split3(fit_ref[k])]
        (added,) = scatter([parts], row(ids, S_HI), onehot(row(ids, S_LO), HALF))
        g0s, ds = g0s_ref[k], ds_ref[k]
        cs = cs_ref[k] + added
        ys = cs / ds
        ys_ref[k] = ys
        return (
            sums[0] + fold8(g0s * g0s * ds),
            sums[1] + fold8(g0s * cs),
            sums[2] + fold8(cs * ys),
        )

    rho, beta, eta = lax.fori_loop(0, 4, finish_star, (rho, beta, eta))
    y = lax.axis_index("y")
    total = jnp.zeros((HI, HALF), F32)
    cross = jnp.zeros((1, LO), F32)
    yf = yf_ref[...]
    for k in range(4):
        x = own_fields(obs_ref, y, k)
        ids = x.astype(BF16)
        w = row(x, W)
        both = gather_both(
            (ys_ref[k], row(x, S_HI), onehot(row(ids, S_LO), HALF)),
            (yf, row(x, P_HI), onehot(row(ids, P_LO), LO)),
        )
        from_star, from_flat = row(both, STAR), row(both, FLAT)
        (added,) = scatter(
            [split3(w * (from_star + from_flat))],
            expo_hi(x).astype(BF16),
            onehot(row(ids, E_LO), HALF),
        )
        total += added
        cross += fold_lanes(w * from_star * from_flat)
    ru = ru_ref[...]
    out_ref[0:16] = jnp.concatenate([ru, total], axis=1)
    g0f, df, cf = g0f_ref[...], df_ref[...], cf_ref[...]
    none = jnp.zeros((2, LO), F32)
    rho = 0.25 * (rho + fold8(g0f * g0f * df))
    beta = 0.25 * (beta + fold8(g0f * cf))
    eta = 0.25 * (eta + fold8(cf * yf))
    delta = 2.0 * cross - (0.25 * SMOOTH) * fold8(yf * beside(yf, none, none))
    out_ref[16:24] = jnp.concatenate([rho, beta, eta, delta, jnp.zeros((4, LO), F32)], axis=0)


def edge_kernel(payload_ref, yf_ref, next_ref, out_ref):
    edge = yf_ref[7:8] * next_ref[0:1] + yf_ref[15:16] * next_ref[1:2]
    edge = jnp.where(row_iota((8, LO)) == 3, -(0.5 * SMOOTH) * edge, 0.0)
    scal = payload_ref[16:24] + edge
    for peer in range(NZ):
        out_ref[peer, 0:16] = payload_ref[0:16]
        out_ref[peer, 16:24] = scal


def whole(a):
    return jnp.sum(jnp.sum(a, axis=0, keepdims=True), axis=1, keepdims=True)


def finish_kernel(
    sums_ref, g0z_ref, dz_ref, g0s_ref, ys_ref, g0f_ref, yf_ref, star_out, zero_out, flat_out
):
    y, zh = lax.axis_index("y"), lax.axis_index("zh")
    scal = sums_ref[0, 16:24]
    for peer in range(1, 32):
        scal = scal + sums_ref[peer, 16:24]
    z_rho = jnp.zeros((HI, HALF), F32)
    z_beta, z_eta, z_delta = z_rho, z_rho, z_rho
    z_own = z_rho
    for i in range(4):
        part = sums_ref[i, 0:16]
        for xc in range(1, 8):
            part = part + sums_ref[xc * 4 + i, 0:16]
        cz, qz = part[:, :HALF], part[:, HALF:]
        g0z, dz = g0z_ref[i], dz_ref[i]
        yz = cz / dz
        z_rho += g0z * g0z * dz
        z_beta += g0z * cz
        z_eta += cz * yz
        z_delta += qz * yz
        z_own = jnp.where(i == y, yz, z_own)
    rho0 = whole(z_rho) + whole(scal[0:1])
    beta = whole(z_beta) + whole(scal[1:2])
    eta = whole(z_eta) + whole(scal[2:3])
    delta = 2.0 * whole(z_delta) + whole(scal[3:4])
    curv0 = rho0 + beta
    step0 = rho0 / curv0
    left = beta / curv0
    rho1 = left * left * rho0 - 2.0 * step0 * left * beta + step0 * step0 * eta
    curv_g = (
        left * left * curv0
        - 2.0 * step0 * left * (beta + eta)
        + step0 * step0 * (eta + delta)
    )
    ratio = rho1 / rho0
    mixed = left * curv0 - step0 * (beta + eta)
    curv1 = curv_g + 2.0 * ratio * mixed + ratio * ratio * curv0
    step1 = rho1 / curv1
    along_g = step0 + step1 * (left + ratio)
    along_y = -step1 * step0
    star = by_rel(along_g * g0s_ref[y] + along_y * ys_ref[y])
    star_out[...] = jnp.where(zh == 0, star, pltpu.roll(star, 4, 0))[0:4]
    zero = along_g * g0z_ref[y] + along_y * z_own
    zero_out[...] = jnp.concatenate([zero[0:4], pltpu.roll(zero[0:8], 4, 0)[0:4]], axis=1)
    flat_out[...] = by_rel(along_g * g0f_ref[...] + along_y * yf_ref[...])


VMEM = pl.BlockSpec(memory_space=pltpu.VMEM)
SMEM = pl.BlockSpec(memory_space=pltpu.SMEM)


def call(kernel, shapes, args, smem=0, scratch=(), mib=8, work=20):
    out = [jax.ShapeDtypeStruct(shape, F32) for shape in shapes]
    many = len(out) > 1
    return pl.pallas_call(
        kernel,
        name=kernel.__name__,
        out_shape=tuple(out) if many else out[0],
        in_specs=[SMEM] * smem + [VMEM] * (len(args) - smem),
        out_specs=tuple([VMEM] * len(out)) if many else VMEM,
        scratch_shapes=list(scratch),
        compiler_params=pltpu.CompilerParams(vmem_limit_bytes=mib << 20),
        cost_estimate=pl.CostEstimate(flops=1 << work, bytes_accessed=1 << 20, transcendentals=0),
    )(*args)


def exchange(blocks, axes):
    return lax.all_to_all(blocks, axes, 0, 0, tiled=True)


def to_all(block, peers, axes):
    return exchange(jnp.broadcast_to(block[None], (peers, *block.shape)), axes)


def flat_pairs():
    def place(tile, y, zh):
        x, rest = divmod(tile, NZ * NC)
        zl, c = divmod(rest, NC)
        return (((x * NZ + zl) * NC + c) * NY + y) * NH + zh

    chip, hop, down = [], [], []
    for tile in range(NX * NZ * NC - 1):
        far = (tile + 1) % (NZ * NC) == 0
        for y in range(NY):
            for zh in range(NH):
                here, there = place(tile, y, zh), place(tile + 1, y, 1 - zh if far else zh)
                (hop if tile % 2 else chip).extend([(here, there), (there, here)])
                down.append((there, here))
    return chip, hop, down


def on_device(star_slot, star_block, exposure, superpixel, magnitude, weight):
    zh = lax.axis_index("zh")
    chip, hop, down = flat_pairs()
    stars, flats = (4, HI, HALF), (HI, LO)
    obs = call(
        pack_kernel, [(4, 8, 512)],
        (star_block, star_slot[0], exposure[0], superpixel[0], magnitude[0], weight[0]), smem=1,
    )
    partner = lax.ppermute(obs, "zh", [(0, 1), (1, 0)])
    expo = exchange(call(expo_kernel, [(16, 8, LO)], (obs,)), ("zl", "zh"))
    expo = expo.reshape(NZ, NH, 8, LO).sum(axis=0)
    expo = jnp.where(zh == 0, expo, expo[::-1]).reshape(HI, LO)
    both = jnp.stack([obs, partner])
    expo, both = lax.optimization_barrier((expo, both))
    tile_obs = to_all(both, NY, "y").reshape(8, 4, 8, 512)
    expo, tile_obs = lax.optimization_barrier((expo, tile_obs))
    expo = to_all(expo, 32, PLANE)
    g0s, ds, g0f, df, hop_row, chip_row = call(
        sums_kernel, [stars] * 2 + [flats] * 2 + [(2, LO)] * 2, (tile_obs,), mib=16, work=29
    )
    by_hop = lax.ppermute(hop_row, ALL, hop)
    by_chip = lax.ppermute(chip_row, ALL, chip)
    cs, cf, ru = call(
        couple_kernel, [stars, flats, (HI, HALF)], (tile_obs, g0s, g0f),
        scratch=[pltpu.VMEM((4, 8, 4096), F32)], mib=16, work=30,
    )
    fit, cf, yf, g0z, dz, first = call(
        expo_apply_kernel, [(4, 8, 4096)] + [flats] * 2 + [stars] * 2 + [(2, LO)],
        (tile_obs, expo.reshape(32, HI, LO), g0f, cf, df, by_hop, by_chip), mib=16, work=30,
    )
    next_first = lax.ppermute(first, ALL, down)
    ys, payload = call(
        last_kernel, [stars, (24, LO)],
        (tile_obs, fit, g0s, ds, cs, g0f, df, cf, yf, ru), mib=16, work=30,
    )
    payload = call(edge_kernel, [(NZ, 24, LO)], (payload, yf, next_first))
    sums = exchange(payload, "zl").sum(axis=0)
    sums = to_all(sums, 32, PLANE)
    star, zero, flat = call(
        finish_kernel, [(4, LO), (4, LO), (8, 2 * LO)], (sums, g0z, dz, g0s, ys, g0f, yf)
    )
    return star.reshape(-1), zero.reshape(-1), flat


def solution(mesh):
    split = Mesh(mesh.devices.reshape(NX, NZ, NC, NY, NH), ALL)
    tile, loop = ("x", "zl", "c"), ("y", "zh")
    placed = (
        P(tile, loop, None),
        P(tile, loop),
        P(tile, loop, None),
        P(tile, loop, None),
        P(tile, loop, None),
        P(tile, loop, None),
    )
    return jax.shard_map(
        on_device,
        mesh=split,
        in_specs=placed,
        out_specs=(P(ALL), P(loop), P(tile, None)),
        check_vma=False,
    )
```

time: 132 us -> 121 us (0.917)
  Pallas kernels: 25.1 us -> 14.5 us
    pallas_call x7 -> x8, Pallas kernels: 25.1 us -> 14.5 us  [call(): pl.pallas_call(kernel, name=kernel.__name__, out_shape=tuple(out) if many...]
    unnamed x16 -> x12, local copies, waits for them, and re-layouts: 2.58 us -> 3.47 us
  transfers between devices with their start and end apart: 6 -> 6, of which waited for: 3 -> 2; matrix products, arithmetic and copies ran while one was open for 0% -> 0% of each run, Pallas kernels for 10% -> 8%
where the time goes in v3:
time: 121 us; the launch traced here: 120 us
  blocking collectives  53.9 us (45%)
  starting transfers between devices  41.9 us (35%)
  Pallas kernels  14.5 us (12%)
  waiting for transfers between devices  4.8 us (4%)
  local copies, waits for them, and re-layouts  4.26 us (4%)
    all_to_all x3, blocking collectives, exchange(): return lax.all_to_all(blocks, axes, 0, 0, tiled=True)  53.9 us
    all_to_all x2, starting transfers between devices, exchange(): return lax.all_to_all(blocks, axes, 0, 0, tiled=True)  22.7 us
    pallas_call x8, Pallas kernels, call(): pl.pallas_call(kernel, name=kernel.__name__, out_shape=tuple(out) if many...  14.5 us
    ppermute x1, starting transfers between devices, on_device(): partner = lax.ppermute(obs, 'zh', [(0, 1), (1, 0)])  12 us
    unnamed x12, local copies, waits for them, and re-layouts  3.47 us
    ppermute x1, waiting for transfers between devices, on_device(): partner = lax.ppermute(obs, 'zh', [(0, 1), (1, 0)])  3.41 us
    ppermute x1, starting transfers between devices, on_device(): by_hop = lax.ppermute(hop_row, ALL, hop)  2.92 us
  transfers between devices with their start and end apart: 6, of which 2 were waited for; matrix products, arithmetic and copies ran while one was open for 0% of the time, Pallas kernels for 8%

profile of v3, /device:TPU:1, one launch (start us, length us, event | category | flops | bytes accessed | tf_op | source)
XLA Modules:
  0.0 120.2 jit_solution(17658701139431807867)
XLA Ops:
  0.7 0.7 copy-done
  1.3 0.7 copy-done.1
  2.0 0.7 copy-done.2
  2.7 0.7 copy-done.3
  3.4 0.7 copy-done.4
  4.1 0.6 pack_kernel.1.obs_ref
  4.8 1.0 expo_kernel.1
  5.7 15.7 %all-to-all-start = ((f32[16,8,128]{2,1,0:T(8,128)}), f32[16,8,128]{2,1,0:T(8,128)S(1)}, u32[]{:S(2)}, u32[]{:S(2)}) async-start(f32[16,8,128]{2,1,0:T(8,128)} %expo_kernel.1), calls=%async_computation | async-start | bytes 131072 | tf_op jit(solution)/shard_map/all_to_all | solution.py:421
  21.5 12.0 %collective-permute-start = (f32[4,8,512]{2,1,0:T(8,128)S(1)}, f32[4,8,512]{2,1,0:T(8,128)S(1)}, u32[]{:S(2)}, u32[]{:S(2)}) collective-permute-start(f32[4,8,512]{2,1,0:T(8,128)S(1)} %pack_kernel.1.obs_ref), channel_id=1, source_target_pairs={{0,1},{1,0},{2,3},{3,2},{4,5},{5,4},{6,7},{7,6},{8,9},{9,8},{10,11... | collective-permute-start | bytes 196616 | tf_op jit(solution)/shard_map/ppermute | solution.py:453
  33.5 3.4 %collective-permute-done = f32[4,8,512]{2,1,0:T(8,128)S(1)} collective-permute-done((f32[4,8,512]{2,1,0:T(8,128)S(1)}, f32[4,8,512]{2,1,0:T(8,128)S(1)}, u32[]{:S(2)}, u32[]{:S(2)}) %collective-permute-start) | collective-permute-done | bytes 65568 | tf_op jit(solution)/shard_map/ppermute | solution.py:453
  37.0 12.5 %all_to_all.25 = f32[4,2,4,8,512]{4,3,2,1,0:T(8,128)S(1)} all-to-all(f32[4,2,4,8,512]{4,3,2,1,0:T(8,128)S(1)} %broadcast_in_dim.6), channel_id=1, replica_groups=mesh['x'=4,'zl'=8,'c'=2,'y'=4,'zh'=2] {'y'}, dimensions={0} | all-to-all | bytes 1048576 | tf_op jit(solution)/shard_map/all_to_all | solution.py:421
  49.5 0.7 broadcast_in_dim.7
  50.2 7.0 %all-to-all-start.2 = ((f32[32,16,128]{2,1,0:T(8,128)}), f32[32,16,128]{2,1,0:T(8,128)S(1)}, u32[]{:S(2)}, u32[]{:S(2)}) async-start(f32[32,16,128]{2,1,0:T(8,128)} %broadcast_in_dim.7), calls=%async_computation.2 | async-start | bytes 524288 | tf_op jit(solution)/shard_map/all_to_all | solution.py:421
  57.2 2.9 %sums_kernel.1 = (f32[4,16,64]{2,1,0:T(8,128)S(1)}, f32[4,16,64]{2,1,0:T(8,128)S(1)}, f32[16,128]{1,0:T(8,128)S(1)}, f32[16,128]{1,0:T(8,128)S(1)}, f32[2,128]{1,0:T(2,128)S(1)}, /*index=5*/f32[2,128]{1,0:T(2,128)S(1)}) custom-call(f32[8,4,8,512]{3,2,1,0:T(8,128)S(1)} %bitcast.14), custom_call_target="tpu_custom_call" | custom-call | flops 536870912 | bytes 1048576 | tf_op jit(solution)/shard_map/sums_kernel/pallas_call | solution.py:408
  60.1 2.9 %collective-permute-start.1 = (f32[2,128]{1,0:T(2,128)S(1)}, f32[2,128]{1,0:T(2,128)S(1)}, u32[]{:S(2)}, u32[]{:S(2)}) collective-permute-start(f32[2,128]{1,0:T(2,128)S(1)} %get-tuple-element.35), channel_id=1, source_target_pairs={{8,16},{16,8},{9,17},{17,9},{10,18},{18,10},{11,19},{19,11},{12,20... | collective-permute-start | bytes 3080 | tf_op jit(solution)/shard_map/ppermute | solution.py:465
  63.1 1.9 %collective-permute-start.2 = (f32[2,128]{1,0:T(2,128)S(1)}, f32[2,128]{1,0:T(2,128)S(1)}, u32[]{:S(2)}, u32[]{:S(2)}) collective-permute-start(f32[2,128]{1,0:T(2,128)S(1)} %get-tuple-element.36), channel_id=1, source_target_pairs={{0,8},{8,0},{1,9},{9,1},{2,10},{10,2},{3,11},{11,3},{4,12},{12,4},... | collective-permute-start | bytes 3080 | tf_op jit(solution)/shard_map/ppermute | solution.py:466
  65.0 4.0 %couple_kernel.1 = (f32[4,16,64]{2,1,0:T(8,128)S(1)}, f32[16,128]{1,0:T(8,128)S(1)}, f32[16,64]{1,0:T(8,128)S(1)}) custom-call(f32[8,4,8,512]{3,2,1,0:T(8,128)S(1)} %bitcast.15, f32[4,16,64]{2,1,0:T(8,128)S(1)} %get-tuple-element.32.g0s_ref, f32[16,128]{1,0:T(8,128)S(1)} %get-tuple-element.31.g0f_ref), custom_call_target="tpu_custom_call" | custom-call | flops 1073741824 | bytes 1048576 | tf_op jit(solution)/shard_map/couple_kernel/pallas_call | solution.py:408
  69.0 2.7 %expo_apply_kernel.1 = (f32[4,8,4096]{2,1,0:T(8,128)S(1)}, f32[16,128]{1,0:T(8,128)S(1)}, f32[16,128]{1,0:T(8,128)S(1)}, f32[4,16,64]{2,1,0:T(8,128)S(1)}, f32[4...) custom-call(f32[8,4,8,512]{3,2,1,0:T(8,128)S(1)} %bitcast.16, f32[32,16,128]{2,1,0:T(8,128)S(1)} %all-to-all-done.2.expo_ref, ...), custom_call_target="tpu_custom_call" | custom-call | flops 1073741824 | bytes 1048576 | tf_op jit(solution)/shard_map/expo_apply_kernel/pallas_call | solution.py:408
  71.7 2.4 %collective-permute-start.3 = (f32[2,128]{1,0:T(2,128)S(1)}, f32[2,128]{1,0:T(2,128)S(1)}, u32[]{:S(2)}, u32[]{:S(2)}) collective-permute-start(f32[2,128]{1,0:T(2,128)S(1)} %get-tuple-element.44), channel_id=1, source_target_pairs={{8,0},{9,1},{10,2},{11,3},{12,4},{13,5},{14,6},{15,7},{16,8},{17,9... | collective-permute-start | bytes 3080 | tf_op jit(solution)/shard_map/ppermute | solution.py:475
  74.1 2.3 %last_kernel.1 = (f32[4,16,64]{2,1,0:T(8,128)S(1)}, f32[24,128]{1,0:T(8,128)S(1)}) custom-call(f32[8,4,8,512]{3,2,1,0:T(8,128)S(1)} %bitcast.17, f32[4,8,4096]{2,1,0:T(8,128)S(1)} %get-tuple-element.37.fit_ref, f32[4,16,64]{2,1,0:T(8,128)S(1)} %get-tuple-element.32.g0s_ref, f32[4,16,64]{2,1,0:T(8,128)S(1)} %get-tuple-element.38.ds_ref, ...), custom_call_target="tpu_custom_call" | custom-call | flops 1073741824 | bytes 1048576 | tf_op jit(solution)/shard_map/last_kernel/pallas_call | solution.py:408
  76.4 1.4 %collective-permute-done.3.next_ref = f32[2,128]{1,0:T(2,128)S(1)} collective-permute-done((f32[2,128]{1,0:T(2,128)S(1)}, f32[2,128]{1,0:T(2,128)S(1)}, u32[]{:S(2)}, u32[]{:S(2)}) %collective-permute-start.3) | collective-permute-done | bytes 1056 | tf_op jit(solution)/shard_map/ppermute | solution.py:475
  77.8 24.8 %all_to_all.26 = f32[8,24,128]{2,1,0:T(8,128)S(1)} all-to-all(f32[8,24,128]{2,1,0:T(8,128)S(1)} %edge_kernel.1), channel_id=1, replica_groups=mesh['x'=4,'zl'=8,'c'=2,'y'=4,'zh'=2] {'zl'}, dimensions={0} | all-to-all | bytes 196608 | tf_op jit(solution)/shard_map/all_to_all | solution.py:421
  102.6 16.6 %all_to_all.27.sums_ref = f32[32,24,128]{2,1,0:T(8,128)S(1)} all-to-all(f32[32,24,128]{2,1,0:T(8,128)S(1)} %broadcast_in_dim.8), channel_id=1, replica_groups=mesh['x'=4,'zl'=8,'c'=2,'y'=4,'zh'=2] {'x','c','y'}, dimensions={0} | all-to-all | bytes 786432 | tf_op jit(solution)/shard_map/all_to_all | solution.py:421
  119.2 1.0 finish_kernel.1
  (18 shorter events, 0.2 us)
Async XLA Ops:
  0.6 0.7 copy-start
  0.6 0.7 copy-start.5
  1.3 0.7 copy-start.1
  2.0 0.7 copy-start.2
  2.7 0.7 copy-start.3
  3.4 0.7 copy-start.4
  5.7 31.2 %all-to-all-start = ((f32[16,8,128]{2,1,0:T(8,128)}), f32[16,8,128]{2,1,0:T(8,128)S(1)}, u32[]{:S(2)}, u32[]{:S(2)}) async-start(f32[16,8,128]{2,1,0:T(8,128)} %expo_kernel.1), calls=%async_computation | async-start | bytes 131072 | tf_op jit(solution)/shard_map/all_to_all | solution.py:421
  21.5 15.4 %collective-permute-start = (f32[4,8,512]{2,1,0:T(8,128)S(1)}, f32[4,8,512]{2,1,0:T(8,128)S(1)}, u32[]{:S(2)}, u32[]{:S(2)}) collective-permute-start(f32[4,8,512]{2,1,0:T(8,128)S(1)} %pack_kernel.1.obs_ref), channel_id=1, source_target_pairs={{0,1},{1,0},{2,3},{3,2},{4,5},{5,4},{6,7},{7,6},{8,9},{9,8},{10,11... | collective-permute-start | bytes 196616 | tf_op jit(solution)/shard_map/ppermute | solution.py:453
  50.2 18.8 %all-to-all-start.2 = ((f32[32,16,128]{2,1,0:T(8,128)}), f32[32,16,128]{2,1,0:T(8,128)S(1)}, u32[]{:S(2)}, u32[]{:S(2)}) async-start(f32[32,16,128]{2,1,0:T(8,128)} %broadcast_in_dim.7), calls=%async_computation.2 | async-start | bytes 524288 | tf_op jit(solution)/shard_map/all_to_all | solution.py:421
  60.1 8.9 %collective-permute-start.1 = (f32[2,128]{1,0:T(2,128)S(1)}, f32[2,128]{1,0:T(2,128)S(1)}, u32[]{:S(2)}, u32[]{:S(2)}) collective-permute-start(f32[2,128]{1,0:T(2,128)S(1)} %get-tuple-element.35), channel_id=1, source_target_pairs={{8,16},{16,8},{9,17},{17,9},{10,18},{18,10},{11,19},{19,11},{12,20... | collective-permute-start | bytes 3080 | tf_op jit(solution)/shard_map/ppermute | solution.py:465
  63.1 5.9 %collective-permute-start.2 = (f32[2,128]{1,0:T(2,128)S(1)}, f32[2,128]{1,0:T(2,128)S(1)}, u32[]{:S(2)}, u32[]{:S(2)}) collective-permute-start(f32[2,128]{1,0:T(2,128)S(1)} %get-tuple-element.36), channel_id=1, source_target_pairs={{0,8},{8,0},{1,9},{9,1},{2,10},{10,2},{3,11},{11,3},{4,12},{12,4},... | collective-permute-start | bytes 3080 | tf_op jit(solution)/shard_map/ppermute | solution.py:466
  71.7 6.1 %collective-permute-start.3 = (f32[2,128]{1,0:T(2,128)S(1)}, f32[2,128]{1,0:T(2,128)S(1)}, u32[]{:S(2)}, u32[]{:S(2)}) collective-permute-start(f32[2,128]{1,0:T(2,128)S(1)} %get-tuple-element.44), channel_id=1, source_target_pairs={{8,0},{9,1},{10,2},{11,3},{12,4},{13,5},{14,6},{15,7},{16,8},{17,9... | collective-permute-start | bytes 3080 | tf_op jit(solution)/shard_map/ppermute | solution.py:475

commit v4 on v3

v4 whole, which is shorter than its diff:
```python
import jax
import jax.numpy as jnp
from jax import lax
from jax.experimental import pallas as pl
from jax.experimental.pallas import tpu as pltpu
from jax.sharding import Mesh
from jax.sharding import PartitionSpec as P

SMOOTH = 2.0
RIDGE = 0.5
LO, HALF, HI = 128, 64, 16
NX, NZ, NC, NY, NH = 4, 8, 2, 4, 2
ALL = ("x", "zl", "c", "y", "zh")
PLANE = ("x", "c", "y")
COLS = ("x", "c")
F32 = jnp.float32
I32 = jnp.int32
BF16 = jnp.bfloat16
NT = (((1,), (1,)), ((), ()))
NN = (((1,), (0,)), ((), ()))
S, PX, E, W, WM = range(5)
STAR, FLAT = 3, 7


def split3(v):
    first = v.astype(BF16)
    rest = v - first.astype(F32)
    second = rest.astype(BF16)
    return first, second, (rest - second.astype(F32)).astype(BF16)


def row_iota(shape):
    return lax.broadcasted_iota(I32, shape, 0)


def row(x, f):
    return x[f : f + 1]


def rows_of(tiles):
    return [row(tile, i) for tile in tiles for i in range(tile.shape[0])]


def small(ids):
    return ids.astype(F32).astype(BF16)


def joined(tiles):
    return jnp.concatenate(tiles, axis=1)


def is_row(ids, count):
    rows = row_iota((count, LO)).astype(F32).astype(ids[0].dtype)
    return [rows == jnp.broadcast_to(one, (count, LO)) for one in ids]


def onehot(lo, size):
    one, zero = jnp.ones((), BF16), jnp.zeros((), BF16)
    return joined([jnp.where(same, one, zero) for same in is_row(lo, size)])


def scatter(values, hi, hot):
    masks = is_row(hi, HI)
    zero = jnp.zeros((), BF16)
    rows = [
        joined([jnp.where(m, jnp.broadcast_to(p, (HI, LO)), zero) for m, p in zip(masks, part)])
        for value in values
        for part in value
    ]
    sums = lax.dot_general(jnp.concatenate(rows, axis=0), hot, NT, preferred_element_type=F32)
    sums = [sums[at : at + HI] for at in range(0, sums.shape[0], HI)]
    return [sums[i] + sums[i + 1] + sums[i + 2] for i in range(0, len(sums), 3)]


def picked(table, hi, hot):
    parts = jnp.concatenate([part.astype(F32) for part in split3(table)], axis=0).astype(BF16)
    parts = lax.dot_general(parts, hot, NN, preferred_element_type=F32)
    found = parts[:HI] + parts[HI : 2 * HI] + parts[2 * HI :]
    found = jnp.where(joined(is_row(hi, HI)), found, 0.0)
    return found[:8] + found[8:]


def folded(a, *shifts):
    for shift in shifts:
        a = a + pltpu.roll(a, shift, 0)
    return a


def gather(table, hi, hot):
    return folded(picked(table, hi, hot), 4, 2, 1)


def gather_both(first, second):
    a, b = folded(picked(*first), 4), folded(picked(*second), 4)
    return folded(jnp.where((row_iota(a.shape) & 7) < 4, a, b), 2, 1)


def across(x, f):
    return [x[f : f + 1, i : i + LO] for i in range(0, x.shape[1], LO)]


def split_rows(tiles):
    return [rows_of(part) for part in zip(*(split3(tile) for tile in tiles))]


class Ids:
    def __init__(self, tiles, size, offsets=None):
        ids = [tile.astype(I32) for tile in tiles]
        if offsets is None:
            high = [i >> 7 for i in ids]
        else:
            high = [((i >> 6) & 1) * 4 + (i >> 7) + at for i, at in zip(ids, offsets)]
        self.size = size
        self.low_rows = rows_of([small(i & (size - 1)) for i in ids])
        self.bf = rows_of([small(h) for h in high])
        self.full = rows_of([h.astype(F32) for h in high])

    def hot(self):
        return onehot(self.low_rows, self.size)


def copies(refs, held, sems):
    return [pltpu.make_async_copy(ref, to, sems.at[i]) for i, (ref, to) in enumerate(zip(refs, held))]


def pack_kernel(block_ref, slot_in, expo_in, pix_in, mag_in, w_in, out_ref, slot, expo, pix, mag, w, sems):
    moves = copies((slot_in, expo_in, pix_in, mag_in, w_in), (slot, expo, pix, mag, w), sems)
    for move in moves:
        move.start()
    for move in moves:
        move.wait()
    rows = row_iota((8, LO))
    for kk in range(2):
        at = pl.ds(8 * kk, 8)
        base = jnp.zeros((8, LO), I32)
        for i in range(8):
            base = jnp.where(rows == i, block_ref[0, 8 * kk + i] * 256 + (i // 2) * 512, base)
        p = pix[at, :]
        out_ref[kk, 0] = (slot[at, :] + base).astype(F32)
        out_ref[kk, 1] = ((((p >> 7) & 1) * 8 + (p >> 8)) * LO + (p & 127)).astype(F32)
        out_ref[kk, 2] = expo[at, :].astype(F32)
        out_ref[kk, 3] = w[at, :]
        out_ref[kk, 4] = w[at, :] * mag[at, :]


def expo_kernel(obs_ref, out_ref):
    ids = Ids([obs_ref[kk, E] for kk in range(2)], HALF, (0, 0))
    weighted, count = scatter(
        [split_rows([obs_ref[kk, f] for kk in range(2)]) for f in (WM, W)], ids.bf, ids.hot()
    )
    both = joined([weighted[:8], count[:8]])
    for peer in range(NZ * NH):
        out_ref[peer] = both


def field(obs_ref, y, rel, kk, f):
    return obs_ref[y, pl.ds(pl.multiple_of(rel * 80 + kk * 40 + f * 8, 8), 8), :]


def chunk(obs_ref, step, f):
    kk, half = step // 2, step % 2
    return [field(obs_ref, 2 * half + yy, rel, kk, f) for yy in range(2) for rel in range(2)]


def own(obs_ref, y, kk, f):
    return [field(obs_ref, y, rel, kk, f) for rel in range(2)]


def sums_kernel(obs_ref, g0s_ref, ds_ref, g0f_ref, df_ref, hop_ref, chip_ref):
    for ref in (g0s_ref, ds_ref, g0f_ref, df_ref):
        ref[...] = jnp.zeros(ref.shape, F32)

    def sums(step, carry):
        values = [split_rows(chunk(obs_ref, step, f)) for f in (WM, W)]
        ids = Ids(chunk(obs_ref, step, S), LO)
        weighted, count = scatter(values, ids.bf, ids.hot())
        g0s_ref[step // 2] += weighted
        ds_ref[step // 2] += count
        ids = Ids(chunk(obs_ref, step, PX), LO)
        weighted, count = scatter(values, ids.bf, ids.hot())
        g0f_ref[...] += weighted
        df_ref[...] += count
        return carry

    lax.fori_loop(0, 4, sums, 0)
    diag = df_ref[...] + (4.0 * SMOOTH + RIDGE)
    g0f = g0f_ref[...] / diag
    df_ref[...] = diag
    g0f_ref[...] = g0f
    diag = ds_ref[...] + RIDGE
    g0s_ref[...] = g0s_ref[...] / diag
    ds_ref[...] = diag
    odd = lax.axis_index("c") == 1
    top = jnp.concatenate([g0f[0:1], g0f[8:9]], axis=0)
    bot = jnp.concatenate([g0f[7:8], g0f[15:16]], axis=0)
    hop_ref[...] = jnp.where(odd, bot, top)
    chip_ref[...] = jnp.where(odd, top, bot)


def couple_kernel(obs_ref, g0s_ref, g0f_ref, cs_ref, cf_ref, ru_ref, fit_ref):
    cs_ref[...] = jnp.zeros(cs_ref.shape, F32)
    cf_ref[...] = jnp.zeros((HI, LO), F32)

    def couple(step, carry):
        star, flat = Ids(chunk(obs_ref, step, S), LO), Ids(chunk(obs_ref, step, PX), LO)
        hs, hp = star.hot(), flat.hot()
        fit = joined(rows_of(chunk(obs_ref, step, W))) * gather_both(
            (g0s_ref[step // 2], star.full, hs), (g0f_ref[...], flat.full, hp)
        )
        parts = split3(fit)
        (added,) = scatter([[across(part, FLAT) for part in parts]], star.bf, hs)
        cs_ref[step // 2] += added
        (added,) = scatter([[across(part, STAR) for part in parts]], flat.bf, hp)
        cf_ref[...] += added
        fit_ref[step] = fit
        return carry

    lax.fori_loop(0, 4, couple, 0)
    y = lax.axis_index("y")
    total = jnp.zeros((HI, HALF), F32)
    for kk in range(2):
        ids = Ids(own(obs_ref, y, kk, E), HALF, (0, 8))
        at = pl.ds(pl.multiple_of((y % 2) * 2048, 2048), 2048)
        fit = fit_ref[2 * kk + y // 2, :, at]
        parts = split3(row(fit, STAR) + row(fit, FLAT))
        (added,) = scatter([[across(part, 0) for part in parts]], ids.bf, ids.hot())
        total += added
    ru_ref[...] = total


def beside(flat, above, below):
    left, right = flat[:8], flat[8:]
    rows = row_iota((8, LO))
    lanes = lax.broadcasted_iota(I32, (8, LO), 1)
    out = []
    left_up, right_up = pltpu.roll(left, 1, 1), pltpu.roll(right, 1, 1)
    left_down, right_down = pltpu.roll(left, 127, 1), pltpu.roll(right, 127, 1)
    sides = (
        jnp.where(lanes == 0, 0.0, left_up) + jnp.where(lanes == 127, right_down, left_down),
        jnp.where(lanes == 0, left_up, right_up) + jnp.where(lanes == 127, 0.0, right_down),
    )
    for i, half in enumerate((left, right)):
        upper = jnp.where(rows == 0, above[i : i + 1], pltpu.roll(half, 1, 0))
        lower = jnp.where(rows == 7, below[i : i + 1], pltpu.roll(half, 7, 0))
        out.append(sides[i] + upper + lower)
    return jnp.concatenate(out, axis=0)


def expo_apply_kernel(
    obs_ref, expo_ref, g0f_ref, cf_ref, df_ref, hop_ref, chip_ref,
    fit_ref, cf_out, yf_out, g0z_out, dz_out, top_out,
):
    part = expo_ref[0]
    for xc in range(1, 8):
        part = part + expo_ref[xc]
    for y in range(4):
        diag = part[16 * y : 16 * y + 16, HALF:] + RIDGE
        g0z_out[y] = part[16 * y : 16 * y + 16, :HALF] / diag
        dz_out[y] = diag
    cf_out[...] = cf_ref[...]

    def apply(step, carry):
        expo = Ids(chunk(obs_ref, step, E), HALF, (0, 8, 0, 8))
        hot = expo.hot()
        found = [
            gather(
                g0z_out[2 * (step % 2) + yy],
                expo.full[16 * yy : 16 * yy + 16],
                hot[:, 2048 * yy : 2048 * (yy + 1)],
            )
            for yy in range(2)
        ]
        fit = joined(rows_of(chunk(obs_ref, step, W))) * joined(found)
        fit_ref[step] = fit
        flat = Ids(chunk(obs_ref, step, PX), LO)
        (added,) = scatter([[across(part, 0) for part in split3(fit)]], flat.bf, flat.hot())
        cf_out[...] += added
        return carry

    lax.fori_loop(0, 4, apply, 0)
    odd = lax.axis_index("c") == 1
    above = jnp.where(odd, chip_ref[...], hop_ref[...])
    below = jnp.where(odd, hop_ref[...], chip_ref[...])
    cf = cf_out[...] - SMOOTH * beside(g0f_ref[...], above, below)
    cf_out[...] = cf
    yf = cf / df_ref[...]
    yf_out[...] = yf
    top_out[...] = jnp.concatenate([yf[0:1], yf[8:9]], axis=0)


def fold8(a):
    total = a[0:8]
    for i in range(8, a.shape[0], 8):
        total = total + a[i : i + 8]
    return jnp.sum(total, axis=0, keepdims=True)


def fold_lanes(a):
    total = a[:, 0:LO]
    for i in range(LO, a.shape[1], LO):
        total = total + a[:, i : i + LO]
    return total


def last_kernel(
    obs_ref, fit_ref, g0s_ref, ds_ref, cs_in, g0f_ref, df_ref, cf_ref, yf_ref, ru_ref, ys_ref, out_ref, cs_ref
):
    cs_ref[...] = cs_in[...]

    def finish_star(step, carry):
        star = Ids(chunk(obs_ref, step, S), LO)
        parts = split3(fit_ref[step])
        (added,) = scatter([[across(part, 0) for part in parts]], star.bf, star.hot())
        cs_ref[step // 2] += added
        return carry

    lax.fori_loop(0, 4, finish_star, 0)
    rho = jnp.zeros((1, LO), F32)
    beta, eta = rho, rho
    for kk in range(2):
        g0s, ds, cs = g0s_ref[kk], ds_ref[kk], cs_ref[kk]
        ys = cs / ds
        ys_ref[kk] = ys
        rho += fold8(g0s * g0s * ds)
        beta += fold8(g0s * cs)
        eta += fold8(cs * ys)
    y = lax.axis_index("y")
    total = jnp.zeros((HI, HALF), F32)
    cross = jnp.zeros((1, LO), F32)
    yf = yf_ref[...]
    for kk in range(2):
        star, flat = Ids(own(obs_ref, y, kk, S), LO), Ids(own(obs_ref, y, kk, PX), LO)
        expo = Ids(own(obs_ref, y, kk, E), HALF, (0, 8))
        w = joined(rows_of(own(obs_ref, y, kk, W)))
        both = gather_both((ys_ref[kk], star.full, star.hot()), (yf, flat.full, flat.hot()))
        from_star, from_flat = row(both, STAR), row(both, FLAT)
        parts = split3(w * (from_star + from_flat))
        (added,) = scatter([[across(part, 0) for part in parts]], expo.bf, expo.hot())
        total += added
        cross += fold_lanes(w * from_star * from_flat)
    ru = ru_ref[...]
    out_ref[0:16] = jnp.concatenate([ru, total], axis=1)
    g0f, df, cf = g0f_ref[...], df_ref[...], cf_ref[...]
    none = jnp.zeros((2, LO), F32)
    rho = 0.25 * (rho + fold8(g0f * g0f * df))
    beta = 0.25 * (beta + fold8(g0f * cf))
    eta = 0.25 * (eta + fold8(cf * yf))
    delta = 2.0 * cross - (0.25 * SMOOTH) * fold8(yf * beside(yf, none, none))
    out_ref[16:24] = jnp.concatenate([rho, beta, eta, delta, jnp.zeros((4, LO), F32)], axis=0)


def edge_kernel(payload_ref, yf_ref, next_ref, out_ref):
    edge = yf_ref[7:8] * next_ref[0:1] + yf_ref[15:16] * next_ref[1:2]
    edge = jnp.where(row_iota((8, LO)) == 3, -(0.5 * SMOOTH) * edge, 0.0)
    scal = payload_ref[16:24] + edge
    for peer in range(NZ):
        out_ref[peer, 0:16] = payload_ref[0:16]
        out_ref[peer, 16:24] = scal


def whole(a):
    return jnp.sum(jnp.sum(a, axis=0, keepdims=True), axis=1, keepdims=True)


def finish_kernel(
    sums_ref, g0z_ref, dz_ref, g0s_ref, ys_ref, g0f_ref, yf_ref, star_out, zero_out, flat_out
):
    y, zh = lax.axis_index("y"), lax.axis_index("zh")
    scal = sums_ref[0, 16:24]
    for peer in range(1, 32):
        scal = scal + sums_ref[peer, 16:24]
    z_rho = jnp.zeros((HI, HALF), F32)
    z_beta, z_eta, z_delta = z_rho, z_rho, z_rho
    z_own = z_rho
    for i in range(4):
        part = sums_ref[i, 0:16]
        for xc in range(1, 8):
            part = part + sums_ref[xc * 4 + i, 0:16]
        cz, qz = part[:, :HALF], part[:, HALF:]
        g0z, dz = g0z_ref[i], dz_ref[i]
        yz = cz / dz
        z_rho += g0z * g0z * dz
        z_beta += g0z * cz
        z_eta += cz * yz
        z_delta += qz * yz
        z_own = jnp.where(i == y, yz, z_own)
    rho0 = whole(z_rho) + whole(scal[0:1])
    beta = whole(z_beta) + whole(scal[1:2])
    eta = whole(z_eta) + whole(scal[2:3])
    delta = 2.0 * whole(z_delta) + whole(scal[3:4])
    curv0 = rho0 + beta
    step0 = rho0 / curv0
    left = beta / curv0
    rho1 = left * left * rho0 - 2.0 * step0 * left * beta + step0 * step0 * eta
    curv_g = (
        left * left * curv0
        - 2.0 * step0 * left * (beta + eta)
        + step0 * step0 * (eta + delta)
    )
    ratio = rho1 / rho0
    mixed = left * curv0 - step0 * (beta + eta)
    curv1 = curv_g + 2.0 * ratio * mixed + ratio * ratio * curv0
    step1 = rho1 / curv1
    along_g = step0 + step1 * (left + ratio)
    along_y = -step1 * step0
    star = along_g * g0s_ref[y // 2] + along_y * ys_ref[y // 2]
    shard = (y % 2) * 2 + zh
    mine = jnp.zeros((4, LO), F32)
    for i in range(4):
        mine = jnp.where(shard == i, star[4 * i : 4 * i + 4], mine)
    star_out[...] = mine
    zero = along_g * g0z_ref[y] + along_y * z_own
    zero_out[...] = jnp.concatenate([zero[0:4], pltpu.roll(zero[0:8], 4, 0)[0:4]], axis=1)
    flat = along_g * g0f_ref[...] + along_y * yf_ref[...]
    flat_out[...] = joined([flat[:8], flat[8:]])


VMEM = pl.BlockSpec(memory_space=pltpu.VMEM)
SMEM = pl.BlockSpec(memory_space=pltpu.SMEM)


HBM = pl.BlockSpec(memory_space=pltpu.HBM)


def call(kernel, shapes, args, specs=None, scratch=(), mib=8, work=20):
    out = [jax.ShapeDtypeStruct(shape, F32) for shape in shapes]
    many = len(out) > 1
    return pl.pallas_call(
        kernel,
        name=kernel.__name__,
        out_shape=tuple(out) if many else out[0],
        in_specs=specs or [VMEM] * len(args),
        out_specs=tuple([VMEM] * len(out)) if many else VMEM,
        scratch_shapes=list(scratch),
        compiler_params=pltpu.CompilerParams(vmem_limit_bytes=mib << 20),
        cost_estimate=pl.CostEstimate(flops=1 << work, bytes_accessed=1 << 20, transcendentals=0),
    )(*args)


def exchange(blocks, axes):
    return lax.all_to_all(blocks, axes, 0, 0, tiled=True)


def to_all(block, peers, axes):
    return exchange(jnp.broadcast_to(block[None], (peers, *block.shape)), axes)


def flat_pairs():
    def place(tile, y, zh):
        x, rest = divmod(tile, NZ * NC)
        zl, c = divmod(rest, NC)
        return (((x * NZ + zl) * NC + c) * NY + y) * NH + zh

    chip, hop, down = [], [], []
    for tile in range(NX * NZ * NC - 1):
        far = (tile + 1) % (NZ * NC) == 0
        for y in range(NY):
            for zh in range(NH):
                here, there = place(tile, y, zh), place(tile + 1, y, 1 - zh if far else zh)
                (hop if tile % 2 else chip).extend([(here, there), (there, here)])
                down.append((there, here))
    return chip, hop, down


def on_device(star_slot, star_block, exposure, superpixel, magnitude, weight):
    zh = lax.axis_index("zh")
    chip, hop, down = flat_pairs()
    stars, flats, expos = (2, HI, LO), (HI, LO), (4, HI, HALF)
    obs = call(
        pack_kernel, [(2, 5, 8, LO)],
        (star_block, star_slot[0], exposure[0], superpixel[0], magnitude[0], weight[0]),
        specs=[SMEM] + [HBM] * 5,
        scratch=[pltpu.VMEM((16, LO), t) for t in (I32, I32, I32, F32, F32)]
        + [pltpu.SemaphoreType.DMA((5,))],
    )
    obs = obs.reshape(80, LO)
    partner = lax.ppermute(obs, "zh", [(0, 1), (1, 0)])
    expo = exchange(call(expo_kernel, [(16, 8, LO)], (obs.reshape(2, 5, 8, LO),)), ("zl", "zh"))
    expo = expo.reshape(NZ, NH, 8, LO).sum(axis=0)
    expo = jnp.where(zh == 0, expo, expo[::-1]).reshape(HI, LO)
    tile_obs = jnp.concatenate([obs, partner, expo], axis=0)
    tile_obs = to_all(lax.optimization_barrier(tile_obs), NY, "y")
    tile_obs = lax.optimization_barrier(tile_obs)
    expo = to_all(tile_obs[:, 160:].reshape(64, LO), 8, COLS)
    g0s, ds, g0f, df, hop_row, chip_row = call(
        sums_kernel, [stars] * 2 + [flats] * 2 + [(2, LO)] * 2, (tile_obs,), mib=16, work=29
    )
    by_hop = lax.ppermute(hop_row, ALL, hop)
    by_chip = lax.ppermute(chip_row, ALL, chip)
    cs, cf, ru = call(
        couple_kernel, [stars, flats, (HI, HALF)], (tile_obs, g0s, g0f),
        scratch=[pltpu.VMEM((4, 8, 4096), F32)], mib=16, work=30,
    )
    fit, cf, yf, g0z, dz, first = call(
        expo_apply_kernel, [(4, 8, 4096)] + [flats] * 2 + [expos] * 2 + [(2, LO)],
        (tile_obs, expo, g0f, cf, df, by_hop, by_chip), mib=16, work=30,
    )
    next_first = lax.ppermute(first, ALL, down)
    ys, payload = call(
        last_kernel, [stars, (24, LO)],
        (tile_obs, fit, g0s, ds, cs, g0f, df, cf, yf, ru),
        scratch=[pltpu.VMEM(stars, F32)], mib=16, work=30,
    )
    payload = call(edge_kernel, [(NZ, 24, LO)], (payload, yf, next_first))
    sums = exchange(payload, "zl").sum(axis=0)
    sums = to_all(sums, 32, PLANE)
    star, zero, flat = call(
        finish_kernel, [(4, LO), (4, LO), (8, 2 * LO)], (sums, g0z, dz, g0s, ys, g0f, yf)
    )
    return star.reshape(-1), zero.reshape(-1), flat


def solution(mesh):
    split = Mesh(mesh.devices.reshape(NX, NZ, NC, NY, NH), ALL)
    tile, loop = ("x", "zl", "c"), ("y", "zh")
    placed = (
        P(tile, loop, None),
        P(tile, loop),
        P(tile, loop, None),
        P(tile, loop, None),
        P(tile, loop, None),
        P(tile, loop, None),
    )
    return jax.shard_map(
        on_device,
        mesh=split,
        in_specs=placed,
        out_specs=(P(ALL), P(loop), P(tile, None)),
        check_vma=False,
    )
```

time: 121 us -> 117 us (0.967)
  blocking collectives: 53.9 us -> 49.7 us
  Pallas kernels: 14.5 us -> 16.5 us
  waiting for transfers between devices: 4.8 us -> 2.89 us
    all_to_all x3, blocking collectives: 53.9 us -> 49.7 us  [exchange(): return lax.all_to_all(blocks, axes, 0, 0, tiled=True)]
    pallas_call x8, Pallas kernels: 14.5 us -> 16.5 us  [call(): pl.pallas_call(kernel, name=kernel.__name__, out_shape=tuple(out) if many...]
    ppermute x1, waiting for transfers between devices: 1.38 us -> 0.01 us  [on_device(): next_first = lax.ppermute(first, ALL, down)]
  transfers between devices with their start and end apart: 6 -> 6, of which waited for: 2 -> 2; matrix products, arithmetic and copies ran while one was open for 0% -> 0% of each run, Pallas kernels for 8% -> 10%
where the time goes in v4:
time: 117 us; the launch traced here: 116 us
  blocking collectives  49.7 us (42%)
  starting transfers between devices  42.3 us (36%)
  Pallas kernels  16.5 us (14%)
  local copies, waits for them, and re-layouts  4.24 us (4%)
  waiting for transfers between devices  2.89 us (2%)
    all_to_all x3, blocking collectives, exchange(): return lax.all_to_all(blocks, axes, 0, 0, tiled=True)  49.7 us
    all_to_all x2, starting transfers between devices, exchange(): return lax.all_to_all(blocks, axes, 0, 0, tiled=True)  23.4 us
    pallas_call x8, Pallas kernels, call(): pl.pallas_call(kernel, name=kernel.__name__, out_shape=tuple(out) if many...  16.5 us
    ppermute x1, starting transfers between devices, on_device(): partner = lax.ppermute(obs, 'zh', [(0, 1), (1, 0)])  12 us
    unnamed x12, local copies, waits for them, and re-layouts  3.47 us
    ppermute x1, waiting for transfers between devices, on_device(): partner = lax.ppermute(obs, 'zh', [(0, 1), (1, 0)])  2.74 us
    ppermute x1, starting transfers between devices, on_device(): by_hop = lax.ppermute(hop_row, ALL, hop)  2.6 us
    ppermute x1, starting transfers between devices, on_device(): next_first = lax.ppermute(first, ALL, down)  2.41 us
  transfers between devices with their start and end apart: 6, of which 2 were waited for; matrix products, arithmetic and copies ran while one was open for 0% of the time, Pallas kernels for 10%

profile of v4, /device:TPU:1, one launch (start us, length us, event | category | flops | bytes accessed | tf_op | source)
XLA Modules:
  0.0 116.5 jit_solution(7664309253158923816)
XLA Ops:
  0.7 0.7 copy-done
  1.3 0.7 copy-done.1
  2.0 0.7 copy-done.2
  2.7 0.7 copy-done.3
  3.4 0.7 copy-done.4
  4.1 0.7 pack_kernel.1.obs_ref
  4.8 1.0 expo_kernel.1
  5.8 15.7 %all-to-all-start = ((f32[16,8,128]{2,1,0:T(8,128)}), f32[16,8,128]{2,1,0:T(8,128)S(1)}, u32[]{:S(2)}, u32[]{:S(2)}) async-start(f32[16,8,128]{2,1,0:T(8,128)} %expo_kernel.1), calls=%async_computation | async-start | bytes 131072 | tf_op jit(solution)/shard_map/all_to_all | solution.py:441
  21.5 12.0 %collective-permute-start = (f32[80,128]{1,0:T(8,128)S(1)}, f32[80,128]{1,0:T(8,128)S(1)}, u32[]{:S(2)}, u32[]{:S(2)}) collective-permute-start(f32[80,128]{1,0:T(8,128)S(1)} %bitcast.12), channel_id=1, source_target_pairs={{0,1},{1,0},{2,3},{3,2},{4,5},{5,4},{6,7},{7,6},{8,9},{9,8},{10,11... | collective-permute-start | bytes 122888 | tf_op jit(solution)/shard_map/ppermute | solution.py:477
  33.5 0.1 all-to-all-done
  33.7 2.7 %collective-permute-done = f32[80,128]{1,0:T(8,128)S(1)} collective-permute-done((f32[80,128]{1,0:T(8,128)S(1)}, f32[80,128]{1,0:T(8,128)S(1)}, u32[]{:S(2)}, u32[]{:S(2)}) %collective-permute-start) | collective-permute-done | bytes 40992 | tf_op jit(solution)/shard_map/ppermute | solution.py:477
  36.4 10.0 %all_to_all.25.obs_ref = f32[4,176,128]{2,1,0:T(8,128)S(1)} all-to-all(f32[4,176,128]{2,1,0:T(8,128)S(1)} %broadcast_in_dim.8), channel_id=1, replica_groups=mesh['x'=4,'zl'=8,'c'=2,'y'=4,'zh'=2] {'y'}, dimensions={0} | all-to-all | bytes 720896 | tf_op jit(solution)/shard_map/all_to_all | solution.py:441
  46.5 0.7 broadcast_in_dim.10
  47.2 7.7 %all-to-all-start.2 = ((f32[8,64,128]{2,1,0:T(8,128)}), f32[8,64,128]{2,1,0:T(8,128)S(1)}, u32[]{:S(2)}, u32[]{:S(2)}) async-start(f32[8,64,128]{2,1,0:T(8,128)} %broadcast_in_dim.10), calls=%async_computation.2 | async-start | bytes 524288 | tf_op jit(solution)/shard_map/all_to_all | solution.py:441
  54.9 3.3 %sums_kernel.1 = (f32[2,16,128]{2,1,0:T(8,128)S(1)}, f32[2,16,128]{2,1,0:T(8,128)S(1)}, f32[16,128]{1,0:T(8,128)S(1)}, f32[16,128]{1,0:T(8,128)S(1)}, f32[2,128]{1,0:T(2,128)S(1)}, /*index=5*/f32[2,128]{1,0:T(2,128)S(1)}) custom-call(f32[4,176,128]{2,1,0:T(8,128)S(1)} %all_to_all.25.obs_ref), custom_call_target="tpu_custom_call" | custom-call | flops 536870912 | bytes 1048576 | tf_op jit(solution)/shard_map/sums_kernel/pallas_call | solution.py:428
  58.2 2.6 %collective-permute-start.1 = (f32[2,128]{1,0:T(2,128)S(1)}, f32[2,128]{1,0:T(2,128)S(1)}, u32[]{:S(2)}, u32[]{:S(2)}) collective-permute-start(f32[2,128]{1,0:T(2,128)S(1)} %get-tuple-element.27), channel_id=1, source_target_pairs={{8,16},{16,8},{9,17},{17,9},{10,18},{18,10},{11,19},{19,11},{12,20... | collective-permute-start | bytes 3080 | tf_op jit(solution)/shard_map/ppermute | solution.py:488
  60.8 1.9 %collective-permute-start.2 = (f32[2,128]{1,0:T(2,128)S(1)}, f32[2,128]{1,0:T(2,128)S(1)}, u32[]{:S(2)}, u32[]{:S(2)}) collective-permute-start(f32[2,128]{1,0:T(2,128)S(1)} %get-tuple-element.28), channel_id=1, source_target_pairs={{0,8},{8,0},{1,9},{9,1},{2,10},{10,2},{3,11},{11,3},{4,12},{12,4},... | collective-permute-start | bytes 3080 | tf_op jit(solution)/shard_map/ppermute | solution.py:489
  62.7 5.0 %couple_kernel.1 = (f32[2,16,128]{2,1,0:T(8,128)S(1)}, f32[16,128]{1,0:T(8,128)S(1)}, f32[16,64]{1,0:T(8,128)S(1)}) custom-call(f32[4,176,128]{2,1,0:T(8,128)S(1)} %all_to_all.25.obs_ref, f32[2,16,128]{2,1,0:T(8,128)S(1)} %get-tuple-element.24.g0s_ref, f32[16,128]{1,0:T(8,128)S(1)} %get-tuple-element.23.g0f_ref), custom_call_target="tpu_custom_call" | custom-call | flops 1073741824 | bytes 1048576 | tf_op jit(solution)/shard_map/couple_kernel/pallas_call | solution.py:428
  67.7 2.7 %expo_apply_kernel.1 = (f32[4,8,4096]{2,1,0:T(8,128)S(1)}, f32[16,128]{1,0:T(8,128)S(1)}, f32[16,128]{1,0:T(8,128)S(1)}, f32[4,16,64]{2,1,0:T(8,128)S(1)}, f32[4...) custom-call(f32[4,176,128]{2,1,0:T(8,128)S(1)} %all_to_all.25.obs_ref, f32[8,64,128]{2,1,0:T(8,128)S(1)} %all-to-all-done.2.expo_ref, ...), custom_call_target="tpu_custom_call" | custom-call | flops 1073741824 | bytes 1048576 | tf_op jit(solution)/shard_map/expo_apply_kernel/pallas_call | solution.py:428
  70.4 2.4 %collective-permute-start.3 = (f32[2,128]{1,0:T(2,128)S(1)}, f32[2,128]{1,0:T(2,128)S(1)}, u32[]{:S(2)}, u32[]{:S(2)}) collective-permute-start(f32[2,128]{1,0:T(2,128)S(1)} %get-tuple-element.36), channel_id=1, source_target_pairs={{8,0},{9,1},{10,2},{11,3},{12,4},{13,5},{14,6},{15,7},{16,8},{17,9... | collective-permute-start | bytes 3080 | tf_op jit(solution)/shard_map/ppermute | solution.py:498
  72.8 2.9 %last_kernel.1 = (f32[2,16,128]{2,1,0:T(8,128)S(1)}, f32[24,128]{1,0:T(8,128)S(1)}) custom-call(f32[4,176,128]{2,1,0:T(8,128)S(1)} %all_to_all.25.obs_ref, f32[4,8,4096]{2,1,0:T(8,128)S(1)} %get-tuple-element.29.fit_ref, f32[2,16,128]{2,1,0:T(8,128)S(1)} %get-tuple-element.24.g0s_ref, f32[2,16,128]{2,1,0:T(8,128)S(1)} %get-tuple-element.30.ds_ref, ...), custom_call_target="tpu_custom_call" | custom-call | flops 1073741824 | bytes 1048576 | tf_op jit(solution)/shard_map/last_kernel/pallas_call | solution.py:428
  75.8 24.9 %all_to_all.26 = f32[8,24,128]{2,1,0:T(8,128)S(1)} all-to-all(f32[8,24,128]{2,1,0:T(8,128)S(1)} %edge_kernel.1), channel_id=1, replica_groups=mesh['x'=4,'zl'=8,'c'=2,'y'=4,'zh'=2] {'zl'}, dimensions={0} | all-to-all | bytes 196608 | tf_op jit(solution)/shard_map/all_to_all | solution.py:441
  100.8 14.7 %all_to_all.27.sums_ref = f32[32,24,128]{2,1,0:T(8,128)S(1)} all-to-all(f32[32,24,128]{2,1,0:T(8,128)S(1)} %broadcast_in_dim.22), channel_id=1, replica_groups=mesh['x'=4,'zl'=8,'c'=2,'y'=4,'zh'=2] {'x','c','y'}, dimensions={0} | all-to-all | bytes 786432 | tf_op jit(solution)/shard_map/all_to_all | solution.py:441
  115.5 1.0 finish_kernel.1
  (19 shorter events, 0.2 us)
Async XLA Ops:
  0.6 0.7 copy-start
  0.6 0.7 copy-start.5
  1.3 0.7 copy-start.1
  2.0 0.7 copy-start.2
  2.7 0.7 copy-start.3
  3.4 0.7 copy-start.4
  5.8 27.9 %all-to-all-start = ((f32[16,8,128]{2,1,0:T(8,128)}), f32[16,8,128]{2,1,0:T(8,128)S(1)}, u32[]{:S(2)}, u32[]{:S(2)}) async-start(f32[16,8,128]{2,1,0:T(8,128)} %expo_kernel.1), calls=%async_computation | async-start | bytes 131072 | tf_op jit(solution)/shard_map/all_to_all | solution.py:441
  21.5 14.9 %collective-permute-start = (f32[80,128]{1,0:T(8,128)S(1)}, f32[80,128]{1,0:T(8,128)S(1)}, u32[]{:S(2)}, u32[]{:S(2)}) collective-permute-start(f32[80,128]{1,0:T(8,128)S(1)} %bitcast.12), channel_id=1, source_target_pairs={{0,1},{1,0},{2,3},{3,2},{4,5},{5,4},{6,7},{7,6},{8,9},{9,8},{10,11... | collective-permute-start | bytes 122888 | tf_op jit(solution)/shard_map/ppermute | solution.py:477
  47.2 20.5 %all-to-all-start.2 = ((f32[8,64,128]{2,1,0:T(8,128)}), f32[8,64,128]{2,1,0:T(8,128)S(1)}, u32[]{:S(2)}, u32[]{:S(2)}) async-start(f32[8,64,128]{2,1,0:T(8,128)} %broadcast_in_dim.10), calls=%async_computation.2 | async-start | bytes 524288 | tf_op jit(solution)/shard_map/all_to_all | solution.py:441
  58.2 9.5 %collective-permute-start.1 = (f32[2,128]{1,0:T(2,128)S(1)}, f32[2,128]{1,0:T(2,128)S(1)}, u32[]{:S(2)}, u32[]{:S(2)}) collective-permute-start(f32[2,128]{1,0:T(2,128)S(1)} %get-tuple-element.27), channel_id=1, source_target_pairs={{8,16},{16,8},{9,17},{17,9},{10,18},{18,10},{11,19},{19,11},{12,20... | collective-permute-start | bytes 3080 | tf_op jit(solution)/shard_map/ppermute | solution.py:488
  60.8 6.9 %collective-permute-start.2 = (f32[2,128]{1,0:T(2,128)S(1)}, f32[2,128]{1,0:T(2,128)S(1)}, u32[]{:S(2)}, u32[]{:S(2)}) collective-permute-start(f32[2,128]{1,0:T(2,128)S(1)} %get-tuple-element.28), channel_id=1, source_target_pairs={{0,8},{8,0},{1,9},{9,1},{2,10},{10,2},{3,11},{11,3},{4,12},{12,4},... | collective-permute-start | bytes 3080 | tf_op jit(solution)/shard_map/ppermute | solution.py:489
  70.4 5.4 %collective-permute-start.3 = (f32[2,128]{1,0:T(2,128)S(1)}, f32[2,128]{1,0:T(2,128)S(1)}, u32[]{:S(2)}, u32[]{:S(2)}) collective-permute-start(f32[2,128]{1,0:T(2,128)S(1)} %get-tuple-element.36), channel_id=1, source_target_pairs={{8,0},{9,1},{10,2},{11,3},{12,4},{13,5},{14,6},{15,7},{16,8},{17,9... | collective-permute-start | bytes 3080 | tf_op jit(solution)/shard_map/ppermute | solution.py:498

commit v5 on v4

--- a/solution.py
+++ b/solution.py
@@ -123,34 +123,38 @@
     return [pltpu.make_async_copy(ref, to, sems.at[i]) for i, (ref, to) in enumerate(zip(refs, held))]
 
 
-def pack_kernel(block_ref, slot_in, expo_in, pix_in, mag_in, w_in, out_ref, slot, expo, pix, mag, w, sems):
+def pack_kernel(
+    block_ref, slot_in, expo_in, pix_in, mag_in, w_in, out_ref, expo_ref, slot, expo, pix, mag, w, sems
+):
     moves = copies((slot_in, expo_in, pix_in, mag_in, w_in), (slot, expo, pix, mag, w), sems)
     for move in moves:
         move.start()
     for move in moves:
         move.wait()
     rows = row_iota((8, LO))
+    weights, weighted = [], []
     for kk in range(2):
         at = pl.ds(8 * kk, 8)
         base = jnp.zeros((8, LO), I32)
         for i in range(8):
             base = jnp.where(rows == i, block_ref[0, 8 * kk + i] * 256 + (i // 2) * 512, base)
         p = pix[at, :]
-        out_ref[kk, 0] = (slot[at, :] + base).astype(F32)
-        out_ref[kk, 1] = ((((p >> 7) & 1) * 8 + (p >> 8)) * LO + (p & 127)).astype(F32)
-        out_ref[kk, 2] = expo[at, :].astype(F32)
-        out_ref[kk, 3] = w[at, :]
-        out_ref[kk, 4] = w[at, :] * mag[at, :]
-
-
-def expo_kernel(obs_ref, out_ref):
-    ids = Ids([obs_ref[kk, E] for kk in range(2)], HALF, (0, 0))
-    weighted, count = scatter(
-        [split_rows([obs_ref[kk, f] for kk in range(2)]) for f in (WM, W)], ids.bf, ids.hot()
-    )
-    both = joined([weighted[:8], count[:8]])
+        weights.append(w[at, :])
+        weighted.append(w[at, :] * mag[at, :])
+        fields = (
+            (slot[at, :] + base).astype(F32),
+            ((((p >> 7) & 1) * 8 + (p >> 8)) * LO + (p & 127)).astype(F32),
+            expo[at, :].astype(F32),
+            weights[kk],
+            weighted[kk],
+        )
+        for f, tile in enumerate(fields):
+            out_ref[40 * kk + 8 * f : 40 * kk + 8 * f + 8] = tile
+    ids = Ids([expo[0:8], expo[8:16]], HALF, (0, 0))
+    total, count = scatter([split_rows(weighted), split_rows(weights)], ids.bf, ids.hot())
+    both = joined([total[:8], count[:8]])
     for peer in range(NZ * NH):
-        out_ref[peer] = both
+        expo_ref[peer] = both
 
 
 def field(obs_ref, y, rel, kk, f):
@@ -248,7 +252,7 @@
 
 def expo_apply_kernel(
     obs_ref, expo_ref, g0f_ref, cf_ref, df_ref, hop_ref, chip_ref,
-    fit_ref, cf_out, yf_out, g0z_out, dz_out, top_out,
+    fit_ref, cf_out, yf_out, g0z_out, dz_out, edge_out,
 ):
     part = expo_ref[0]
     for xc in range(1, 8):
@@ -285,7 +289,7 @@
     cf_out[...] = cf
     yf = cf / df_ref[...]
     yf_out[...] = yf
-    top_out[...] = jnp.concatenate([yf[0:1], yf[8:9]], axis=0)
+    edge_out[...] = jnp.concatenate([yf[0:1], yf[8:9], yf[7:8], yf[15:16]], axis=0)
 
 
 def fold8(a):
@@ -349,13 +353,36 @@
     out_ref[16:24] = jnp.concatenate([rho, beta, eta, delta, jnp.zeros((4, LO), F32)], axis=0)
 
 
-def edge_kernel(payload_ref, yf_ref, next_ref, out_ref):
-    edge = yf_ref[7:8] * next_ref[0:1] + yf_ref[15:16] * next_ref[1:2]
-    edge = jnp.where(row_iota((8, LO)) == 3, -(0.5 * SMOOTH) * edge, 0.0)
-    scal = payload_ref[16:24] + edge
+def edge_dot(last, first):
+    both = last * first
+    return -(0.25 * SMOOTH) * (both[0:1] + both[1:2])
+
+
+def edge_kernel(payload_ref, mine_ref, other_ref, out_ref):
+    odd = lax.axis_index("c") == 1
+    mine, other = mine_ref[...], other_ref[...]
+    upper, lower = jnp.where(odd, other, mine), jnp.where(odd, mine, other)
+    chip = edge_dot(upper[2:4], lower[0:2])
+    scal = payload_ref[16:24]
+    scal = scal + jnp.where(row_iota((8, LO)) == 3, chip, 0.0)
+    scal = jnp.concatenate([scal[0:4], upper[0:2], lower[2:4]], axis=0)
     for peer in range(NZ):
         out_ref[peer, 0:16] = payload_ref[0:16]
         out_ref[peer, 16:24] = scal
+
+
+def column_kernel(parts_ref, out_ref):
+    total = parts_ref[0]
+    for peer in range(1, NZ):
+        total = total + parts_ref[peer]
+    between = edge_dot(parts_ref[0, 22:24], parts_ref[1, 20:22])
+    for peer in range(1, NZ - 1):
+        between += edge_dot(parts_ref[peer, 22:24], parts_ref[peer + 1, 20:22])
+    scal = total[16:20] + jnp.where(row_iota((4, LO)) == 3, between, 0.0)
+    ends = jnp.concatenate([scal, parts_ref[0, 20:22], parts_ref[NZ - 1, 22:24]], axis=0)
+    for peer in range(NX * NC * NY):
+        out_ref[peer, 0:16] = total[0:16]
+        out_ref[peer, 16:24] = ends
 
 
 def whole(a):
@@ -387,7 +414,10 @@
     rho0 = whole(z_rho) + whole(scal[0:1])
     beta = whole(z_beta) + whole(scal[1:2])
     eta = whole(z_eta) + whole(scal[2:3])
-    delta = 2.0 * whole(z_delta) + whole(scal[3:4])
+    between = jnp.zeros((1, LO), F32)
+    for x in range(NX - 1):
+        between += 8.0 * edge_dot(sums_ref[8 * x, 22:24], sums_ref[8 * x + 8, 20:22])
+    delta = 2.0 * whole(z_delta) + whole(scal[3:4] + between)
     curv0 = rho0 + beta
     step0 = rho0 / curv0
     left = beta / curv0
@@ -427,12 +457,11 @@
     many = len(out) > 1
     return pl.pallas_call(
         kernel,
-        name=kernel.__name__,
         out_shape=tuple(out) if many else out[0],
         in_specs=specs or [VMEM] * len(args),
         out_specs=tuple([VMEM] * len(out)) if many else VMEM,
         scratch_shapes=list(scratch),
-        compiler_params=pltpu.CompilerParams(vmem_limit_bytes=mib << 20),
+        compiler_params=pltpu.CompilerParams(vmem_limit_bytes=mib << 20 if mib else None),
         cost_estimate=pl.CostEstimate(flops=1 << work, bytes_accessed=1 << 20, transcendentals=0),
     )(*args)
 
@@ -451,31 +480,30 @@
         zl, c = divmod(rest, NC)
         return (((x * NZ + zl) * NC + c) * NY + y) * NH + zh
 
-    chip, hop, down = [], [], []
+    chip, hop = [], []
     for tile in range(NX * NZ * NC - 1):
         far = (tile + 1) % (NZ * NC) == 0
         for y in range(NY):
             for zh in range(NH):
                 here, there = place(tile, y, zh), place(tile + 1, y, 1 - zh if far else zh)
                 (hop if tile % 2 else chip).extend([(here, there), (there, here)])
-                down.append((there, here))
-    return chip, hop, down
+    return chip, hop
 
 
 def on_device(star_slot, star_block, exposure, superpixel, magnitude, weight):
     zh = lax.axis_index("zh")
-    chip, hop, down = flat_pairs()
+    chip, hop = flat_pairs()
     stars, flats, expos = (2, HI, LO), (HI, LO), (4, HI, HALF)
-    obs = call(
-        pack_kernel, [(2, 5, 8, LO)],
+    obs, expo = call(
+        pack_kernel, [(80, LO), (16, 8, LO)],
         (star_block, star_slot[0], exposure[0], superpixel[0], magnitude[0], weight[0]),
         specs=[SMEM] + [HBM] * 5,
         scratch=[pltpu.VMEM((16, LO), t) for t in (I32, I32, I32, F32, F32)]
         + [pltpu.SemaphoreType.DMA((5,))],
-    )
-    obs = obs.reshape(80, LO)
+        mib=None,
+    )
     partner = lax.ppermute(obs, "zh", [(0, 1), (1, 0)])
-    expo = exchange(call(expo_kernel, [(16, 8, LO)], (obs.reshape(2, 5, 8, LO),)), ("zl", "zh"))
+    expo = exchange(expo, ("zl", "zh"))
     expo = expo.reshape(NZ, NH, 8, LO).sum(axis=0)
     expo = jnp.where(zh == 0, expo, expo[::-1]).reshape(HI, LO)
     tile_obs = jnp.concatenate([obs, partner, expo], axis=0)
@@ -491,19 +519,18 @@
         couple_kernel, [stars, flats, (HI, HALF)], (tile_obs, g0s, g0f),
         scratch=[pltpu.VMEM((4, 8, 4096), F32)], mib=16, work=30,
     )
-    fit, cf, yf, g0z, dz, first = call(
-        expo_apply_kernel, [(4, 8, 4096)] + [flats] * 2 + [expos] * 2 + [(2, LO)],
+    fit, cf, yf, g0z, dz, edges = call(
+        expo_apply_kernel, [(4, 8, 4096)] + [flats] * 2 + [expos] * 2 + [(4, LO)],
         (tile_obs, expo, g0f, cf, df, by_hop, by_chip), mib=16, work=30,
     )
-    next_first = lax.ppermute(first, ALL, down)
+    others = lax.ppermute(edges, "c", [(0, 1), (1, 0)])
     ys, payload = call(
         last_kernel, [stars, (24, LO)],
         (tile_obs, fit, g0s, ds, cs, g0f, df, cf, yf, ru),
         scratch=[pltpu.VMEM(stars, F32)], mib=16, work=30,
     )
-    payload = call(edge_kernel, [(NZ, 24, LO)], (payload, yf, next_first))
-    sums = exchange(payload, "zl").sum(axis=0)
-    sums = to_all(sums, 32, PLANE)
+    payload = exchange(call(edge_kernel, [(NZ, 24, LO)], (payload, edges, others)), "zl")
+    sums = exchange(call(column_kernel, [(32, 24, LO)], (payload,)), PLANE)
     star, zero, flat = call(
         finish_kernel, [(4, LO), (4, LO), (8, 2 * LO)], (sums, g0z, dz, g0s, ys, g0f, yf)
     )

time: 117 us -> 114 us (0.974)
  local copies, waits for them, and re-layouts: 4.24 us -> 0.76 us
    unnamed x12 -> x2, local copies, waits for them, and re-layouts: 3.47 us -> 0.01 us
where the time goes in v5:
time: 114 us
  blocking collectives  49.5 us (43%)
  starting transfers between devices  42.4 us (37%)
  Pallas kernels  17.4 us (15%)
  waiting for transfers between devices  2.86 us (3%)
    all_to_all x3, blocking collectives, exchange(): return lax.all_to_all(blocks, axes, 0, 0, tiled=True)  49.5 us
    all_to_all x2, starting transfers between devices, exchange(): return lax.all_to_all(blocks, axes, 0, 0, tiled=True)  23.5 us
    pallas_call x8, Pallas kernels, call(): pl.pallas_call(kernel, out_shape=tuple(out) if many else out[0], in_specs...  17.4 us
    ppermute x1, starting transfers between devices, on_device(): partner = lax.ppermute(obs, 'zh', [(0, 1), (1, 0)])  12 us
    ppermute x1, waiting for transfers between devices, on_device(): partner = lax.ppermute(obs, 'zh', [(0, 1), (1, 0)])  2.73 us
    ppermute x1, starting transfers between devices, on_device(): by_hop = lax.ppermute(hop_row, ALL, hop)  2.58 us
    ppermute x1, starting transfers between devices, on_device(): others = lax.ppermute(edges, 'c', [(0, 1), (1, 0)])  2.41 us
  transfers between devices with their start and end apart: 6, of which 2 were waited for; matrix products, arithmetic and copies ran while one was open for 0% of the time, Pallas kernels for 10%

profile of v5, /device:TPU:1, one launch (start us, length us, event | category | flops | bytes accessed | tf_op | source)
XLA Modules:
  0.0 113.6 jit_solution(6065038335426415011)
XLA Ops:
  0.6 2.5 %shard_map.85 = (f32[80,128]{1,0:T(8,128)}, f32[16,8,128]{2,1,0:T(8,128)}) custom-call(s32[1,16]{1,0:T(1,128)} %block_ref.1, s32[16,128]{1,0:T(8,128)} %bitcast.13, s32[16,128]{1,0:T(8,128)} %bitcast.14, s32[16,128]{1,0:T(8,128)} %bitcast.15, f32[16,128]{1,0:T(8,128)} %bitcast.16, f32[16,128]{1,0:T(8,128)} %bitcast.17), custom_call_target="tpu_custom_call" | custom-call | flops 1048576 | bytes 1048576 | tf_op jit(solution)/shard_map/pallas_call | solution.py:458
  3.1 15.7 %all-to-all-start = ((f32[16,8,128]{2,1,0:T(8,128)}), f32[16,8,128]{2,1,0:T(8,128)S(1)}, u32[]{:S(2)}, u32[]{:S(2)}) async-start(f32[16,8,128]{2,1,0:T(8,128)} %get-tuple-element.26), calls=%async_computation | async-start | bytes 131072 | tf_op jit(solution)/shard_map/all_to_all | solution.py:470
  18.9 0.0 copy-done
  18.9 12.0 %collective-permute-start = (f32[80,128]{1,0:T(8,128)S(1)}, f32[80,128]{1,0:T(8,128)S(1)}, u32[]{:S(2)}, u32[]{:S(2)}) collective-permute-start(f32[80,128]{1,0:T(8,128)S(1)} %copy-done), channel_id=1, source_target_pairs={{0,1},{1,0},{2,3},{3,2},{4,5},{5,4},{6,7},{7,6},{8,9},{9,8},{10,11... | collective-permute-start | bytes 122888 | tf_op jit(solution)/shard_map/ppermute | solution.py:505
  30.9 0.1 all-to-all-done
  31.0 2.7 %collective-permute-done = f32[80,128]{1,0:T(8,128)S(1)} collective-permute-done((f32[80,128]{1,0:T(8,128)S(1)}, f32[80,128]{1,0:T(8,128)S(1)}, u32[]{:S(2)}, u32[]{:S(2)}) %collective-permute-start) | collective-permute-done | bytes 40992 | tf_op jit(solution)/shard_map/ppermute | solution.py:505
  33.8 10.0 %all_to_all.25.obs_ref = f32[4,176,128]{2,1,0:T(8,128)S(1)} all-to-all(f32[4,176,128]{2,1,0:T(8,128)S(1)} %broadcast_in_dim.6), channel_id=1, replica_groups=mesh['x'=4,'zl'=8,'c'=2,'y'=4,'zh'=2] {'y'}, dimensions={0} | all-to-all | bytes 720896 | tf_op jit(solution)/shard_map/all_to_all | solution.py:470
  43.8 0.7 broadcast_in_dim.15
  44.5 7.7 %all-to-all-start.2 = ((f32[8,64,128]{2,1,0:T(8,128)}), f32[8,64,128]{2,1,0:T(8,128)S(1)}, u32[]{:S(2)}, u32[]{:S(2)}) async-start(f32[8,64,128]{2,1,0:T(8,128)} %broadcast_in_dim.15), calls=%async_computation.2 | async-start | bytes 524288 | tf_op jit(solution)/shard_map/all_to_all | solution.py:470
  52.3 3.3 %shard_map.86 = (f32[2,16,128]{2,1,0:T(8,128)S(1)}, f32[2,16,128]{2,1,0:T(8,128)S(1)}, f32[16,128]{1,0:T(8,128)S(1)}, f32[16,128]{1,0:T(8,128)S(1)}, f32[2,128]{1,0:T(2,128)S(1)}, /*index=5*/f32[2,128]{1,0:T(2,128)S(1)}) custom-call(f32[4,176,128]{2,1,0:T(8,128)S(1)} %all_to_all.25.obs_ref), custom_call_target="tpu_custom_call" | custom-call | flops 536870912 | bytes 1048576 | tf_op jit(solution)/shard_map/pallas_call | solution.py:458
  55.6 2.6 %collective-permute-start.1 = (f32[2,128]{1,0:T(2,128)S(1)}, f32[2,128]{1,0:T(2,128)S(1)}, u32[]{:S(2)}, u32[]{:S(2)}) collective-permute-start(f32[2,128]{1,0:T(2,128)S(1)} %get-tuple-element.31), channel_id=1, source_target_pairs={{8,16},{16,8},{9,17},{17,9},{10,18},{18,10},{11,19},{19,11},{12,20... | collective-permute-start | bytes 3080 | tf_op jit(solution)/shard_map/ppermute | solution.py:516
  58.2 1.9 %collective-permute-start.2 = (f32[2,128]{1,0:T(2,128)S(1)}, f32[2,128]{1,0:T(2,128)S(1)}, u32[]{:S(2)}, u32[]{:S(2)}) collective-permute-start(f32[2,128]{1,0:T(2,128)S(1)} %get-tuple-element.32), channel_id=1, source_target_pairs={{0,8},{8,0},{1,9},{9,1},{2,10},{10,2},{3,11},{11,3},{4,12},{12,4},... | collective-permute-start | bytes 3080 | tf_op jit(solution)/shard_map/ppermute | solution.py:517
  60.1 5.0 %shard_map.87 = (f32[2,16,128]{2,1,0:T(8,128)S(1)}, f32[16,128]{1,0:T(8,128)S(1)}, f32[16,64]{1,0:T(8,128)S(1)}) custom-call(f32[4,176,128]{2,1,0:T(8,128)S(1)} %all_to_all.25.obs_ref, f32[2,16,128]{2,1,0:T(8,128)S(1)} %get-tuple-element.28.g0s_ref, f32[16,128]{1,0:T(8,128)S(1)} %get-tuple-element.27.g0f_ref), custom_call_target="tpu_custom_call" | custom-call | flops 1073741824 | bytes 1048576 | tf_op jit(solution)/shard_map/pallas_call | solution.py:458
  65.1 0.0 collective-permute-done.1.hop_ref
  65.1 0.0 collective-permute-done.2.chip_ref
  65.1 0.0 all-to-all-done.2.expo_ref
  65.1 2.7 %shard_map.88 = (f32[4,8,4096]{2,1,0:T(8,128)S(1)}, f32[16,128]{1,0:T(8,128)S(1)}, f32[16,128]{1,0:T(8,128)S(1)}, f32[4,16,64]{2,1,0:T(8,128)S(1)}, f32[4,16,64]{2,1,0:T(8,128)S(1)}, /*index=5*/f32[4,128]{1,0:T(4,128)S(1)}) custom-call(f32[4,176,128]{2,1,0:T(8,128)S(1)} %all_to_all.25.obs_ref, f32[8,64,128]{2,1,0:T(8,128)S(1)} %all-to-all-done.2.expo_ref, ...), custom_call_target="tpu_custom_call" | custom-call | flops 1073741824 | bytes 1048576 | tf_op jit(solution)/shard_map/pallas_call | solution.py:458
  67.8 2.4 %collective-permute-start.3 = (f32[4,128]{1,0:T(4,128)S(1)}, f32[4,128]{1,0:T(4,128)S(1)}, u32[]{:S(2)}, u32[]{:S(2)}) collective-permute-start(f32[4,128]{1,0:T(4,128)S(1)} %get-tuple-element.40.mine_ref), channel_id=1, source_target_pairs={{0,8},{8,0},{1,9},{9,1},{2,10},{10,2},{3,11},{11,3},{4,12},{12,4},... | collective-permute-start | bytes 6152 | tf_op jit(solution)/shard_map/ppermute | solution.py:526
  70.2 2.9 %shard_map.89 = (f32[2,16,128]{2,1,0:T(8,128)S(1)}, f32[24,128]{1,0:T(8,128)S(1)}) custom-call(f32[4,176,128]{2,1,0:T(8,128)S(1)} %all_to_all.25.obs_ref, f32[4,8,4096]{2,1,0:T(8,128)S(1)} %get-tuple-element.33.fit_ref, f32[2,16,128]{2,1,0:T(8,128)S(1)} %get-tuple-element.28.g0s_ref, f32[2,16,128]{2,1,0:T(8,128)S(1)} %get-tuple-element.34.ds_ref, ...), custom_call_target="tpu_custom_call" | custom-call | flops 1073741824 | bytes 1048576 | tf_op jit(solution)/shard_map/pallas_call | solution.py:458
  73.1 0.0 collective-permute-done.3.other_ref
  73.1 0.1 shard_map.90
  73.2 23.0 %all_to_all.26.parts_ref = f32[8,24,128]{2,1,0:T(8,128)S(1)} all-to-all(f32[8,24,128]{2,1,0:T(8,128)S(1)} %shard_map.90), channel_id=1, replica_groups=mesh['x'=4,'zl'=8,'c'=2,'y'=4,'zh'=2] {'zl'}, dimensions={0} | all-to-all | bytes 196608 | tf_op jit(solution)/shard_map/all_to_all | solution.py:470
  96.2 16.4 %all_to_all.27.sums_ref = f32[32,24,128]{2,1,0:T(8,128)S(1)} all-to-all(f32[32,24,128]{2,1,0:T(8,128)S(1)} %shard_map.91), channel_id=1, replica_groups=mesh['x'=4,'zl'=8,'c'=2,'y'=4,'zh'=2] {'x','c','y'}, dimensions={0} | all-to-all | bytes 786432 | tf_op jit(solution)/shard_map/all_to_all | solution.py:470
  112.6 1.0 shard_map.92
  (7 shorter events, 0.1 us)
Async XLA Ops:
  3.1 15.8 %copy-start = (f32[80,128]{1,0:T(8,128)S(1)}, f32[80,128]{1,0:T(8,128)}, u32[]{:S(2)}) copy-start(f32[80,128]{1,0:T(8,128)} %get-tuple-element.25) | copy-start | bytes 122884
  3.1 27.9 %all-to-all-start = ((f32[16,8,128]{2,1,0:T(8,128)}), f32[16,8,128]{2,1,0:T(8,128)S(1)}, u32[]{:S(2)}, u32[]{:S(2)}) async-start(f32[16,8,128]{2,1,0:T(8,128)} %get-tuple-element.26), calls=%async_computation | async-start | bytes 131072 | tf_op jit(solution)/shard_map/all_to_all | solution.py:470
  18.9 14.9 %collective-permute-start = (f32[80,128]{1,0:T(8,128)S(1)}, f32[80,128]{1,0:T(8,128)S(1)}, u32[]{:S(2)}, u32[]{:S(2)}) collective-permute-start(f32[80,128]{1,0:T(8,128)S(1)} %copy-done), channel_id=1, source_target_pairs={{0,1},{1,0},{2,3},{3,2},{4,5},{5,4},{6,7},{7,6},{8,9},{9,8},{10,11... | collective-permute-start | bytes 122888 | tf_op jit(solution)/shard_map/ppermute | solution.py:505
  44.5 20.5 %all-to-all-start.2 = ((f32[8,64,128]{2,1,0:T(8,128)}), f32[8,64,128]{2,1,0:T(8,128)S(1)}, u32[]{:S(2)}, u32[]{:S(2)}) async-start(f32[8,64,128]{2,1,0:T(8,128)} %broadcast_in_dim.15), calls=%async_computation.2 | async-start | bytes 524288 | tf_op jit(solution)/shard_map/all_to_all | solution.py:470
  55.6 9.5 %collective-permute-start.1 = (f32[2,128]{1,0:T(2,128)S(1)}, f32[2,128]{1,0:T(2,128)S(1)}, u32[]{:S(2)}, u32[]{:S(2)}) collective-permute-start(f32[2,128]{1,0:T(2,128)S(1)} %get-tuple-element.31), channel_id=1, source_target_pairs={{8,16},{16,8},{9,17},{17,9},{10,18},{18,10},{11,19},{19,11},{12,20... | collective-permute-start | bytes 3080 | tf_op jit(solution)/shard_map/ppermute | solution.py:516
  58.2 6.9 %collective-permute-start.2 = (f32[2,128]{1,0:T(2,128)S(1)}, f32[2,128]{1,0:T(2,128)S(1)}, u32[]{:S(2)}, u32[]{:S(2)}) collective-permute-start(f32[2,128]{1,0:T(2,128)S(1)} %get-tuple-element.32), channel_id=1, source_target_pairs={{0,8},{8,0},{1,9},{9,1},{2,10},{10,2},{3,11},{11,3},{4,12},{12,4},... | collective-permute-start | bytes 3080 | tf_op jit(solution)/shard_map/ppermute | solution.py:517
  67.8 5.4 %collective-permute-start.3 = (f32[4,128]{1,0:T(4,128)S(1)}, f32[4,128]{1,0:T(4,128)S(1)}, u32[]{:S(2)}, u32[]{:S(2)}) collective-permute-start(f32[4,128]{1,0:T(4,128)S(1)} %get-tuple-element.40.mine_ref), channel_id=1, source_target_pairs={{0,8},{8,0},{1,9},{9,1},{2,10},{10,2},{3,11},{11,3},{4,12},{12,4},... | collective-permute-start | bytes 6152 | tf_op jit(solution)/shard_map/ppermute | solution.py:526

commit v6 on v5

--- a/solution.py
+++ b/solution.py
@@ -19,14 +19,16 @@
 NT = (((1,), (1,)), ((), ()))
 NN = (((1,), (0,)), ((), ()))
 S, PX, E, W, WM = range(5)
+EXACT, FEW = 3, 2
 STAR, FLAT = 3, 7
 
 
-def split3(v):
-    first = v.astype(BF16)
-    rest = v - first.astype(F32)
-    second = rest.astype(BF16)
-    return first, second, (rest - second.astype(F32)).astype(BF16)
+def split(v, count):
+    parts = []
+    for _ in range(count):
+        parts.append(v.astype(BF16))
+        v = v - parts[-1].astype(F32)
+    return parts
 
 
 def row_iota(shape):
@@ -69,13 +71,15 @@
     ]
     sums = lax.dot_general(jnp.concatenate(rows, axis=0), hot, NT, preferred_element_type=F32)
     sums = [sums[at : at + HI] for at in range(0, sums.shape[0], HI)]
-    return [sums[i] + sums[i + 1] + sums[i + 2] for i in range(0, len(sums), 3)]
+    count = len(values[0])
+    return [sum(sums[i + 1 : i + count], sums[i]) for i in range(0, len(sums), count)]
 
 
 def picked(table, hi, hot):
-    parts = jnp.concatenate([part.astype(F32) for part in split3(table)], axis=0).astype(BF16)
-    parts = lax.dot_general(parts, hot, NN, preferred_element_type=F32)
-    found = parts[:HI] + parts[HI : 2 * HI] + parts[2 * HI :]
+    parts = lax.dot_general(
+        jnp.concatenate(split(table, FEW), axis=0), hot, NN, preferred_element_type=F32
+    )
+    found = sum((parts[at : at + HI] for at in range(HI, parts.shape[0], HI)), parts[:HI])
     found = jnp.where(joined(is_row(hi, HI)), found, 0.0)
     return found[:8] + found[8:]
 
@@ -100,7 +104,7 @@
 
 
 def split_rows(tiles):
-    return [rows_of(part) for part in zip(*(split3(tile) for tile in tiles))]
+    return [rows_of(part) for part in zip(*(split(tile, EXACT) for tile in tiles))]
 
 
 class Ids:
@@ -170,7 +174,11 @@
     return [field(obs_ref, y, rel, kk, f) for rel in range(2)]
 
 
-def sums_kernel(obs_ref, g0s_ref, ds_ref, g0f_ref, df_ref, hop_ref, chip_ref):
+def edge_rows(flat):
+    return jnp.concatenate([flat[0:1], flat[8:9], flat[7:8], flat[15:16]], axis=0)
+
+
+def sums_kernel(obs_ref, g0s_ref, ds_ref, g0f_ref, df_ref, hop_ref, plane_ref):
     for ref in (g0s_ref, ds_ref, g0f_ref, df_ref):
         ref[...] = jnp.zeros(ref.shape, F32)
 
@@ -194,11 +202,13 @@
     diag = ds_ref[...] + RIDGE
     g0s_ref[...] = g0s_ref[...] / diag
     ds_ref[...] = diag
-    odd = lax.axis_index("c") == 1
-    top = jnp.concatenate([g0f[0:1], g0f[8:9]], axis=0)
-    bot = jnp.concatenate([g0f[7:8], g0f[15:16]], axis=0)
-    hop_ref[...] = jnp.where(odd, bot, top)
-    chip_ref[...] = jnp.where(odd, top, bot)
+    edges = edge_rows(g0f)
+    hop_ref[...] = jnp.where(lax.axis_index("c") == 1, edges[2:4], edges[0:2])
+    for peer in range(NX * NC):
+        for y in range(NY):
+            plane_ref[peer, 16 * y : 16 * y + 16] = obs_ref[y, 160:176]
+        plane_ref[peer, 64:68] = edges
+        plane_ref[peer, 68:72] = jnp.zeros((4, LO), F32)
 
 
 def couple_kernel(obs_ref, g0s_ref, g0f_ref, cs_ref, cf_ref, ru_ref, fit_ref):
@@ -211,7 +221,7 @@
         fit = joined(rows_of(chunk(obs_ref, step, W))) * gather_both(
             (g0s_ref[step // 2], star.full, hs), (g0f_ref[...], flat.full, hp)
         )
-        parts = split3(fit)
+        parts = split(fit, FEW)
         (added,) = scatter([[across(part, FLAT) for part in parts]], star.bf, hs)
         cs_ref[step // 2] += added
         (added,) = scatter([[across(part, STAR) for part in parts]], flat.bf, hp)
@@ -226,7 +236,7 @@
         ids = Ids(own(obs_ref, y, kk, E), HALF, (0, 8))
         at = pl.ds(pl.multiple_of((y % 2) * 2048, 2048), 2048)
         fit = fit_ref[2 * kk + y // 2, :, at]
-        parts = split3(row(fit, STAR) + row(fit, FLAT))
+        parts = split(row(fit, STAR) + row(fit, FLAT), FEW)
         (added,) = scatter([[across(part, 0) for part in parts]], ids.bf, ids.hot())
         total += added
     ru_ref[...] = total
@@ -251,12 +261,12 @@
 
 
 def expo_apply_kernel(
-    obs_ref, expo_ref, g0f_ref, cf_ref, df_ref, hop_ref, chip_ref,
-    fit_ref, cf_out, yf_out, g0z_out, dz_out, edge_out,
+    obs_ref, expo_ref, g0f_ref, cf_ref, df_ref, hop_ref,
+    fit_ref, cf_out, yf_out, g0z_out, dz_out,
 ):
-    part = expo_ref[0]
+    part = expo_ref[0, 0:64]
     for xc in range(1, 8):
-        part = part + expo_ref[xc]
+        part = part + expo_ref[xc, 0:64]
     for y in range(4):
         diag = part[16 * y : 16 * y + 16, HALF:] + RIDGE
         g0z_out[y] = part[16 * y : 16 * y + 16, :HALF] / diag
@@ -277,19 +287,19 @@
         fit = joined(rows_of(chunk(obs_ref, step, W))) * joined(found)
         fit_ref[step] = fit
         flat = Ids(chunk(obs_ref, step, PX), LO)
-        (added,) = scatter([[across(part, 0) for part in split3(fit)]], flat.bf, flat.hot())
+        (added,) = scatter([[across(part, 0) for part in split(fit, FEW)]], flat.bf, flat.hot())
         cf_out[...] += added
         return carry
 
     lax.fori_loop(0, 4, apply, 0)
-    odd = lax.axis_index("c") == 1
-    above = jnp.where(odd, chip_ref[...], hop_ref[...])
-    below = jnp.where(odd, hop_ref[...], chip_ref[...])
+    x, c = lax.axis_index("x"), lax.axis_index("c")
+    chip = expo_ref[2 * x + 1 - c, 64:68]
+    above = jnp.where(c == 1, chip[2:4], hop_ref[...])
+    below = jnp.where(c == 1, hop_ref[...], chip[0:2])
     cf = cf_out[...] - SMOOTH * beside(g0f_ref[...], above, below)
     cf_out[...] = cf
     yf = cf / df_ref[...]
     yf_out[...] = yf
-    edge_out[...] = jnp.concatenate([yf[0:1], yf[8:9], yf[7:8], yf[15:16]], axis=0)
 
 
 def fold8(a):
@@ -313,7 +323,7 @@
 
     def finish_star(step, carry):
         star = Ids(chunk(obs_ref, step, S), LO)
-        parts = split3(fit_ref[step])
+        parts = split(fit_ref[step], FEW)
         (added,) = scatter([[across(part, 0) for part in parts]], star.bf, star.hot())
         cs_ref[step // 2] += added
         return carry
@@ -338,51 +348,41 @@
         w = joined(rows_of(own(obs_ref, y, kk, W)))
         both = gather_both((ys_ref[kk], star.full, star.hot()), (yf, flat.full, flat.hot()))
         from_star, from_flat = row(both, STAR), row(both, FLAT)
-        parts = split3(w * (from_star + from_flat))
+        parts = split(w * (from_star + from_flat), FEW)
         (added,) = scatter([[across(part, 0) for part in parts]], expo.bf, expo.hot())
         total += added
         cross += fold_lanes(w * from_star * from_flat)
-    ru = ru_ref[...]
-    out_ref[0:16] = jnp.concatenate([ru, total], axis=1)
+    expos = joined([ru_ref[...], total])
     g0f, df, cf = g0f_ref[...], df_ref[...], cf_ref[...]
     none = jnp.zeros((2, LO), F32)
     rho = 0.25 * (rho + fold8(g0f * g0f * df))
     beta = 0.25 * (beta + fold8(g0f * cf))
     eta = 0.25 * (eta + fold8(cf * yf))
     delta = 2.0 * cross - (0.25 * SMOOTH) * fold8(yf * beside(yf, none, none))
-    out_ref[16:24] = jnp.concatenate([rho, beta, eta, delta, jnp.zeros((4, LO), F32)], axis=0)
+    scal = jnp.concatenate([rho, beta, eta, delta, edge_rows(yf)], axis=0)
+    for zl in range(NZ):
+        for c in range(NC):
+            out_ref[NC * zl + c, 0:8] = expos[8 * c : 8 * c + 8]
+            out_ref[NC * zl + c, 8:16] = scal
 
 
 def edge_dot(last, first):
     both = last * first
-    return -(0.25 * SMOOTH) * (both[0:1] + both[1:2])
-
-
-def edge_kernel(payload_ref, mine_ref, other_ref, out_ref):
-    odd = lax.axis_index("c") == 1
-    mine, other = mine_ref[...], other_ref[...]
-    upper, lower = jnp.where(odd, other, mine), jnp.where(odd, mine, other)
-    chip = edge_dot(upper[2:4], lower[0:2])
-    scal = payload_ref[16:24]
-    scal = scal + jnp.where(row_iota((8, LO)) == 3, chip, 0.0)
-    scal = jnp.concatenate([scal[0:4], upper[0:2], lower[2:4]], axis=0)
-    for peer in range(NZ):
-        out_ref[peer, 0:16] = payload_ref[0:16]
-        out_ref[peer, 16:24] = scal
+    return -(0.5 * SMOOTH) * (both[0:1] + both[1:2])
 
 
 def column_kernel(parts_ref, out_ref):
     total = parts_ref[0]
-    for peer in range(1, NZ):
+    for peer in range(1, NZ * NC):
         total = total + parts_ref[peer]
-    between = edge_dot(parts_ref[0, 22:24], parts_ref[1, 20:22])
-    for peer in range(1, NZ - 1):
-        between += edge_dot(parts_ref[peer, 22:24], parts_ref[peer + 1, 20:22])
-    scal = total[16:20] + jnp.where(row_iota((4, LO)) == 3, between, 0.0)
-    ends = jnp.concatenate([scal, parts_ref[0, 20:22], parts_ref[NZ - 1, 22:24]], axis=0)
+    between = edge_dot(parts_ref[0, 14:16], parts_ref[1, 12:14])
+    for peer in range(1, NZ * NC - 1):
+        between += edge_dot(parts_ref[peer, 14:16], parts_ref[peer + 1, 12:14])
+    scal = total[8:12] + jnp.where(row_iota((4, LO)) == 3, between, 0.0)
+    ends = jnp.concatenate([scal, parts_ref[0, 12:14], parts_ref[NZ * NC - 1, 14:16]], axis=0)
     for peer in range(NX * NC * NY):
-        out_ref[peer, 0:16] = total[0:16]
-        out_ref[peer, 16:24] = ends
+        out_ref[peer, 0:8] = total[0:8]
+        out_ref[peer, 8:16] = ends
 
 
 def whole(a):
@@ -393,16 +393,21 @@
     sums_ref, g0z_ref, dz_ref, g0s_ref, ys_ref, g0f_ref, yf_ref, star_out, zero_out, flat_out
 ):
     y, zh = lax.axis_index("y"), lax.axis_index("zh")
-    scal = sums_ref[0, 16:24]
-    for peer in range(1, 32):
-        scal = scal + sums_ref[peer, 16:24]
+    scal = jnp.zeros((4, LO), F32)
+    for x in range(NX):
+        for i in range(NY):
+            scal = scal + sums_ref[8 * x + i, 8:12]
     z_rho = jnp.zeros((HI, HALF), F32)
     z_beta, z_eta, z_delta = z_rho, z_rho, z_rho
     z_own = z_rho
     for i in range(4):
-        part = sums_ref[i, 0:16]
-        for xc in range(1, 8):
-            part = part + sums_ref[xc * 4 + i, 0:16]
+        halves = []
+        for c in range(NC):
+            half = sums_ref[4 * c + i, 0:8]
+            for x in range(1, NX):
+                half = half + sums_ref[8 * x + 4 * c + i, 0:8]
+            halves.append(half)
+        part = jnp.concatenate(halves, axis=0)
         cz, qz = part[:, :HALF], part[:, HALF:]
         g0z, dz = g0z_ref[i], dz_ref[i]
         yz = cz / dz
@@ -416,7 +421,7 @@
     eta = whole(z_eta) + whole(scal[2:3])
     between = jnp.zeros((1, LO), F32)
     for x in range(NX - 1):
-        between += 8.0 * edge_dot(sums_ref[8 * x, 22:24], sums_ref[8 * x + 8, 20:22])
+        between += 4.0 * edge_dot(sums_ref[8 * x, 14:16], sums_ref[8 * x + 8, 12:14])
     delta = 2.0 * whole(z_delta) + whole(scal[3:4] + between)
     curv0 = rho0 + beta
     step0 = rho0 / curv0
@@ -474,25 +479,25 @@
     return exchange(jnp.broadcast_to(block[None], (peers, *block.shape)), axes)
 
 
-def flat_pairs():
+def hop_pairs():
     def place(tile, y, zh):
         x, rest = divmod(tile, NZ * NC)
         zl, c = divmod(rest, NC)
         return (((x * NZ + zl) * NC + c) * NY + y) * NH + zh
 
-    chip, hop = [], []
-    for tile in range(NX * NZ * NC - 1):
+    hop = []
+    for tile in range(1, NX * NZ * NC - 1, 2):
         far = (tile + 1) % (NZ * NC) == 0
         for y in range(NY):
             for zh in range(NH):
                 here, there = place(tile, y, zh), place(tile + 1, y, 1 - zh if far else zh)
-                (hop if tile % 2 else chip).extend([(here, there), (there, here)])
-    return chip, hop
+                hop.extend([(here, there), (there, here)])
+    return hop
 
 
 def on_device(star_slot, star_block, exposure, superpixel, magnitude, weight):
     zh = lax.axis_index("zh")
-    chip, hop = flat_pairs()
+    hop = hop_pairs()
     stars, flats, expos = (2, HI, LO), (HI, LO), (4, HI, HALF)
     obs, expo = call(
         pack_kernel, [(80, LO), (16, 8, LO)],
@@ -508,29 +513,26 @@
     expo = jnp.where(zh == 0, expo, expo[::-1]).reshape(HI, LO)
     tile_obs = jnp.concatenate([obs, partner, expo], axis=0)
     tile_obs = to_all(lax.optimization_barrier(tile_obs), NY, "y")
-    tile_obs = lax.optimization_barrier(tile_obs)
-    expo = to_all(tile_obs[:, 160:].reshape(64, LO), 8, COLS)
-    g0s, ds, g0f, df, hop_row, chip_row = call(
-        sums_kernel, [stars] * 2 + [flats] * 2 + [(2, LO)] * 2, (tile_obs,), mib=16, work=29
-    )
+    g0s, ds, g0f, df, hop_row, plane = call(
+        sums_kernel, [stars] * 2 + [flats] * 2 + [(2, LO), (8, 72, LO)], (tile_obs,), mib=16, work=29
+    )
+    expo = exchange(plane, COLS)
     by_hop = lax.ppermute(hop_row, ALL, hop)
-    by_chip = lax.ppermute(chip_row, ALL, chip)
     cs, cf, ru = call(
         couple_kernel, [stars, flats, (HI, HALF)], (tile_obs, g0s, g0f),
         scratch=[pltpu.VMEM((4, 8, 4096), F32)], mib=16, work=30,
     )
-    fit, cf, yf, g0z, dz, edges = call(
-        expo_apply_kernel, [(4, 8, 4096)] + [flats] * 2 + [expos] * 2 + [(4, LO)],
-        (tile_obs, expo, g0f, cf, df, by_hop, by_chip), mib=16, work=30,
-    )
-    others = lax.ppermute(edges, "c", [(0, 1), (1, 0)])
+    fit, cf, yf, g0z, dz = call(
+        expo_apply_kernel, [(4, 8, 4096)] + [flats] * 2 + [expos] * 2,
+        (tile_obs, expo, g0f, cf, df, by_hop), mib=16, work=30,
+    )
     ys, payload = call(
-        last_kernel, [stars, (24, LO)],
+        last_kernel, [stars, (16, 16, LO)],
         (tile_obs, fit, g0s, ds, cs, g0f, df, cf, yf, ru),
         scratch=[pltpu.VMEM(stars, F32)], mib=16, work=30,
     )
-    payload = exchange(call(edge_kernel, [(NZ, 24, LO)], (payload, edges, others)), "zl")
-    sums = exchange(call(column_kernel, [(32, 24, LO)], (payload,)), PLANE)
+    payload = exchange(payload, ("zl", "c"))
+    sums = exchange(call(column_kernel, [(32, 16, LO)], (payload,)), PLANE)
     star, zero, flat = call(
         finish_kernel, [(4, LO), (4, LO), (8, 2 * LO)], (sums, g0z, dz, g0s, ys, g0f, yf)
     )

time: 114 us -> 109 us (0.956)
  starting transfers between devices: 42.4 us -> 38 us
    ppermute x2 -> x0, starting transfers between devices: 4.33 us -> none  [the longest x1 2.41 us: on_device(): others = lax.ppermute(edges, 'c', [(0, 1), (1, 0)])]
    pallas_call x8 -> x7, Pallas kernels: 17.4 us -> 17.8 us  [call(): pl.pallas_call(kernel, out_shape=tuple(out) if many else out[0], in_specs...]
  transfers between devices with their start and end apart: 6 -> 4, of which waited for: 2 -> 2; matrix products, arithmetic and copies ran while one was open for 0% -> 0% of each run, Pallas kernels for 10% -> 5%
where the time goes in v6:
time: 109 us; the launch traced here: 108 us
  blocking collectives  48.9 us (45%)
  starting transfers between devices  38 us (35%)
  Pallas kernels  17.8 us (16%)
  waiting for transfers between devices  2.84 us (3%)
    all_to_all x3, blocking collectives, exchange(): return lax.all_to_all(blocks, axes, 0, 0, tiled=True)  48.9 us
    all_to_all x2, starting transfers between devices, exchange(): return lax.all_to_all(blocks, axes, 0, 0, tiled=True)  23.5 us
    pallas_call x7, Pallas kernels, call(): pl.pallas_call(kernel, out_shape=tuple(out) if many else out[0], in_specs...  17.8 us
    ppermute x1, starting transfers between devices, on_device(): partner = lax.ppermute(obs, 'zh', [(0, 1), (1, 0)])  12 us
    ppermute x1, waiting for transfers between devices, on_device(): partner = lax.ppermute(obs, 'zh', [(0, 1), (1, 0)])  2.73 us
    ppermute x1, starting transfers between devices, on_device(): by_hop = lax.ppermute(hop_row, ALL, hop)  2.57 us
  transfers between devices with their start and end apart: 4, of which 2 were waited for; matrix products, arithmetic and copies ran while one was open for 0% of the time, Pallas kernels for 5%

profile of v6, /device:TPU:1, one launch (start us, length us, event | category | flops | bytes accessed | tf_op | source)
XLA Modules:
  0.0 108.4 jit_solution(7061862254885348577)
XLA Ops:
  0.6 2.5 %shard_map.85 = (f32[80,128]{1,0:T(8,128)}, f32[16,8,128]{2,1,0:T(8,128)}) custom-call(s32[1,16]{1,0:T(1,128)} %block_ref.1, s32[16,128]{1,0:T(8,128)} %bitcast.11, s32[16,128]{1,0:T(8,128)} %bitcast.12, s32[16,128]{1,0:T(8,128)} %bitcast.13, f32[16,128]{1,0:T(8,128)} %bitcast.14, f32[16,128]{1,0:T(8,128)} %bitcast.15), custom_call_target="tpu_custom_call" | custom-call | flops 1048576 | bytes 1048576 | tf_op jit(solution)/shard_map/pallas_call | solution.py:463
  3.1 0.0 copy-start
  3.1 15.7 %all-to-all-start = ((f32[16,8,128]{2,1,0:T(8,128)}), f32[16,8,128]{2,1,0:T(8,128)S(1)}, u32[]{:S(2)}, u32[]{:S(2)}) async-start(f32[16,8,128]{2,1,0:T(8,128)} %get-tuple-element.25), calls=%async_computation | async-start | bytes 131072 | tf_op jit(solution)/shard_map/all_to_all | solution.py:475
  18.9 0.0 copy-done
  18.9 12.0 %collective-permute-start = (f32[80,128]{1,0:T(8,128)S(1)}, f32[80,128]{1,0:T(8,128)S(1)}, u32[]{:S(2)}, u32[]{:S(2)}) collective-permute-start(f32[80,128]{1,0:T(8,128)S(1)} %copy-done), channel_id=1, source_target_pairs={{0,1},{1,0},{2,3},{3,2},{4,5},{5,4},{6,7},{7,6},{8,9},{9,8},{10,11... | collective-permute-start | bytes 122888 | tf_op jit(solution)/shard_map/ppermute | solution.py:510
  30.9 0.1 all-to-all-done
  31.0 2.7 %collective-permute-done = f32[80,128]{1,0:T(8,128)S(1)} collective-permute-done((f32[80,128]{1,0:T(8,128)S(1)}, f32[80,128]{1,0:T(8,128)S(1)}, u32[]{:S(2)}, u32[]{:S(2)}) %collective-permute-start) | collective-permute-done | bytes 40992 | tf_op jit(solution)/shard_map/ppermute | solution.py:510
  33.8 10.0 %all_to_all.25.obs_ref = f32[4,176,128]{2,1,0:T(8,128)S(1)} all-to-all(f32[4,176,128]{2,1,0:T(8,128)S(1)} %broadcast_in_dim.2), channel_id=1, replica_groups=mesh['x'=4,'zl'=8,'c'=2,'y'=4,'zh'=2] {'y'}, dimensions={0} | all-to-all | bytes 720896 | tf_op jit(solution)/shard_map/all_to_all | solution.py:475
  43.8 4.0 %shard_map.86 = (f32[2,16,128]{2,1,0:T(8,128)S(1)}, f32[2,16,128]{2,1,0:T(8,128)S(1)}, f32[16,128]{1,0:T(8,128)S(1)}, f32[16,128]{1,0:T(8,128)S(1)}, f32[2,128]{1,0:T(2,128)S(1)}, /*index=5*/f32[8,72,128]{2,1,0:T(8,128)}) custom-call(f32[4,176,128]{2,1,0:T(8,128)S(1)} %all_to_all.25.obs_ref), custom_call_target="tpu_custom_call" | custom-call | flops 536870912 | bytes 1048576 | tf_op jit(solution)/shard_map/pallas_call | solution.py:463
  47.8 7.7 %all-to-all-start.2 = ((f32[8,72,128]{2,1,0:T(8,128)}), f32[8,72,128]{2,1,0:T(8,128)S(1)}, u32[]{:S(2)}, u32[]{:S(2)}) async-start(f32[8,72,128]{2,1,0:T(8,128)} %get-tuple-element.26), calls=%async_computation.2 | async-start | bytes 589824 | tf_op jit(solution)/shard_map/all_to_all | solution.py:475
  55.6 2.6 %collective-permute-start.1 = (f32[2,128]{1,0:T(2,128)S(1)}, f32[2,128]{1,0:T(2,128)S(1)}, u32[]{:S(2)}, u32[]{:S(2)}) collective-permute-start(f32[2,128]{1,0:T(2,128)S(1)} %get-tuple-element.31), channel_id=1, source_target_pairs={{8,16},{16,8},{9,17},{17,9},{10,18},{18,10},{11,19},{19,11},{12,20... | collective-permute-start | bytes 3080 | tf_op jit(solution)/shard_map/ppermute | solution.py:520
  58.1 4.9 %shard_map.87 = (f32[2,16,128]{2,1,0:T(8,128)S(1)}, f32[16,128]{1,0:T(8,128)S(1)}, f32[16,64]{1,0:T(8,128)S(1)}) custom-call(f32[4,176,128]{2,1,0:T(8,128)S(1)} %all_to_all.25.obs_ref, f32[2,16,128]{2,1,0:T(8,128)S(1)} %get-tuple-element.28.g0s_ref, f32[16,128]{1,0:T(8,128)S(1)} %get-tuple-element.27.g0f_ref), custom_call_target="tpu_custom_call" | custom-call | flops 1073741824 | bytes 1048576 | tf_op jit(solution)/shard_map/pallas_call | solution.py:463
  63.0 0.0 collective-permute-done.1.hop_ref
  63.0 0.0 all-to-all-done.2.expo_ref
  63.1 2.6 %shard_map.88 = (f32[4,8,4096]{2,1,0:T(8,128)S(1)}, f32[16,128]{1,0:T(8,128)S(1)}, f32[16,128]{1,0:T(8,128)S(1)}, f32[4,16,64]{2,1,0:T(8,128)S(1)}, f32[4,16,64]{2,1,0:T(8,128)S(1)}) custom-call(f32[4,176,128]{2,1,0:T(8,128)S(1)} %all_to_all.25.obs_ref, f32[8,72,128]{2,1,0:T(8,128)S(1)} %all-to-all-done.2.expo_ref, f32[16,128]{1,0:T(8,128)S(1)} %get-tuple-element.27.g0f_ref, ...), custom_call_target="tpu_custom_call" | custom-call | flops 1073741824 | bytes 1048576 | tf_op jit(solution)/shard_map/pallas_call | solution.py:463
  65.7 2.8 %shard_map.89 = (f32[2,16,128]{2,1,0:T(8,128)S(1)}, f32[16,16,128]{2,1,0:T(8,128)S(1)}) custom-call(f32[4,176,128]{2,1,0:T(8,128)S(1)} %all_to_all.25.obs_ref, f32[4,8,4096]{2,1,0:T(8,128)S(1)} %get-tuple-element.32.fit_ref, f32[2,16,128]{2,1,0:T(8,128)S(1)} %get-tuple-element.28.g0s_ref, f32[2,16,128]{2,1,0:T(8,128)S(1)} %get-tuple-element.33.ds_ref, ...), custom_call_target="tpu_custom_call" | custom-call | flops 1073741824 | bytes 1048576 | tf_op jit(solution)/shard_map/pallas_call | solution.py:463
  68.5 25.3 %all_to_all.26.parts_ref = f32[16,16,128]{2,1,0:T(8,128)S(1)} all-to-all(f32[16,16,128]{2,1,0:T(8,128)S(1)} %get-tuple-element.38), channel_id=1, replica_groups=mesh['x'=4,'zl'=8,'c'=2,'y'=4,'zh'=2] {'zl','c'}, dimensions={0} | all-to-all | bytes 262144 | tf_op jit(solution)/shard_map/all_to_all | solution.py:475
  93.9 13.6 %all_to_all.27.sums_ref = f32[32,16,128]{2,1,0:T(8,128)S(1)} all-to-all(f32[32,16,128]{2,1,0:T(8,128)S(1)} %shard_map.90), channel_id=1, replica_groups=mesh['x'=4,'zl'=8,'c'=2,'y'=4,'zh'=2] {'x','c','y'}, dimensions={0} | all-to-all | bytes 524288 | tf_op jit(solution)/shard_map/all_to_all | solution.py:475
  107.4 1.0 shard_map.91
  (5 shorter events, 0.1 us)
Async XLA Ops:
  3.1 15.8 %copy-start = (f32[80,128]{1,0:T(8,128)S(1)}, f32[80,128]{1,0:T(8,128)}, u32[]{:S(2)}) copy-start(f32[80,128]{1,0:T(8,128)} %get-tuple-element.24) | copy-start | bytes 122884
  3.1 27.9 %all-to-all-start = ((f32[16,8,128]{2,1,0:T(8,128)}), f32[16,8,128]{2,1,0:T(8,128)S(1)}, u32[]{:S(2)}, u32[]{:S(2)}) async-start(f32[16,8,128]{2,1,0:T(8,128)} %get-tuple-element.25), calls=%async_computation | async-start | bytes 131072 | tf_op jit(solution)/shard_map/all_to_all | solution.py:475
  18.9 14.9 %collective-permute-start = (f32[80,128]{1,0:T(8,128)S(1)}, f32[80,128]{1,0:T(8,128)S(1)}, u32[]{:S(2)}, u32[]{:S(2)}) collective-permute-start(f32[80,128]{1,0:T(8,128)S(1)} %copy-done), channel_id=1, source_target_pairs={{0,1},{1,0},{2,3},{3,2},{4,5},{5,4},{6,7},{7,6},{8,9},{9,8},{10,11... | collective-permute-start | bytes 122888 | tf_op jit(solution)/shard_map/ppermute | solution.py:510
  47.8 15.2 %all-to-all-start.2 = ((f32[8,72,128]{2,1,0:T(8,128)}), f32[8,72,128]{2,1,0:T(8,128)S(1)}, u32[]{:S(2)}, u32[]{:S(2)}) async-start(f32[8,72,128]{2,1,0:T(8,128)} %get-tuple-element.26), calls=%async_computation.2 | async-start | bytes 589824 | tf_op jit(solution)/shard_map/all_to_all | solution.py:475
  55.6 7.5 %collective-permute-start.1 = (f32[2,128]{1,0:T(2,128)S(1)}, f32[2,128]{1,0:T(2,128)S(1)}, u32[]{:S(2)}, u32[]{:S(2)}) collective-permute-start(f32[2,128]{1,0:T(2,128)S(1)} %get-tuple-element.31), channel_id=1, source_target_pairs={{8,16},{16,8},{9,17},{17,9},{10,18},{18,10},{11,19},{19,11},{12,20... | collective-permute-start | bytes 3080 | tf_op jit(solution)/shard_map/ppermute | solution.py:520

commit v7 on v6

--- a/solution.py
+++ b/solution.py
@@ -12,7 +12,6 @@
 NX, NZ, NC, NY, NH = 4, 8, 2, 4, 2
 ALL = ("x", "zl", "c", "y", "zh")
 PLANE = ("x", "c", "y")
-COLS = ("x", "c")
 F32 = jnp.float32
 I32 = jnp.int32
 BF16 = jnp.bfloat16
@@ -170,15 +169,19 @@
     return [field(obs_ref, 2 * half + yy, rel, kk, f) for yy in range(2) for rel in range(2)]
 
 
-def own(obs_ref, y, kk, f):
-    return [field(obs_ref, y, rel, kk, f) for rel in range(2)]
+def own(obs_ref, kk, f):
+    return [field(obs_ref, 0, rel, kk, f) for rel in range(2)]
+
+
+def loop_row(slot):
+    return (lax.axis_index("y") + NY - slot) % NY
 
 
 def edge_rows(flat):
     return jnp.concatenate([flat[0:1], flat[8:9], flat[7:8], flat[15:16]], axis=0)
 
 
-def sums_kernel(obs_ref, g0s_ref, ds_ref, g0f_ref, df_ref, hop_ref, plane_ref):
+def sums_kernel(obs_ref, expo_ref, g0s_ref, ds_ref, g0f_ref, df_ref, hop_ref, plane_ref):
     for ref in (g0s_ref, ds_ref, g0f_ref, df_ref):
         ref[...] = jnp.zeros(ref.shape, F32)
 
@@ -204,11 +207,10 @@
     ds_ref[...] = diag
     edges = edge_rows(g0f)
     hop_ref[...] = jnp.where(lax.axis_index("c") == 1, edges[2:4], edges[0:2])
-    for peer in range(NX * NC):
-        for y in range(NY):
-            plane_ref[peer, 16 * y : 16 * y + 16] = obs_ref[y, 160:176]
-        plane_ref[peer, 64:68] = edges
-        plane_ref[peer, 68:72] = jnp.zeros((4, LO), F32)
+    for peer in range(NX * NC * NY):
+        plane_ref[peer, 0:16] = expo_ref[...]
+        plane_ref[peer, 16:20] = edges
+        plane_ref[peer, 20:24] = jnp.zeros((4, LO), F32)
 
 
 def couple_kernel(obs_ref, g0s_ref, g0f_ref, cs_ref, cf_ref, ru_ref, fit_ref):
@@ -230,12 +232,10 @@
         return carry
 
     lax.fori_loop(0, 4, couple, 0)
-    y = lax.axis_index("y")
     total = jnp.zeros((HI, HALF), F32)
     for kk in range(2):
-        ids = Ids(own(obs_ref, y, kk, E), HALF, (0, 8))
-        at = pl.ds(pl.multiple_of((y % 2) * 2048, 2048), 2048)
-        fit = fit_ref[2 * kk + y // 2, :, at]
+        ids = Ids(own(obs_ref, kk, E), HALF, (0, 8))
+        fit = fit_ref[2 * kk, :, 0:2048]
         parts = split(row(fit, STAR) + row(fit, FLAT), FEW)
         (added,) = scatter([[across(part, 0) for part in parts]], ids.bf, ids.hot())
         total += added
@@ -264,12 +264,12 @@
     obs_ref, expo_ref, g0f_ref, cf_ref, df_ref, hop_ref,
     fit_ref, cf_out, yf_out, g0z_out, dz_out,
 ):
-    part = expo_ref[0, 0:64]
-    for xc in range(1, 8):
-        part = part + expo_ref[xc, 0:64]
-    for y in range(4):
-        diag = part[16 * y : 16 * y + 16, HALF:] + RIDGE
-        g0z_out[y] = part[16 * y : 16 * y + 16, :HALF] / diag
+    for y in range(NY):
+        part = expo_ref[y, 0:16]
+        for xc in range(1, NX * NC):
+            part = part + expo_ref[NY * xc + y, 0:16]
+        diag = part[:, HALF:] + RIDGE
+        g0z_out[y] = part[:, :HALF] / diag
         dz_out[y] = diag
     cf_out[...] = cf_ref[...]
 
@@ -278,7 +278,7 @@
         hot = expo.hot()
         found = [
             gather(
-                g0z_out[2 * (step % 2) + yy],
+                g0z_out[loop_row(2 * (step % 2) + yy)],
                 expo.full[16 * yy : 16 * yy + 16],
                 hot[:, 2048 * yy : 2048 * (yy + 1)],
             )
@@ -293,7 +293,7 @@
 
     lax.fori_loop(0, 4, apply, 0)
     x, c = lax.axis_index("x"), lax.axis_index("c")
-    chip = expo_ref[2 * x + 1 - c, 64:68]
+    chip = expo_ref[8 * x + 4 * (1 - c) + lax.axis_index("y"), 16:20]
     above = jnp.where(c == 1, chip[2:4], hop_ref[...])
     below = jnp.where(c == 1, hop_ref[...], chip[0:2])
     cf = cf_out[...] - SMOOTH * beside(g0f_ref[...], above, below)
@@ -338,14 +338,13 @@
         rho += fold8(g0s * g0s * ds)
         beta += fold8(g0s * cs)
         eta += fold8(cs * ys)
-    y = lax.axis_index("y")
     total = jnp.zeros((HI, HALF), F32)
     cross = jnp.zeros((1, LO), F32)
     yf = yf_ref[...]
     for kk in range(2):
-        star, flat = Ids(own(obs_ref, y, kk, S), LO), Ids(own(obs_ref, y, kk, PX), LO)
-        expo = Ids(own(obs_ref, y, kk, E), HALF, (0, 8))
-        w = joined(rows_of(own(obs_ref, y, kk, W)))
+        star, flat = Ids(own(obs_ref, kk, S), LO), Ids(own(obs_ref, kk, PX), LO)
+        expo = Ids(own(obs_ref, kk, E), HALF, (0, 8))
+        w = joined(rows_of(own(obs_ref, kk, W)))
         both = gather_both((ys_ref[kk], star.full, star.hot()), (yf, flat.full, flat.hot()))
         from_star, from_flat = row(both, STAR), row(both, FLAT)
         parts = split(w * (from_star + from_flat), FEW)
@@ -475,10 +474,6 @@
     return lax.all_to_all(blocks, axes, 0, 0, tiled=True)
 
 
-def to_all(block, peers, axes):
-    return exchange(jnp.broadcast_to(block[None], (peers, *block.shape)), axes)
-
-
 def hop_pairs():
     def place(tile, y, zh):
         x, rest = divmod(tile, NZ * NC)
@@ -509,14 +504,15 @@
     )
     partner = lax.ppermute(obs, "zh", [(0, 1), (1, 0)])
     expo = exchange(expo, ("zl", "zh"))
+    both = jnp.concatenate([obs, partner], axis=0)
+    turned = [lax.ppermute(both, "y", [(i, (i + k) % NY) for i in range(NY)]) for k in range(1, NY)]
+    tile_obs = jnp.stack([both, *turned])
     expo = expo.reshape(NZ, NH, 8, LO).sum(axis=0)
     expo = jnp.where(zh == 0, expo, expo[::-1]).reshape(HI, LO)
-    tile_obs = jnp.concatenate([obs, partner, expo], axis=0)
-    tile_obs = to_all(lax.optimization_barrier(tile_obs), NY, "y")
     g0s, ds, g0f, df, hop_row, plane = call(
-        sums_kernel, [stars] * 2 + [flats] * 2 + [(2, LO), (8, 72, LO)], (tile_obs,), mib=16, work=29
-    )
-    expo = exchange(plane, COLS)
+        sums_kernel, [stars] * 2 + [flats] * 2 + [(2, LO), (32, 24, LO)], (tile_obs, expo), mib=16, work=29
+    )
+    expo = exchange(plane, PLANE)
     by_hop = lax.ppermute(hop_row, ALL, hop)
     cs, cf, ru = call(
         couple_kernel, [stars, flats, (HI, HALF)], (tile_obs, g0s, g0f),

time: 109 us -> 116 us (1.064)
  starting transfers between devices: 38 us -> 49 us
  blocking collectives: 48.9 us -> 38.2 us
  waiting for transfers between devices: 2.84 us -> 9.33 us
    all_to_all x3 -> x2, blocking collectives: 48.9 us -> 38.2 us  [exchange(): return lax.all_to_all(blocks, axes, 0, 0, tiled=True)]
    ppermute x0 -> x3, starting transfers between devices: none -> 9.49 us  [on_device(): lax.ppermute(both, 'y', [(i, (i + k) % NY) for i in range(NY)])]
    ppermute x0 -> x3, waiting for transfers between devices: none -> 4.12 us  [on_device(): lax.ppermute(both, 'y', [(i, (i + k) % NY) for i in range(NY)])]
    all_to_all x2, waiting for transfers between devices: 0.11 us -> 2.36 us  [exchange(): return lax.all_to_all(blocks, axes, 0, 0, tiled=True)]
    all_to_all x2, starting transfers between devices: 23.5 us -> 24.7 us  [exchange(): return lax.all_to_all(blocks, axes, 0, 0, tiled=True)]
  transfers between devices with their start and end apart: 4 -> 7, of which waited for: 2 -> 4; matrix products, arithmetic and copies ran while one was open for 0% -> 0% of each run, Pallas kernels for 5% -> 4%
where the time goes in v7:
time: 116 us; the launch traced here: 115 us
  starting transfers between devices  49 us (42%)
  blocking collectives  38.2 us (33%)
  Pallas kernels  17.8 us (15%)
  waiting for transfers between devices  9.33 us (8%)
    all_to_all x2, blocking collectives, exchange(): return lax.all_to_all(blocks, axes, 0, 0, tiled=True)  38.2 us
    all_to_all x2, starting transfers between devices, exchange(): return lax.all_to_all(blocks, axes, 0, 0, tiled=True)  24.7 us
    pallas_call x7, Pallas kernels, call(): pl.pallas_call(kernel, out_shape=tuple(out) if many else out[0], in_specs...  17.8 us
    ppermute x1, starting transfers between devices, on_device(): partner = lax.ppermute(obs, 'zh', [(0, 1), (1, 0)])  12 us
    ppermute x3, starting transfers between devices, on_device(): lax.ppermute(both, 'y', [(i, (i + k) % NY) for i in range(NY)])  9.49 us
    ppermute x3, waiting for transfers between devices, on_device(): lax.ppermute(both, 'y', [(i, (i + k) % NY) for i in range(NY)])  4.12 us
    ppermute x1, waiting for transfers between devices, on_device(): partner = lax.ppermute(obs, 'zh', [(0, 1), (1, 0)])  2.85 us
    ppermute x1, starting transfers between devices, on_device(): by_hop = lax.ppermute(hop_row, ALL, hop)  2.81 us
  transfers between devices with their start and end apart: 7, of which 4 were waited for; matrix products, arithmetic and copies ran while one was open for 0% of the time, Pallas kernels for 4%

profile of v7, /device:TPU:1, one launch (start us, length us, event | category | flops | bytes accessed | tf_op | source)
XLA Modules:
  0.0 115.2 jit_solution(12245239925574522946)
XLA Ops:
  0.6 2.5 %shard_map.85 = (f32[80,128]{1,0:T(8,128)}, f32[16,8,128]{2,1,0:T(8,128)}) custom-call(s32[1,16]{1,0:T(1,128)} %block_ref.1, s32[16,128]{1,0:T(8,128)} %bitcast.19, s32[16,128]{1,0:T(8,128)} %bitcast.20, s32[16,128]{1,0:T(8,128)} %bitcast.21, f32[16,128]{1,0:T(8,128)} %bitcast.22, f32[16,128]{1,0:T(8,128)} %bitcast.23), custom_call_target="tpu_custom_call" | custom-call | flops 1048576 | bytes 1048576 | tf_op jit(solution)/shard_map/pallas_call | solution.py:462
  3.1 0.0 copy-start
  3.1 15.7 %all-to-all-start = ((f32[16,8,128]{2,1,0:T(8,128)}), f32[16,8,128]{2,1,0:T(8,128)S(1)}, u32[]{:S(2)}, u32[]{:S(2)}) async-start(f32[16,8,128]{2,1,0:T(8,128)} %get-tuple-element.25), calls=%async_computation | async-start | bytes 131072 | tf_op jit(solution)/shard_map/all_to_all | solution.py:474
  18.9 0.0 copy-done
  18.9 12.0 %collective-permute-start = (f32[80,128]{1,0:T(8,128)S(1)}, f32[80,128]{1,0:T(8,128)S(1)}, u32[]{:S(2)}, u32[]{:S(2)}) collective-permute-start(f32[80,128]{1,0:T(8,128)S(1)} %copy-done), channel_id=1, source_target_pairs={{0,1},{1,0},{2,3},{3,2},{4,5},{5,4},{6,7},{7,6},{8,9},{9,8},{10,11... | collective-permute-start | bytes 122888 | tf_op jit(solution)/shard_map/ppermute | solution.py:505
  30.9 2.9 %collective-permute-done = f32[80,128]{1,0:T(8,128)S(1)} collective-permute-done((f32[80,128]{1,0:T(8,128)S(1)}, f32[80,128]{1,0:T(8,128)S(1)}, u32[]{:S(2)}, u32[]{:S(2)}) %collective-permute-start) | collective-permute-done | bytes 40992 | tf_op jit(solution)/shard_map/ppermute | solution.py:505
  33.7 4.6 %collective-permute-start.3 = (f32[160,128]{1,0:T(8,128)S(1)}, f32[160,128]{1,0:T(8,128)S(1)}, u32[]{:S(2)}, u32[]{:S(2)}) collective-permute-start(f32[160,128]{1,0:T(8,128)S(1)} %constant_dynamic-update-slice_fusion), channel_id=1, source_target_pairs={{0,6},{2,0},{4,2},{6,4},{1,7},{3,1},{5,3},{7,5},{8,14},{10,8},{12,... | collective-permute-start | bytes 245768 | tf_op jit(solution)/shard_map/ppermute | solution.py:508
  38.4 2.3 %collective-permute-start.2 = (f32[160,128]{1,0:T(8,128)S(1)}, f32[160,128]{1,0:T(8,128)S(1)}, u32[]{:S(2)}, u32[]{:S(2)}) collective-permute-start(f32[160,128]{1,0:T(8,128)S(1)} %constant_dynamic-update-slice_fusion), channel_id=1, source_target_pairs={{0,4},{2,6},{4,0},{6,2},{1,5},{3,7},{5,1},{7,3},{8,12},{10,14},{12... | collective-permute-start | bytes 245768 | tf_op jit(solution)/shard_map/ppermute | solution.py:508
  40.6 2.6 %collective-permute-start.1 = (f32[160,128]{1,0:T(8,128)S(1)}, f32[160,128]{1,0:T(8,128)S(1)}, u32[]{:S(2)}, u32[]{:S(2)}) collective-permute-start(f32[160,128]{1,0:T(8,128)S(1)} %constant_dynamic-update-slice_fusion), channel_id=1, source_target_pairs={{0,2},{2,4},{4,6},{6,0},{1,3},{3,5},{5,7},{7,1},{8,10},{10,12},{12... | collective-permute-start | bytes 245768 | tf_op jit(solution)/shard_map/ppermute | solution.py:508
  43.2 0.0 collective-permute-done.3
  43.3 1.8 %collective-permute-done.2 = f32[160,128]{1,0:T(8,128)S(1)} collective-permute-done((f32[160,128]{1,0:T(8,128)S(1)}, f32[160,128]{1,0:T(8,128)S(1)}, u32[]{:S(2)}, u32[]{:S(2)}) %collective-permute-start.2) | collective-permute-done | bytes 81952 | tf_op jit(solution)/shard_map/ppermute | solution.py:508
  45.1 2.3 %collective-permute-done.1 = f32[160,128]{1,0:T(8,128)S(1)} collective-permute-done((f32[160,128]{1,0:T(8,128)S(1)}, f32[160,128]{1,0:T(8,128)S(1)}, u32[]{:S(2)}, u32[]{:S(2)}) %collective-permute-start.1) | collective-permute-done | bytes 81952 | tf_op jit(solution)/shard_map/ppermute | solution.py:508
  47.4 0.0 all-to-all-done
  47.4 4.1 %shard_map.86 = (f32[2,16,128]{2,1,0:T(8,128)S(1)}, f32[2,16,128]{2,1,0:T(8,128)S(1)}, f32[16,128]{1,0:T(8,128)S(1)}, f32[16,128]{1,0:T(8,128)S(1)}, f32[2,128]{1,0:T(2,128)S(1)}, /*index=5*/f32[32,24,128]{2,1,0:T(8,128)}) custom-call(f32[4,160,128]{2,1,0:T(8,128)S(1)} %pad_maximum_fusion.obs_ref, f32[16,128]{1,0:T(8,128)S(1)} %fusion.expo_ref), custom_call_target="tpu_custom_call" | custom-call | flops 536870912 | bytes 1048576 | tf_op jit(solution)/shard_map/pallas_call | solution.py:462
  51.5 9.0 %all-to-all-start.1 = ((f32[32,24,128]{2,1,0:T(8,128)}), f32[32,24,128]{2,1,0:T(8,128)S(1)}, u32[]{:S(2)}, u32[]{:S(2)}) async-start(f32[32,24,128]{2,1,0:T(8,128)} %get-tuple-element.26), calls=%async_computation.1 | async-start | bytes 786432 | tf_op jit(solution)/shard_map/all_to_all | solution.py:474
  60.5 2.8 %collective-permute-start.4 = (f32[2,128]{1,0:T(2,128)S(1)}, f32[2,128]{1,0:T(2,128)S(1)}, u32[]{:S(2)}, u32[]{:S(2)}) collective-permute-start(f32[2,128]{1,0:T(2,128)S(1)} %get-tuple-element.31), channel_id=1, source_target_pairs={{8,16},{16,8},{9,17},{17,9},{10,18},{18,10},{11,19},{19,11},{12,20... | collective-permute-start | bytes 3080 | tf_op jit(solution)/shard_map/ppermute | solution.py:516
  63.3 4.9 %shard_map.87 = (f32[2,16,128]{2,1,0:T(8,128)S(1)}, f32[16,128]{1,0:T(8,128)S(1)}, f32[16,64]{1,0:T(8,128)S(1)}) custom-call(f32[4,160,128]{2,1,0:T(8,128)S(1)} %pad_maximum_fusion.obs_ref, f32[2,16,128]{2,1,0:T(8,128)S(1)} %get-tuple-element.28.g0s_ref, f32[16,128]{1,0:T(8,128)S(1)} %get-tuple-element.27.g0f_ref), custom_call_target="tpu_custom_call" | custom-call | flops 1073741824 | bytes 1048576 | tf_op jit(solution)/shard_map/pallas_call | solution.py:462
  68.2 0.0 collective-permute-done.4.hop_ref
  68.2 2.4 %all-to-all-done.1.expo_ref = f32[32,24,128]{2,1,0:T(8,128)S(1)} async-done(((f32[32,24,128]{2,1,0:T(8,128)}), f32[32,24,128]{2,1,0:T(8,128)S(1)}, u32[]{:S(2)}, u32[]{:S(2)}) %all-to-all-start.1) | async-done | bytes 393248 | tf_op jit(solution)/shard_map/all_to_all | solution.py:474
  70.6 2.6 %shard_map.88 = (f32[4,8,4096]{2,1,0:T(8,128)S(1)}, f32[16,128]{1,0:T(8,128)S(1)}, f32[16,128]{1,0:T(8,128)S(1)}, f32[4,16,64]{2,1,0:T(8,128)S(1)}, f32[4,16,64]{2,1,0:T(8,128)S(1)}) custom-call(f32[4,160,128]{2,1,0:T(8,128)S(1)} %pad_maximum_fusion.obs_ref, f32[32,24,128]{2,1,0:T(8,128)S(1)} %all-to-all-done.1.expo_ref, ...), custom_call_target="tpu_custom_call" | custom-call | flops 1073741824 | bytes 1048576 | tf_op jit(solution)/shard_map/pallas_call | solution.py:462
  73.2 2.8 %shard_map.89 = (f32[2,16,128]{2,1,0:T(8,128)S(1)}, f32[16,16,128]{2,1,0:T(8,128)S(1)}) custom-call(f32[4,160,128]{2,1,0:T(8,128)S(1)} %pad_maximum_fusion.obs_ref, f32[4,8,4096]{2,1,0:T(8,128)S(1)} %get-tuple-element.32.fit_ref, f32[2,16,128]{2,1,0:T(8,128)S(1)} %get-tuple-element.28.g0s_ref, f32[2,16,128]{2,1,0:T(8,128)S(1)} %get-tuple-element.33.ds_ref, ...), custom_call_target="tpu_custom_call" | custom-call | flops 1073741824 | bytes 1048576 | tf_op jit(solution)/shard_map/pallas_call | solution.py:462
  76.0 22.8 %all_to_all.20.parts_ref = f32[16,16,128]{2,1,0:T(8,128)S(1)} all-to-all(f32[16,16,128]{2,1,0:T(8,128)S(1)} %get-tuple-element.38), channel_id=1, replica_groups=mesh['x'=4,'zl'=8,'c'=2,'y'=4,'zh'=2] {'zl','c'}, dimensions={0} | all-to-all | bytes 262144 | tf_op jit(solution)/shard_map/all_to_all | solution.py:474
  98.8 15.4 %all_to_all.21.sums_ref = f32[32,16,128]{2,1,0:T(8,128)S(1)} all-to-all(f32[32,16,128]{2,1,0:T(8,128)S(1)} %shard_map.90), channel_id=1, replica_groups=mesh['x'=4,'zl'=8,'c'=2,'y'=4,'zh'=2] {'x','c','y'}, dimensions={0} | all-to-all | bytes 524288 | tf_op jit(solution)/shard_map/all_to_all | solution.py:474
  114.2 1.0 shard_map.91
  (6 shorter events, 0.1 us)
Async XLA Ops:
  3.1 15.8 %copy-start = (f32[80,128]{1,0:T(8,128)S(1)}, f32[80,128]{1,0:T(8,128)}, u32[]{:S(2)}) copy-start(f32[80,128]{1,0:T(8,128)} %get-tuple-element.24) | copy-start | bytes 122884
  3.1 44.3 %all-to-all-start = ((f32[16,8,128]{2,1,0:T(8,128)}), f32[16,8,128]{2,1,0:T(8,128)S(1)}, u32[]{:S(2)}, u32[]{:S(2)}) async-start(f32[16,8,128]{2,1,0:T(8,128)} %get-tuple-element.25), calls=%async_computation | async-start | bytes 131072 | tf_op jit(solution)/shard_map/all_to_all | solution.py:474
  18.9 14.9 %collective-permute-start = (f32[80,128]{1,0:T(8,128)S(1)}, f32[80,128]{1,0:T(8,128)S(1)}, u32[]{:S(2)}, u32[]{:S(2)}) collective-permute-start(f32[80,128]{1,0:T(8,128)S(1)} %copy-done), channel_id=1, source_target_pairs={{0,1},{1,0},{2,3},{3,2},{4,5},{5,4},{6,7},{7,6},{8,9},{9,8},{10,11... | collective-permute-start | bytes 122888 | tf_op jit(solution)/shard_map/ppermute | solution.py:505
  33.7 9.5 %collective-permute-start.3 = (f32[160,128]{1,0:T(8,128)S(1)}, f32[160,128]{1,0:T(8,128)S(1)}, u32[]{:S(2)}, u32[]{:S(2)}) collective-permute-start(f32[160,128]{1,0:T(8,128)S(1)} %constant_dynamic-update-slice_fusion), channel_id=1, source_target_pairs={{0,6},{2,0},{4,2},{6,4},{1,7},{3,1},{5,3},{7,5},{8,14},{10,8},{12,... | collective-permute-start | bytes 245768 | tf_op jit(solution)/shard_map/ppermute | solution.py:508
  38.4 6.7 %collective-permute-start.2 = (f32[160,128]{1,0:T(8,128)S(1)}, f32[160,128]{1,0:T(8,128)S(1)}, u32[]{:S(2)}, u32[]{:S(2)}) collective-permute-start(f32[160,128]{1,0:T(8,128)S(1)} %constant_dynamic-update-slice_fusion), channel_id=1, source_target_pairs={{0,4},{2,6},{4,0},{6,2},{1,5},{3,7},{5,1},{7,3},{8,12},{10,14},{12... | collective-permute-start | bytes 245768 | tf_op jit(solution)/shard_map/ppermute | solution.py:508
  40.6 6.7 %collective-permute-start.1 = (f32[160,128]{1,0:T(8,128)S(1)}, f32[160,128]{1,0:T(8,128)S(1)}, u32[]{:S(2)}, u32[]{:S(2)}) collective-permute-start(f32[160,128]{1,0:T(8,128)S(1)} %constant_dynamic-update-slice_fusion), channel_id=1, source_target_pairs={{0,2},{2,4},{4,6},{6,0},{1,3},{3,5},{5,7},{7,1},{8,10},{10,12},{12... | collective-permute-start | bytes 245768 | tf_op jit(solution)/shard_map/ppermute | solution.py:508
  51.5 19.1 %all-to-all-start.1 = ((f32[32,24,128]{2,1,0:T(8,128)}), f32[32,24,128]{2,1,0:T(8,128)S(1)}, u32[]{:S(2)}, u32[]{:S(2)}) async-start(f32[32,24,128]{2,1,0:T(8,128)} %get-tuple-element.26), calls=%async_computation.1 | async-start | bytes 786432 | tf_op jit(solution)/shard_map/all_to_all | solution.py:474
  60.5 7.7 %collective-permute-start.4 = (f32[2,128]{1,0:T(2,128)S(1)}, f32[2,128]{1,0:T(2,128)S(1)}, u32[]{:S(2)}, u32[]{:S(2)}) collective-permute-start(f32[2,128]{1,0:T(2,128)S(1)} %get-tuple-element.31), channel_id=1, source_target_pairs={{8,16},{16,8},{9,17},{17,9},{10,18},{18,10},{11,19},{19,11},{12,20... | collective-permute-start | bytes 3080 | tf_op jit(solution)/shard_map/ppermute | solution.py:516

commit v8 on v7

--- a/solution.py
+++ b/solution.py
@@ -317,7 +317,7 @@
 
 
 def last_kernel(
-    obs_ref, fit_ref, g0s_ref, ds_ref, cs_in, g0f_ref, df_ref, cf_ref, yf_ref, ru_ref, ys_ref, out_ref, cs_ref
+    obs_ref, fit_ref, g0s_ref, ds_ref, cs_in, g0f_ref, df_ref, cf_ref, yf_ref, ru_ref, ys_ref, keep_ref, send_ref, cs_ref
 ):
     cs_ref[...] = cs_in[...]
 
@@ -359,10 +359,11 @@
     eta = 0.25 * (eta + fold8(cf * yf))
     delta = 2.0 * cross - (0.25 * SMOOTH) * fold8(yf * beside(yf, none, none))
     scal = jnp.concatenate([rho, beta, eta, delta, edge_rows(yf)], axis=0)
-    for zl in range(NZ):
-        for c in range(NC):
-            out_ref[NC * zl + c, 0:8] = expos[8 * c : 8 * c + 8]
-            out_ref[NC * zl + c, 8:16] = scal
+    odd = lax.axis_index("c") == 1
+    keep_ref[0:8] = jnp.where(odd, expos[8:16], expos[0:8])
+    send_ref[0:8] = jnp.where(odd, expos[0:8], expos[8:16])
+    keep_ref[8:16] = scal
+    send_ref[8:16] = scal
 
 
 def edge_dot(last, first):
@@ -370,15 +371,27 @@
     return -(0.5 * SMOOTH) * (both[0:1] + both[1:2])
 
 
+def chip_kernel(keep_ref, got_ref, out_ref):
+    odd = lax.axis_index("c") == 1
+    keep, got = keep_ref[...], got_ref[...]
+    upper, lower = jnp.where(odd, got, keep), jnp.where(odd, keep, got)
+    scal = keep[8:12] + got[8:12]
+    scal = scal + jnp.where(row_iota((4, LO)) == 3, edge_dot(upper[14:16], lower[12:14]), 0.0)
+    scal = jnp.concatenate([scal, upper[12:14], lower[14:16]], axis=0)
+    for peer in range(NZ):
+        out_ref[peer, 0:8] = keep[0:8] + got[0:8]
+        out_ref[peer, 8:16] = scal
+
+
 def column_kernel(parts_ref, out_ref):
     total = parts_ref[0]
-    for peer in range(1, NZ * NC):
+    for peer in range(1, NZ):
         total = total + parts_ref[peer]
     between = edge_dot(parts_ref[0, 14:16], parts_ref[1, 12:14])
-    for peer in range(1, NZ * NC - 1):
+    for peer in range(1, NZ - 1):
         between += edge_dot(parts_ref[peer, 14:16], parts_ref[peer + 1, 12:14])
     scal = total[8:12] + jnp.where(row_iota((4, LO)) == 3, between, 0.0)
-    ends = jnp.concatenate([scal, parts_ref[0, 12:14], parts_ref[NZ * NC - 1, 14:16]], axis=0)
+    ends = jnp.concatenate([scal, parts_ref[0, 12:14], parts_ref[NZ - 1, 14:16]], axis=0)
     for peer in range(NX * NC * NY):
         out_ref[peer, 0:8] = total[0:8]
         out_ref[peer, 8:16] = ends
@@ -522,12 +535,13 @@
         expo_apply_kernel, [(4, 8, 4096)] + [flats] * 2 + [expos] * 2,
         (tile_obs, expo, g0f, cf, df, by_hop), mib=16, work=30,
     )
-    ys, payload = call(
-        last_kernel, [stars, (16, 16, LO)],
+    ys, keep, send = call(
+        last_kernel, [stars, (16, LO), (16, LO)],
         (tile_obs, fit, g0s, ds, cs, g0f, df, cf, yf, ru),
         scratch=[pltpu.VMEM(stars, F32)], mib=16, work=30,
     )
-    payload = exchange(payload, ("zl", "c"))
+    got = lax.ppermute(send, "c", [(0, 1), (1, 0)])
+    payload = exchange(call(chip_kernel, [(NZ, 16, LO)], (keep, got)), "zl")
     sums = exchange(call(column_kernel, [(32, 16, LO)], (payload,)), PLANE)
     star, zero, flat = call(
         finish_kernel, [(4, LO), (4, LO), (8, 2 * LO)], (sums, g0z, dz, g0s, ys, g0f, yf)

time: 116 us -> 118 us (1.017)
  starting transfers between devices: 49 us -> 51.6 us
  blocking collectives: 38.2 us -> 36.5 us
    ppermute x0 -> x1, starting transfers between devices: none -> 2.59 us  [on_device(): got = lax.ppermute(send, 'c', [(0, 1), (1, 0)])]
    all_to_all x2, blocking collectives: 38.2 us -> 36.5 us  [exchange(): return lax.all_to_all(blocks, axes, 0, 0, tiled=True)]
    pallas_call x7 -> x8, Pallas kernels: 17.8 us -> 17.8 us  [call(): pl.pallas_call(kernel, out_shape=tuple(out) if many else out[0], in_specs...]
  transfers between devices with their start and end apart: 7 -> 8, of which waited for: 4 -> 5; matrix products, arithmetic and copies ran while one was open for 0% -> 0% of each run, Pallas kernels for 4% -> 4%
where the time goes in v8:
time: 118 us; the launch traced here: 117 us
  starting transfers between devices  51.6 us (44%)
  blocking collectives  36.5 us (31%)
  Pallas kernels  17.8 us (15%)
  waiting for transfers between devices  10.1 us (9%)
    all_to_all x2, blocking collectives, exchange(): return lax.all_to_all(blocks, axes, 0, 0, tiled=True)  36.5 us
    all_to_all x2, starting transfers between devices, exchange(): return lax.all_to_all(blocks, axes, 0, 0, tiled=True)  24.7 us
    pallas_call x8, Pallas kernels, call(): pl.pallas_call(kernel, out_shape=tuple(out) if many else out[0], in_specs...  17.8 us
    ppermute x1, starting transfers between devices, on_device(): partner = lax.ppermute(obs, 'zh', [(0, 1), (1, 0)])  12 us
    ppermute x3, starting transfers between devices, on_device(): lax.ppermute(both, 'y', [(i, (i + k) % NY) for i in range(NY)])  9.49 us
    ppermute x3, waiting for transfers between devices, on_device(): lax.ppermute(both, 'y', [(i, (i + k) % NY) for i in range(NY)])  4.12 us
    ppermute x1, waiting for transfers between devices, on_device(): partner = lax.ppermute(obs, 'zh', [(0, 1), (1, 0)])  2.85 us
    ppermute x1, starting transfers between devices, on_device(): by_hop = lax.ppermute(hop_row, ALL, hop)  2.8 us
  transfers between devices with their start and end apart: 8, of which 5 were waited for; matrix products, arithmetic and copies ran while one was open for 0% of the time, Pallas kernels for 4%

profile of v8, /device:TPU:1, one launch (start us, length us, event | category | flops | bytes accessed | tf_op | source)
XLA Modules:
  0.0 116.9 jit_solution(15273423842854435418)
XLA Ops:
  0.6 2.4 %shard_map.85 = (f32[80,128]{1,0:T(8,128)}, f32[16,8,128]{2,1,0:T(8,128)}) custom-call(s32[1,16]{1,0:T(1,128)} %block_ref.1, s32[16,128]{1,0:T(8,128)} %bitcast.19, s32[16,128]{1,0:T(8,128)} %bitcast.20, s32[16,128]{1,0:T(8,128)} %bitcast.21, f32[16,128]{1,0:T(8,128)} %bitcast.22, f32[16,128]{1,0:T(8,128)} %bitcast.23), custom_call_target="tpu_custom_call" | custom-call | flops 1048576 | bytes 1048576 | tf_op jit(solution)/shard_map/pallas_call | solution.py:475
  3.1 15.7 %all-to-all-start = ((f32[16,8,128]{2,1,0:T(8,128)}), f32[16,8,128]{2,1,0:T(8,128)S(1)}, u32[]{:S(2)}, u32[]{:S(2)}) async-start(f32[16,8,128]{2,1,0:T(8,128)} %get-tuple-element.26), calls=%async_computation | async-start | bytes 131072 | tf_op jit(solution)/shard_map/all_to_all | solution.py:487
  18.9 12.0 %collective-permute-start = (f32[80,128]{1,0:T(8,128)S(1)}, f32[80,128]{1,0:T(8,128)S(1)}, u32[]{:S(2)}, u32[]{:S(2)}) collective-permute-start(f32[80,128]{1,0:T(8,128)S(1)} %copy-done), channel_id=1, source_target_pairs={{0,1},{1,0},{2,3},{3,2},{4,5},{5,4},{6,7},{7,6},{8,9},{9,8},{10,11... | collective-permute-start | bytes 122888 | tf_op jit(solution)/shard_map/ppermute | solution.py:518
  30.9 2.9 %collective-permute-done = f32[80,128]{1,0:T(8,128)S(1)} collective-permute-done((f32[80,128]{1,0:T(8,128)S(1)}, f32[80,128]{1,0:T(8,128)S(1)}, u32[]{:S(2)}, u32[]{:S(2)}) %collective-permute-start) | collective-permute-done | bytes 40992 | tf_op jit(solution)/shard_map/ppermute | solution.py:518
  33.7 4.6 %collective-permute-start.3 = (f32[160,128]{1,0:T(8,128)S(1)}, f32[160,128]{1,0:T(8,128)S(1)}, u32[]{:S(2)}, u32[]{:S(2)}) collective-permute-start(f32[160,128]{1,0:T(8,128)S(1)} %constant_dynamic-update-slice_fusion), channel_id=1, source_target_pairs={{0,6},{2,0},{4,2},{6,4},{1,7},{3,1},{5,3},{7,5},{8,14},{10,8},{12,... | collective-permute-start | bytes 245768 | tf_op jit(solution)/shard_map/ppermute | solution.py:521
  38.4 2.3 %collective-permute-start.2 = (f32[160,128]{1,0:T(8,128)S(1)}, f32[160,128]{1,0:T(8,128)S(1)}, u32[]{:S(2)}, u32[]{:S(2)}) collective-permute-start(f32[160,128]{1,0:T(8,128)S(1)} %constant_dynamic-update-slice_fusion), channel_id=1, source_target_pairs={{0,4},{2,6},{4,0},{6,2},{1,5},{3,7},{5,1},{7,3},{8,12},{10,14},{12... | collective-permute-start | bytes 245768 | tf_op jit(solution)/shard_map/ppermute | solution.py:521
  40.6 2.6 %collective-permute-start.1 = (f32[160,128]{1,0:T(8,128)S(1)}, f32[160,128]{1,0:T(8,128)S(1)}, u32[]{:S(2)}, u32[]{:S(2)}) collective-permute-start(f32[160,128]{1,0:T(8,128)S(1)} %constant_dynamic-update-slice_fusion), channel_id=1, source_target_pairs={{0,2},{2,4},{4,6},{6,0},{1,3},{3,5},{5,7},{7,1},{8,10},{10,12},{12... | collective-permute-start | bytes 245768 | tf_op jit(solution)/shard_map/ppermute | solution.py:521
  43.2 0.0 collective-permute-done.3
  43.2 1.8 %collective-permute-done.2 = f32[160,128]{1,0:T(8,128)S(1)} collective-permute-done((f32[160,128]{1,0:T(8,128)S(1)}, f32[160,128]{1,0:T(8,128)S(1)}, u32[]{:S(2)}, u32[]{:S(2)}) %collective-permute-start.2) | collective-permute-done | bytes 81952 | tf_op jit(solution)/shard_map/ppermute | solution.py:521
  45.0 2.3 %collective-permute-done.1 = f32[160,128]{1,0:T(8,128)S(1)} collective-permute-done((f32[160,128]{1,0:T(8,128)S(1)}, f32[160,128]{1,0:T(8,128)S(1)}, u32[]{:S(2)}, u32[]{:S(2)}) %collective-permute-start.1) | collective-permute-done | bytes 81952 | tf_op jit(solution)/shard_map/ppermute | solution.py:521
  47.4 0.0 all-to-all-done
  47.4 4.1 %shard_map.86 = (f32[2,16,128]{2,1,0:T(8,128)S(1)}, f32[2,16,128]{2,1,0:T(8,128)S(1)}, f32[16,128]{1,0:T(8,128)S(1)}, f32[16,128]{1,0:T(8,128)S(1)}, f32[2,128]{1,0:T(2,128)S(1)}, /*index=5*/f32[32,24,128]{2,1,0:T(8,128)}) custom-call(f32[4,160,128]{2,1,0:T(8,128)S(1)} %pad_maximum_fusion.obs_ref, f32[16,128]{1,0:T(8,128)S(1)} %fusion.expo_ref), custom_call_target="tpu_custom_call" | custom-call | flops 536870912 | bytes 1048576 | tf_op jit(solution)/shard_map/pallas_call | solution.py:475
  51.5 9.0 %all-to-all-start.1 = ((f32[32,24,128]{2,1,0:T(8,128)}), f32[32,24,128]{2,1,0:T(8,128)S(1)}, u32[]{:S(2)}, u32[]{:S(2)}) async-start(f32[32,24,128]{2,1,0:T(8,128)} %get-tuple-element.27), calls=%async_computation.1 | async-start | bytes 786432 | tf_op jit(solution)/shard_map/all_to_all | solution.py:487
  60.5 2.8 %collective-permute-start.4 = (f32[2,128]{1,0:T(2,128)S(1)}, f32[2,128]{1,0:T(2,128)S(1)}, u32[]{:S(2)}, u32[]{:S(2)}) collective-permute-start(f32[2,128]{1,0:T(2,128)S(1)} %get-tuple-element.32), channel_id=1, source_target_pairs={{8,16},{16,8},{9,17},{17,9},{10,18},{18,10},{11,19},{19,11},{12,20... | collective-permute-start | bytes 3080 | tf_op jit(solution)/shard_map/ppermute | solution.py:529
  63.3 4.9 %shard_map.87 = (f32[2,16,128]{2,1,0:T(8,128)S(1)}, f32[16,128]{1,0:T(8,128)S(1)}, f32[16,64]{1,0:T(8,128)S(1)}) custom-call(f32[4,160,128]{2,1,0:T(8,128)S(1)} %pad_maximum_fusion.obs_ref, f32[2,16,128]{2,1,0:T(8,128)S(1)} %get-tuple-element.29.g0s_ref, f32[16,128]{1,0:T(8,128)S(1)} %get-tuple-element.28.g0f_ref), custom_call_target="tpu_custom_call" | custom-call | flops 1073741824 | bytes 1048576 | tf_op jit(solution)/shard_map/pallas_call | solution.py:475
  68.2 0.0 collective-permute-done.4.hop_ref
  68.2 2.4 %all-to-all-done.1.expo_ref = f32[32,24,128]{2,1,0:T(8,128)S(1)} async-done(((f32[32,24,128]{2,1,0:T(8,128)}), f32[32,24,128]{2,1,0:T(8,128)S(1)}, u32[]{:S(2)}, u32[]{:S(2)}) %all-to-all-start.1) | async-done | bytes 393248 | tf_op jit(solution)/shard_map/all_to_all | solution.py:487
  70.6 2.6 %shard_map.88 = (f32[4,8,4096]{2,1,0:T(8,128)S(1)}, f32[16,128]{1,0:T(8,128)S(1)}, f32[16,128]{1,0:T(8,128)S(1)}, f32[4,16,64]{2,1,0:T(8,128)S(1)}, f32[4,16,64]{2,1,0:T(8,128)S(1)}) custom-call(f32[4,160,128]{2,1,0:T(8,128)S(1)} %pad_maximum_fusion.obs_ref, f32[32,24,128]{2,1,0:T(8,128)S(1)} %all-to-all-done.1.expo_ref, ...), custom_call_target="tpu_custom_call" | custom-call | flops 1073741824 | bytes 1048576 | tf_op jit(solution)/shard_map/pallas_call | solution.py:475
  73.2 2.8 %shard_map.89 = (f32[2,16,128]{2,1,0:T(8,128)S(1)}, f32[16,128]{1,0:T(8,128)S(1)}, f32[16,128]{1,0:T(8,128)S(1)}) custom-call(f32[4,160,128]{2,1,0:T(8,128)S(1)} %pad_maximum_fusion.obs_ref, f32[4,8,4096]{2,1,0:T(8,128)S(1)} %get-tuple-element.33.fit_ref, f32[2,16,128]{2,1,0:T(8,128)S(1)} %get-tuple-element.29.g0s_ref, ...), custom_call_target="tpu_custom_call" | custom-call | flops 1073741824 | bytes 1048576 | tf_op jit(solution)/shard_map/pallas_call | solution.py:475
  76.0 2.6 %collective-permute-start.5 = (f32[16,128]{1,0:T(8,128)S(1)}, f32[16,128]{1,0:T(8,128)S(1)}, u32[]{:S(2)}, u32[]{:S(2)}) collective-permute-start(f32[16,128]{1,0:T(8,128)S(1)} %get-tuple-element.40), channel_id=1, source_target_pairs={{0,8},{8,0},{1,9},{9,1},{2,10},{10,2},{3,11},{11,3},{4,12},{12,4},... | collective-permute-start | bytes 24584 | tf_op jit(solution)/shard_map/ppermute | solution.py:543
  78.6 0.8 collective-permute-done.5.got_ref
  79.4 19.9 %all_to_all.20.parts_ref = f32[8,16,128]{2,1,0:T(8,128)S(1)} all-to-all(f32[8,16,128]{2,1,0:T(8,128)S(1)} %shard_map.90), channel_id=1, replica_groups=mesh['x'=4,'zl'=8,'c'=2,'y'=4,'zh'=2] {'zl'}, dimensions={0} | all-to-all | bytes 131072 | tf_op jit(solution)/shard_map/all_to_all | solution.py:487
  99.3 16.6 %all_to_all.21.sums_ref = f32[32,16,128]{2,1,0:T(8,128)S(1)} all-to-all(f32[32,16,128]{2,1,0:T(8,128)S(1)} %shard_map.91), channel_id=1, replica_groups=mesh['x'=4,'zl'=8,'c'=2,'y'=4,'zh'=2] {'x','c','y'}, dimensions={0} | all-to-all | bytes 524288 | tf_op jit(solution)/shard_map/all_to_all | solution.py:487
  116.0 1.0 shard_map.92
  (9 shorter events, 0.1 us)
Async XLA Ops:
  3.1 15.8 %copy-start = (f32[80,128]{1,0:T(8,128)S(1)}, f32[80,128]{1,0:T(8,128)}, u32[]{:S(2)}) copy-start(f32[80,128]{1,0:T(8,128)} %get-tuple-element.25) | copy-start | bytes 122884
  3.1 44.3 %all-to-all-start = ((f32[16,8,128]{2,1,0:T(8,128)}), f32[16,8,128]{2,1,0:T(8,128)S(1)}, u32[]{:S(2)}, u32[]{:S(2)}) async-start(f32[16,8,128]{2,1,0:T(8,128)} %get-tuple-element.26), calls=%async_computation | async-start | bytes 131072 | tf_op jit(solution)/shard_map/all_to_all | solution.py:487
  18.9 14.9 %collective-permute-start = (f32[80,128]{1,0:T(8,128)S(1)}, f32[80,128]{1,0:T(8,128)S(1)}, u32[]{:S(2)}, u32[]{:S(2)}) collective-permute-start(f32[80,128]{1,0:T(8,128)S(1)} %copy-done), channel_id=1, source_target_pairs={{0,1},{1,0},{2,3},{3,2},{4,5},{5,4},{6,7},{7,6},{8,9},{9,8},{10,11... | collective-permute-start | bytes 122888 | tf_op jit(solution)/shard_map/ppermute | solution.py:518
  33.7 9.5 %collective-permute-start.3 = (f32[160,128]{1,0:T(8,128)S(1)}, f32[160,128]{1,0:T(8,128)S(1)}, u32[]{:S(2)}, u32[]{:S(2)}) collective-permute-start(f32[160,128]{1,0:T(8,128)S(1)} %constant_dynamic-update-slice_fusion), channel_id=1, source_target_pairs={{0,6},{2,0},{4,2},{6,4},{1,7},{3,1},{5,3},{7,5},{8,14},{10,8},{12,... | collective-permute-start | bytes 245768 | tf_op jit(solution)/shard_map/ppermute | solution.py:521
  38.4 6.7 %collective-permute-start.2 = (f32[160,128]{1,0:T(8,128)S(1)}, f32[160,128]{1,0:T(8,128)S(1)}, u32[]{:S(2)}, u32[]{:S(2)}) collective-permute-start(f32[160,128]{1,0:T(8,128)S(1)} %constant_dynamic-update-slice_fusion), channel_id=1, source_target_pairs={{0,4},{2,6},{4,0},{6,2},{1,5},{3,7},{5,1},{7,3},{8,12},{10,14},{12... | collective-permute-start | bytes 245768 | tf_op jit(solution)/shard_map/ppermute | solution.py:521
  40.6 6.7 %collective-permute-start.1 = (f32[160,128]{1,0:T(8,128)S(1)}, f32[160,128]{1,0:T(8,128)S(1)}, u32[]{:S(2)}, u32[]{:S(2)}) collective-permute-start(f32[160,128]{1,0:T(8,128)S(1)} %constant_dynamic-update-slice_fusion), channel_id=1, source_target_pairs={{0,2},{2,4},{4,6},{6,0},{1,3},{3,5},{5,7},{7,1},{8,10},{10,12},{12... | collective-permute-start | bytes 245768 | tf_op jit(solution)/shard_map/ppermute | solution.py:521
  51.5 19.1 %all-to-all-start.1 = ((f32[32,24,128]{2,1,0:T(8,128)}), f32[32,24,128]{2,1,0:T(8,128)S(1)}, u32[]{:S(2)}, u32[]{:S(2)}) async-start(f32[32,24,128]{2,1,0:T(8,128)} %get-tuple-element.27), calls=%async_computation.1 | async-start | bytes 786432 | tf_op jit(solution)/shard_map/all_to_all | solution.py:487
  60.5 7.7 %collective-permute-start.4 = (f32[2,128]{1,0:T(2,128)S(1)}, f32[2,128]{1,0:T(2,128)S(1)}, u32[]{:S(2)}, u32[]{:S(2)}) collective-permute-start(f32[2,128]{1,0:T(2,128)S(1)} %get-tuple-element.32), channel_id=1, source_target_pairs={{8,16},{16,8},{9,17},{17,9},{10,18},{18,10},{11,19},{19,11},{12,20... | collective-permute-start | bytes 3080 | tf_op jit(solution)/shard_map/ppermute | solution.py:529
  76.0 3.4 %collective-permute-start.5 = (f32[16,128]{1,0:T(8,128)S(1)}, f32[16,128]{1,0:T(8,128)S(1)}, u32[]{:S(2)}, u32[]{:S(2)}) collective-permute-start(f32[16,128]{1,0:T(8,128)S(1)} %get-tuple-element.40), channel_id=1, source_target_pairs={{0,8},{8,0},{1,9},{9,1},{2,10},{10,2},{3,11},{11,3},{4,12},{12,4},... | collective-permute-start | bytes 24584 | tf_op jit(solution)/shard_map/ppermute | solution.py:543

commit v9 on v6

--- a/solution.py
+++ b/solution.py
@@ -260,77 +260,65 @@
     return jnp.concatenate(out, axis=0)
 
 
-def expo_apply_kernel(
-    obs_ref, expo_ref, g0f_ref, cf_ref, df_ref, hop_ref,
-    fit_ref, cf_out, yf_out, g0z_out, dz_out,
+def fold8(a):
+    total = a[0:8]
+    for i in range(8, a.shape[0], 8):
+        total = total + a[i : i + 8]
+    return jnp.sum(total, axis=0, keepdims=True)
+
+
+def fold_lanes(a):
+    total = a[:, 0:LO]
+    for i in range(LO, a.shape[1], LO):
+        total = total + a[:, i : i + LO]
+    return total
+
+
+def apply_kernel(
+    obs_ref, expo_ref, g0s_ref, ds_ref, cs_in, g0f_ref, cf_in, df_ref, ru_ref, hop_ref,
+    ys_ref, yf_ref, g0z_ref, dz_ref, out_ref, cs_ref, cf_ref,
 ):
     part = expo_ref[0, 0:64]
     for xc in range(1, 8):
         part = part + expo_ref[xc, 0:64]
     for y in range(4):
         diag = part[16 * y : 16 * y + 16, HALF:] + RIDGE
-        g0z_out[y] = part[16 * y : 16 * y + 16, :HALF] / diag
-        dz_out[y] = diag
-    cf_out[...] = cf_ref[...]
+        g0z_ref[y] = part[16 * y : 16 * y + 16, :HALF] / diag
+        dz_ref[y] = diag
+    cs_ref[...] = cs_in[...]
+    cf_ref[...] = cf_in[...]
 
     def apply(step, carry):
         expo = Ids(chunk(obs_ref, step, E), HALF, (0, 8, 0, 8))
         hot = expo.hot()
         found = [
             gather(
-                g0z_out[2 * (step % 2) + yy],
+                g0z_ref[2 * (step % 2) + yy],
                 expo.full[16 * yy : 16 * yy + 16],
                 hot[:, 2048 * yy : 2048 * (yy + 1)],
             )
             for yy in range(2)
         ]
         fit = joined(rows_of(chunk(obs_ref, step, W))) * joined(found)
-        fit_ref[step] = fit
+        values = [[across(part, 0) for part in split(fit, FEW)]]
         flat = Ids(chunk(obs_ref, step, PX), LO)
-        (added,) = scatter([[across(part, 0) for part in split(fit, FEW)]], flat.bf, flat.hot())
-        cf_out[...] += added
+        (added,) = scatter(values, flat.bf, flat.hot())
+        cf_ref[...] += added
+        star = Ids(chunk(obs_ref, step, S), LO)
+        (added,) = scatter(values, star.bf, star.hot())
+        cs_ref[step // 2] += added
         return carry
 
     lax.fori_loop(0, 4, apply, 0)
-    x, c = lax.axis_index("x"), lax.axis_index("c")
+    x, c, y = lax.axis_index("x"), lax.axis_index("c"), lax.axis_index("y")
     chip = expo_ref[2 * x + 1 - c, 64:68]
     above = jnp.where(c == 1, chip[2:4], hop_ref[...])
     below = jnp.where(c == 1, hop_ref[...], chip[0:2])
-    cf = cf_out[...] - SMOOTH * beside(g0f_ref[...], above, below)
-    cf_out[...] = cf
-    yf = cf / df_ref[...]
-    yf_out[...] = yf
-
-
-def fold8(a):
-    total = a[0:8]
-    for i in range(8, a.shape[0], 8):
-        total = total + a[i : i + 8]
-    return jnp.sum(total, axis=0, keepdims=True)
-
-
-def fold_lanes(a):
-    total = a[:, 0:LO]
-    for i in range(LO, a.shape[1], LO):
-        total = total + a[:, i : i + LO]
-    return total
-
-
-def last_kernel(
-    obs_ref, fit_ref, g0s_ref, ds_ref, cs_in, g0f_ref, df_ref, cf_ref, yf_ref, ru_ref, ys_ref, out_ref, cs_ref
-):
-    cs_ref[...] = cs_in[...]
-
-    def finish_star(step, carry):
-        star = Ids(chunk(obs_ref, step, S), LO)
-        parts = split(fit_ref[step], FEW)
-        (added,) = scatter([[across(part, 0) for part in parts]], star.bf, star.hot())
-        cs_ref[step // 2] += added
-        return carry
-
-    lax.fori_loop(0, 4, finish_star, 0)
-    rho = jnp.zeros((1, LO), F32)
-    beta, eta = rho, rho
+    g0f, df = g0f_ref[...], df_ref[...]
+    cf = cf_ref[...] - SMOOTH * beside(g0f, above, below)
+    yf = cf / df
+    yf_ref[...] = yf
+    rho, beta, eta = fold8(g0f * g0f * df), fold8(g0f * cf), fold8(cf * yf)
     for kk in range(2):
         g0s, ds, cs = g0s_ref[kk], ds_ref[kk], cs_ref[kk]
         ys = cs / ds
@@ -338,10 +326,8 @@
         rho += fold8(g0s * g0s * ds)
         beta += fold8(g0s * cs)
         eta += fold8(cs * ys)
-    y = lax.axis_index("y")
     total = jnp.zeros((HI, HALF), F32)
     cross = jnp.zeros((1, LO), F32)
-    yf = yf_ref[...]
     for kk in range(2):
         star, flat = Ids(own(obs_ref, y, kk, S), LO), Ids(own(obs_ref, y, kk, PX), LO)
         expo = Ids(own(obs_ref, y, kk, E), HALF, (0, 8))
@@ -353,17 +339,15 @@
         total += added
         cross += fold_lanes(w * from_star * from_flat)
     expos = joined([ru_ref[...], total])
-    g0f, df, cf = g0f_ref[...], df_ref[...], cf_ref[...]
     none = jnp.zeros((2, LO), F32)
-    rho = 0.25 * (rho + fold8(g0f * g0f * df))
-    beta = 0.25 * (beta + fold8(g0f * cf))
-    eta = 0.25 * (eta + fold8(cf * yf))
     delta = 2.0 * cross - (0.25 * SMOOTH) * fold8(yf * beside(yf, none, none))
-    scal = jnp.concatenate([rho, beta, eta, delta, edge_rows(yf)], axis=0)
+    scal = jnp.concatenate(
+        [0.25 * rho, 0.25 * beta, 0.25 * eta, delta, edge_rows(yf)], axis=0
+    )
     for zl in range(NZ):
-        for c in range(NC):
-            out_ref[NC * zl + c, 0:8] = expos[8 * c : 8 * c + 8]
-            out_ref[NC * zl + c, 8:16] = scal
+        for half in range(NC):
+            out_ref[NC * zl + half, 0:8] = expos[8 * half : 8 * half + 8]
+            out_ref[NC * zl + half, 8:16] = scal
 
 
 def edge_dot(last, first):
@@ -511,7 +495,8 @@
     expo = exchange(expo, ("zl", "zh"))
     expo = expo.reshape(NZ, NH, 8, LO).sum(axis=0)
     expo = jnp.where(zh == 0, expo, expo[::-1]).reshape(HI, LO)
-    tile_obs = jnp.concatenate([obs, partner, expo], axis=0)
+    both = lax.optimization_barrier(jnp.concatenate([obs, partner], axis=0))
+    tile_obs = jnp.concatenate([both, expo], axis=0)
     tile_obs = to_all(lax.optimization_barrier(tile_obs), NY, "y")
     g0s, ds, g0f, df, hop_row, plane = call(
         sums_kernel, [stars] * 2 + [flats] * 2 + [(2, LO), (8, 72, LO)], (tile_obs,), mib=16, work=29
@@ -522,14 +507,10 @@
         couple_kernel, [stars, flats, (HI, HALF)], (tile_obs, g0s, g0f),
         scratch=[pltpu.VMEM((4, 8, 4096), F32)], mib=16, work=30,
     )
-    fit, cf, yf, g0z, dz = call(
-        expo_apply_kernel, [(4, 8, 4096)] + [flats] * 2 + [expos] * 2,
-        (tile_obs, expo, g0f, cf, df, by_hop), mib=16, work=30,
-    )
-    ys, payload = call(
-        last_kernel, [stars, (16, 16, LO)],
-        (tile_obs, fit, g0s, ds, cs, g0f, df, cf, yf, ru),
-        scratch=[pltpu.VMEM(stars, F32)], mib=16, work=30,
+    ys, yf, g0z, dz, payload = call(
+        apply_kernel, [stars, flats] + [expos] * 2 + [(16, 16, LO)],
+        (tile_obs, expo, g0s, ds, cs, g0f, cf, df, ru, by_hop),
+        scratch=[pltpu.VMEM(stars, F32), pltpu.VMEM(flats, F32)], mib=16, work=30,
     )
     payload = exchange(payload, ("zl", "c"))
     sums = exchange(call(column_kernel, [(32, 16, LO)], (payload,)), PLANE)

time: 109 us -> 108 us (level)
    pallas_call x7 -> x6, Pallas kernels: 17.8 us -> 17.2 us  [call(): pl.pallas_call(kernel, out_shape=tuple(out) if many else out[0], in_specs...]
  transfers between devices with their start and end apart: 4 -> 4, of which waited for: 2 -> 1; matrix products, arithmetic and copies ran while one was open for 0% -> 0% of each run, Pallas kernels for 5% -> 5%
where the time goes in v9:
time: 108 us
  blocking collectives  49 us (45%)
  starting transfers between devices  38 us (35%)
  Pallas kernels  17.2 us (16%)
  waiting for transfers between devices  2.87 us (3%)
    all_to_all x3, blocking collectives, exchange(): return lax.all_to_all(blocks, axes, 0, 0, tiled=True)  49 us
    all_to_all x2, starting transfers between devices, exchange(): return lax.all_to_all(blocks, axes, 0, 0, tiled=True)  23.5 us
    pallas_call x6, Pallas kernels, call(): pl.pallas_call(kernel, out_shape=tuple(out) if many else out[0], in_specs...  17.2 us
    ppermute x1, starting transfers between devices, on_device(): partner = lax.ppermute(obs, 'zh', [(0, 1), (1, 0)])  12 us
    ppermute x1, waiting for transfers between devices, on_device(): partner = lax.ppermute(obs, 'zh', [(0, 1), (1, 0)])  2.86 us
    ppermute x1, starting transfers between devices, on_device(): by_hop = lax.ppermute(hop_row, ALL, hop)  2.57 us
  transfers between devices with their start and end apart: 4, of which 1 were waited for; matrix products, arithmetic and copies ran while one was open for 0% of the time, Pallas kernels for 5%

profile of v9, /device:TPU:1, one launch (start us, length us, event | category | flops | bytes accessed | tf_op | source)
XLA Modules:
  0.0 107.9 jit_solution(16229362897194856204)
XLA Ops:
  0.6 2.4 %shard_map.85 = (f32[80,128]{1,0:T(8,128)}, f32[16,8,128]{2,1,0:T(8,128)}) custom-call(s32[1,16]{1,0:T(1,128)} %block_ref.1, s32[16,128]{1,0:T(8,128)} %bitcast.11, s32[16,128]{1,0:T(8,128)} %bitcast.12, s32[16,128]{1,0:T(8,128)} %bitcast.13, f32[16,128]{1,0:T(8,128)} %bitcast.14, f32[16,128]{1,0:T(8,128)} %bitcast.15), custom_call_target="tpu_custom_call" | custom-call | flops 1048576 | bytes 1048576 | tf_op jit(solution)/shard_map/pallas_call | solution.py:447
  3.1 0.0 copy-start
  3.1 15.7 %all-to-all-start = ((f32[16,8,128]{2,1,0:T(8,128)}), f32[16,8,128]{2,1,0:T(8,128)S(1)}, u32[]{:S(2)}, u32[]{:S(2)}) async-start(f32[16,8,128]{2,1,0:T(8,128)} %get-tuple-element.23), calls=%async_computation | async-start | bytes 131072 | tf_op jit(solution)/shard_map/all_to_all | solution.py:459
  18.8 0.0 copy-done
  18.9 12.0 %collective-permute-start = (f32[80,128]{1,0:T(8,128)S(1)}, f32[80,128]{1,0:T(8,128)S(1)}, u32[]{:S(2)}, u32[]{:S(2)}) collective-permute-start(f32[80,128]{1,0:T(8,128)S(1)} %copy-done), channel_id=1, source_target_pairs={{0,1},{1,0},{2,3},{3,2},{4,5},{5,4},{6,7},{7,6},{8,9},{9,8},{10,11... | collective-permute-start | bytes 122888 | tf_op jit(solution)/shard_map/ppermute | solution.py:494
  30.9 2.9 %collective-permute-done = f32[80,128]{1,0:T(8,128)S(1)} collective-permute-done((f32[80,128]{1,0:T(8,128)S(1)}, f32[80,128]{1,0:T(8,128)S(1)}, u32[]{:S(2)}, u32[]{:S(2)}) %collective-permute-start) | collective-permute-done | bytes 40992 | tf_op jit(solution)/shard_map/ppermute | solution.py:494
  33.7 0.0 all-to-all-done
  33.8 10.0 %all_to_all.25.obs_ref = f32[4,176,128]{2,1,0:T(8,128)S(1)} all-to-all(f32[4,176,128]{2,1,0:T(8,128)S(1)} %broadcast_in_dim.2), channel_id=1, replica_groups=mesh['x'=4,'zl'=8,'c'=2,'y'=4,'zh'=2] {'y'}, dimensions={0} | all-to-all | bytes 720896 | tf_op jit(solution)/shard_map/all_to_all | solution.py:459
  43.9 4.0 %shard_map.86 = (f32[2,16,128]{2,1,0:T(8,128)S(1)}, f32[2,16,128]{2,1,0:T(8,128)S(1)}, f32[16,128]{1,0:T(8,128)S(1)}, f32[16,128]{1,0:T(8,128)S(1)}, f32[2,128]{1,0:T(2,128)S(1)}, /*index=5*/f32[8,72,128]{2,1,0:T(8,128)}) custom-call(f32[4,176,128]{2,1,0:T(8,128)S(1)} %all_to_all.25.obs_ref), custom_call_target="tpu_custom_call" | custom-call | flops 536870912 | bytes 1048576 | tf_op jit(solution)/shard_map/pallas_call | solution.py:447
  47.9 7.7 %all-to-all-start.2 = ((f32[8,72,128]{2,1,0:T(8,128)}), f32[8,72,128]{2,1,0:T(8,128)S(1)}, u32[]{:S(2)}, u32[]{:S(2)}) async-start(f32[8,72,128]{2,1,0:T(8,128)} %get-tuple-element.24), calls=%async_computation.2 | async-start | bytes 589824 | tf_op jit(solution)/shard_map/all_to_all | solution.py:459
  55.6 2.6 %collective-permute-start.1 = (f32[2,128]{1,0:T(2,128)S(1)}, f32[2,128]{1,0:T(2,128)S(1)}, u32[]{:S(2)}, u32[]{:S(2)}) collective-permute-start(f32[2,128]{1,0:T(2,128)S(1)} %get-tuple-element.32), channel_id=1, source_target_pairs={{8,16},{16,8},{9,17},{17,9},{10,18},{18,10},{11,19},{19,11},{12,20... | collective-permute-start | bytes 3080 | tf_op jit(solution)/shard_map/ppermute | solution.py:505
  58.2 4.9 %shard_map.87 = (f32[2,16,128]{2,1,0:T(8,128)S(1)}, f32[16,128]{1,0:T(8,128)S(1)}, f32[16,64]{1,0:T(8,128)S(1)}) custom-call(f32[4,176,128]{2,1,0:T(8,128)S(1)} %all_to_all.25.obs_ref, f32[2,16,128]{2,1,0:T(8,128)S(1)} %get-tuple-element.25.g0s_ref, f32[16,128]{1,0:T(8,128)S(1)} %get-tuple-element.27.g0f_ref), custom_call_target="tpu_custom_call" | custom-call | flops 1073741824 | bytes 1048576 | tf_op jit(solution)/shard_map/pallas_call | solution.py:447
  63.1 0.0 collective-permute-done.1.hop_ref
  63.1 0.0 all-to-all-done.2.expo_ref
  63.1 4.9 %shard_map.88 = (f32[2,16,128]{2,1,0:T(8,128)S(1)}, f32[16,128]{1,0:T(8,128)S(1)}, f32[4,16,64]{2,1,0:T(8,128)S(1)}, f32[4,16,64]{2,1,0:T(8,128)S(1)}, f32[16,16,128]{2,1,0:T(8,128)S(1)}) custom-call(f32[4,176,128]{2,1,0:T(8,128)S(1)} %all_to_all.25.obs_ref, f32[8,72,128]{2,1,0:T(8,128)S(1)} %all-to-all-done.2.expo_ref, ...), custom_call_target="tpu_custom_call" | custom-call | flops 1073741824 | bytes 1048576 | tf_op jit(solution)/shard_map/pallas_call | solution.py:447
  68.0 25.3 %all_to_all.26.parts_ref = f32[16,16,128]{2,1,0:T(8,128)S(1)} all-to-all(f32[16,16,128]{2,1,0:T(8,128)S(1)} %get-tuple-element.33), channel_id=1, replica_groups=mesh['x'=4,'zl'=8,'c'=2,'y'=4,'zh'=2] {'zl','c'}, dimensions={0} | all-to-all | bytes 262144 | tf_op jit(solution)/shard_map/all_to_all | solution.py:459
  93.3 13.6 %all_to_all.27.sums_ref = f32[32,16,128]{2,1,0:T(8,128)S(1)} all-to-all(f32[32,16,128]{2,1,0:T(8,128)S(1)} %shard_map.89), channel_id=1, replica_groups=mesh['x'=4,'zl'=8,'c'=2,'y'=4,'zh'=2] {'x','c','y'}, dimensions={0} | all-to-all | bytes 524288 | tf_op jit(solution)/shard_map/all_to_all | solution.py:459
  106.9 1.0 shard_map.90
  (6 shorter events, 0.1 us)
Async XLA Ops:
  3.1 15.8 %copy-start = (f32[80,128]{1,0:T(8,128)S(1)}, f32[80,128]{1,0:T(8,128)}, u32[]{:S(2)}) copy-start(f32[80,128]{1,0:T(8,128)} %get-tuple-element.22) | copy-start | bytes 122884
  3.1 30.6 %all-to-all-start = ((f32[16,8,128]{2,1,0:T(8,128)}), f32[16,8,128]{2,1,0:T(8,128)S(1)}, u32[]{:S(2)}, u32[]{:S(2)}) async-start(f32[16,8,128]{2,1,0:T(8,128)} %get-tuple-element.23), calls=%async_computation | async-start | bytes 131072 | tf_op jit(solution)/shard_map/all_to_all | solution.py:459
  18.9 14.9 %collective-permute-start = (f32[80,128]{1,0:T(8,128)S(1)}, f32[80,128]{1,0:T(8,128)S(1)}, u32[]{:S(2)}, u32[]{:S(2)}) collective-permute-start(f32[80,128]{1,0:T(8,128)S(1)} %copy-done), channel_id=1, source_target_pairs={{0,1},{1,0},{2,3},{3,2},{4,5},{5,4},{6,7},{7,6},{8,9},{9,8},{10,11... | collective-permute-start | bytes 122888 | tf_op jit(solution)/shard_map/ppermute | solution.py:494
  47.9 15.2 %all-to-all-start.2 = ((f32[8,72,128]{2,1,0:T(8,128)}), f32[8,72,128]{2,1,0:T(8,128)S(1)}, u32[]{:S(2)}, u32[]{:S(2)}) async-start(f32[8,72,128]{2,1,0:T(8,128)} %get-tuple-element.24), calls=%async_computation.2 | async-start | bytes 589824 | tf_op jit(solution)/shard_map/all_to_all | solution.py:459
  55.6 7.5 %collective-permute-start.1 = (f32[2,128]{1,0:T(2,128)S(1)}, f32[2,128]{1,0:T(2,128)S(1)}, u32[]{:S(2)}, u32[]{:S(2)}) collective-permute-start(f32[2,128]{1,0:T(2,128)S(1)} %get-tuple-element.32), channel_id=1, source_target_pairs={{8,16},{16,8},{9,17},{17,9},{10,18},{18,10},{11,19},{19,11},{12,20... | collective-permute-start | bytes 3080 | tf_op jit(solution)/shard_map/ppermute | solution.py:505

commit v10 on v9

--- a/solution.py
+++ b/solution.py
@@ -178,23 +178,45 @@
     return jnp.concatenate([flat[0:1], flat[8:9], flat[7:8], flat[15:16]], axis=0)
 
 
-def sums_kernel(obs_ref, g0s_ref, ds_ref, g0f_ref, df_ref, hop_ref, plane_ref):
-    for ref in (g0s_ref, ds_ref, g0f_ref, df_ref):
+def add_sums(tiles, kk, star_ref, star_count_ref, flat_ref, flat_count_ref):
+    values = [split_rows(tiles(f)) for f in (WM, W)]
+    ids = Ids(tiles(S), LO)
+    weighted, count = scatter(values, ids.bf, ids.hot())
+    star_ref[kk] += weighted
+    star_count_ref[kk] += count
+    ids = Ids(tiles(PX), LO)
+    weighted, count = scatter(values, ids.bf, ids.hot())
+    flat_ref[...] += weighted
+    flat_count_ref[...] += count
+
+
+def own_sums_kernel(both_ref, *totals):
+    for ref in totals:
         ref[...] = jnp.zeros(ref.shape, F32)
-
-    def sums(step, carry):
-        values = [split_rows(chunk(obs_ref, step, f)) for f in (WM, W)]
-        ids = Ids(chunk(obs_ref, step, S), LO)
-        weighted, count = scatter(values, ids.bf, ids.hot())
-        g0s_ref[step // 2] += weighted
-        ds_ref[step // 2] += count
-        ids = Ids(chunk(obs_ref, step, PX), LO)
-        weighted, count = scatter(values, ids.bf, ids.hot())
-        g0f_ref[...] += weighted
-        df_ref[...] += count
+    for kk in range(2):
+
+        def tiles(f):
+            return [both_ref[80 * rel + 40 * kk + 8 * f : 80 * rel + 40 * kk + 8 * f + 8] for rel in range(2)]
+
+        add_sums(tiles, kk, *totals)
+
+
+def sums_kernel(
+    obs_ref, star_in, star_count_in, flat_in, flat_count_in, g0s_ref, ds_ref, g0f_ref, df_ref, hop_ref, plane_ref
+):
+    totals = (g0s_ref, ds_ref, g0f_ref, df_ref)
+    for ref, given in zip(totals, (star_in, star_count_in, flat_in, flat_count_in)):
+        ref[...] = given[...]
+    y = lax.axis_index("y")
+
+    def sums(kk, carry):
+        def tiles(f):
+            return [tile for d in range(1, NY) for tile in own(obs_ref, (y + d) % NY, kk, f)]
+
+        add_sums(tiles, kk, *totals)
         return carry
 
-    lax.fori_loop(0, 4, sums, 0)
+    lax.fori_loop(0, 2, sums, 0)
     diag = df_ref[...] + (4.0 * SMOOTH + RIDGE)
     g0f = g0f_ref[...] / diag
     df_ref[...] = diag
@@ -496,10 +518,12 @@
     expo = expo.reshape(NZ, NH, 8, LO).sum(axis=0)
     expo = jnp.where(zh == 0, expo, expo[::-1]).reshape(HI, LO)
     both = lax.optimization_barrier(jnp.concatenate([obs, partner], axis=0))
+    totals = call(own_sums_kernel, [stars] * 2 + [flats] * 2, (both,), work=26)
+    both, totals = lax.optimization_barrier((both, totals))
     tile_obs = jnp.concatenate([both, expo], axis=0)
     tile_obs = to_all(lax.optimization_barrier(tile_obs), NY, "y")
     g0s, ds, g0f, df, hop_row, plane = call(
-        sums_kernel, [stars] * 2 + [flats] * 2 + [(2, LO), (8, 72, LO)], (tile_obs,), mib=16, work=29
+        sums_kernel, [stars] * 2 + [flats] * 2 + [(2, LO), (8, 72, LO)], (tile_obs, *totals), mib=16, work=29
     )
     expo = exchange(plane, COLS)
     by_hop = lax.ppermute(hop_row, ALL, hop)

time: 108 us -> 108 us (level)
    pallas_call x6 -> x7, Pallas kernels: 17.2 us -> 17 us  [call(): pl.pallas_call(kernel, out_shape=tuple(out) if many else out[0], in_specs...]
where the time goes in v10:
time: 108 us
  blocking collectives  48.9 us (45%)
  starting transfers between devices  38 us (35%)
  Pallas kernels  17 us (16%)
  waiting for transfers between devices  2.87 us (3%)
    all_to_all x3, blocking collectives, exchange(): return lax.all_to_all(blocks, axes, 0, 0, tiled=True)  48.9 us
    all_to_all x2, starting transfers between devices, exchange(): return lax.all_to_all(blocks, axes, 0, 0, tiled=True)  23.5 us
    pallas_call x7, Pallas kernels, call(): pl.pallas_call(kernel, out_shape=tuple(out) if many else out[0], in_specs...  17 us
    ppermute x1, starting transfers between devices, on_device(): partner = lax.ppermute(obs, 'zh', [(0, 1), (1, 0)])  12 us
    ppermute x1, waiting for transfers between devices, on_device(): partner = lax.ppermute(obs, 'zh', [(0, 1), (1, 0)])  2.86 us
    ppermute x1, starting transfers between devices, on_device(): by_hop = lax.ppermute(hop_row, ALL, hop)  2.57 us
  transfers between devices with their start and end apart: 4, of which 1 were waited for; matrix products, arithmetic and copies ran while one was open for 0% of the time, Pallas kernels for 5%

profile of v10, /device:TPU:1, one launch (start us, length us, event | category | flops | bytes accessed | tf_op | source)
XLA Modules:
  0.0 107.7 jit_solution(18249970952525360185)
XLA Ops:
  0.6 2.5 %shard_map.85 = (f32[80,128]{1,0:T(8,128)}, f32[16,8,128]{2,1,0:T(8,128)}) custom-call(s32[1,16]{1,0:T(1,128)} %block_ref.1, s32[16,128]{1,0:T(8,128)} %bitcast.11, s32[16,128]{1,0:T(8,128)} %bitcast.12, s32[16,128]{1,0:T(8,128)} %bitcast.13, f32[16,128]{1,0:T(8,128)} %bitcast.14, f32[16,128]{1,0:T(8,128)} %bitcast.15), custom_call_target="tpu_custom_call" | custom-call | flops 1048576 | bytes 1048576 | tf_op jit(solution)/shard_map/pallas_call | solution.py:469
  3.1 0.0 copy-start
  3.1 15.7 %all-to-all-start = ((f32[16,8,128]{2,1,0:T(8,128)}), f32[16,8,128]{2,1,0:T(8,128)S(1)}, u32[]{:S(2)}, u32[]{:S(2)}) async-start(f32[16,8,128]{2,1,0:T(8,128)} %get-tuple-element.37), calls=%async_computation | async-start | bytes 131072 | tf_op jit(solution)/shard_map/all_to_all | solution.py:481
  18.9 0.0 copy-done
  18.9 12.0 %collective-permute-start = (f32[80,128]{1,0:T(8,128)S(1)}, f32[80,128]{1,0:T(8,128)S(1)}, u32[]{:S(2)}, u32[]{:S(2)}) collective-permute-start(f32[80,128]{1,0:T(8,128)S(1)} %copy-done), channel_id=1, source_target_pairs={{0,1},{1,0},{2,3},{3,2},{4,5},{5,4},{6,7},{7,6},{8,9},{9,8},{10,11... | collective-permute-start | bytes 122888 | tf_op jit(solution)/shard_map/ppermute | solution.py:516
  30.9 2.9 %collective-permute-done = f32[80,128]{1,0:T(8,128)S(1)} collective-permute-done((f32[80,128]{1,0:T(8,128)S(1)}, f32[80,128]{1,0:T(8,128)S(1)}, u32[]{:S(2)}, u32[]{:S(2)}) %collective-permute-start) | collective-permute-done | bytes 40992 | tf_op jit(solution)/shard_map/ppermute | solution.py:516
  33.7 0.7 shard_map.86
  34.5 0.0 all-to-all-done
  34.6 10.0 %all_to_all.25.obs_ref = f32[4,176,128]{2,1,0:T(8,128)S(1)} all-to-all(f32[4,176,128]{2,1,0:T(8,128)S(1)} %broadcast_in_dim.2), channel_id=1, replica_groups=mesh['x'=4,'zl'=8,'c'=2,'y'=4,'zh'=2] {'y'}, dimensions={0} | all-to-all | bytes 720896 | tf_op jit(solution)/shard_map/all_to_all | solution.py:481
  44.6 3.0 %shard_map.87 = (f32[2,16,128]{2,1,0:T(8,128)S(1)}, f32[2,16,128]{2,1,0:T(8,128)S(1)}, f32[16,128]{1,0:T(8,128)S(1)}, f32[16,128]{1,0:T(8,128)S(1)}, f32[2,128]{1,0:T(2,128)S(1)}, /*index=5*/f32[8,72,128]{2,1,0:T(8,128)}) custom-call(f32[4,176,128]{2,1,0:T(8,128)S(1)} %all_to_all.25.obs_ref, f32[2,16,128]{2,1,0:T(8,128)S(1)} %get-tuple-element.38.star_in, ...), custom_call_target="tpu_custom_call" | custom-call | flops 536870912 | bytes 1048576 | tf_op jit(solution)/shard_map/pallas_call | solution.py:469
  47.6 7.7 %all-to-all-start.2 = ((f32[8,72,128]{2,1,0:T(8,128)}), f32[8,72,128]{2,1,0:T(8,128)S(1)}, u32[]{:S(2)}, u32[]{:S(2)}) async-start(f32[8,72,128]{2,1,0:T(8,128)} %get-tuple-element.42), calls=%async_computation.2 | async-start | bytes 589824 | tf_op jit(solution)/shard_map/all_to_all | solution.py:481
  55.4 2.6 %collective-permute-start.1 = (f32[2,128]{1,0:T(2,128)S(1)}, f32[2,128]{1,0:T(2,128)S(1)}, u32[]{:S(2)}, u32[]{:S(2)}) collective-permute-start(f32[2,128]{1,0:T(2,128)S(1)} %get-tuple-element.50), channel_id=1, source_target_pairs={{8,16},{16,8},{9,17},{17,9},{10,18},{18,10},{11,19},{19,11},{12,20... | collective-permute-start | bytes 3080 | tf_op jit(solution)/shard_map/ppermute | solution.py:529
  58.0 4.9 %shard_map.88 = (f32[2,16,128]{2,1,0:T(8,128)S(1)}, f32[16,128]{1,0:T(8,128)S(1)}, f32[16,64]{1,0:T(8,128)S(1)}) custom-call(f32[4,176,128]{2,1,0:T(8,128)S(1)} %all_to_all.25.obs_ref, f32[2,16,128]{2,1,0:T(8,128)S(1)} %get-tuple-element.43.g0s_ref, f32[16,128]{1,0:T(8,128)S(1)} %get-tuple-element.45.g0f_ref), custom_call_target="tpu_custom_call" | custom-call | flops 1073741824 | bytes 1048576 | tf_op jit(solution)/shard_map/pallas_call | solution.py:469
  62.9 0.0 collective-permute-done.1.hop_ref
  62.9 0.0 all-to-all-done.2.expo_ref
  62.9 4.9 %shard_map.89 = (f32[2,16,128]{2,1,0:T(8,128)S(1)}, f32[16,128]{1,0:T(8,128)S(1)}, f32[4,16,64]{2,1,0:T(8,128)S(1)}, f32[4,16,64]{2,1,0:T(8,128)S(1)}, f32[16,16,128]{2,1,0:T(8,128)S(1)}) custom-call(f32[4,176,128]{2,1,0:T(8,128)S(1)} %all_to_all.25.obs_ref, f32[8,72,128]{2,1,0:T(8,128)S(1)} %all-to-all-done.2.expo_ref, ...), custom_call_target="tpu_custom_call" | custom-call | flops 1073741824 | bytes 1048576 | tf_op jit(solution)/shard_map/pallas_call | solution.py:469
  67.7 25.3 %all_to_all.26.parts_ref = f32[16,16,128]{2,1,0:T(8,128)S(1)} all-to-all(f32[16,16,128]{2,1,0:T(8,128)S(1)} %get-tuple-element.51), channel_id=1, replica_groups=mesh['x'=4,'zl'=8,'c'=2,'y'=4,'zh'=2] {'zl','c'}, dimensions={0} | all-to-all | bytes 262144 | tf_op jit(solution)/shard_map/all_to_all | solution.py:481
  93.1 13.6 %all_to_all.27.sums_ref = f32[32,16,128]{2,1,0:T(8,128)S(1)} all-to-all(f32[32,16,128]{2,1,0:T(8,128)S(1)} %shard_map.90), channel_id=1, replica_groups=mesh['x'=4,'zl'=8,'c'=2,'y'=4,'zh'=2] {'x','c','y'}, dimensions={0} | all-to-all | bytes 524288 | tf_op jit(solution)/shard_map/all_to_all | solution.py:481
  106.7 1.0 shard_map.91
  (6 shorter events, 0.1 us)
Async XLA Ops:
  3.1 15.8 %copy-start = (f32[80,128]{1,0:T(8,128)S(1)}, f32[80,128]{1,0:T(8,128)}, u32[]{:S(2)}) copy-start(f32[80,128]{1,0:T(8,128)} %get-tuple-element.31) | copy-start | bytes 122884
  3.1 31.4 %all-to-all-start = ((f32[16,8,128]{2,1,0:T(8,128)}), f32[16,8,128]{2,1,0:T(8,128)S(1)}, u32[]{:S(2)}, u32[]{:S(2)}) async-start(f32[16,8,128]{2,1,0:T(8,128)} %get-tuple-element.37), calls=%async_computation | async-start | bytes 131072 | tf_op jit(solution)/shard_map/all_to_all | solution.py:481
  18.9 14.9 %collective-permute-start = (f32[80,128]{1,0:T(8,128)S(1)}, f32[80,128]{1,0:T(8,128)S(1)}, u32[]{:S(2)}, u32[]{:S(2)}) collective-permute-start(f32[80,128]{1,0:T(8,128)S(1)} %copy-done), channel_id=1, source_target_pairs={{0,1},{1,0},{2,3},{3,2},{4,5},{5,4},{6,7},{7,6},{8,9},{9,8},{10,11... | collective-permute-start | bytes 122888 | tf_op jit(solution)/shard_map/ppermute | solution.py:516
  47.6 15.2 %all-to-all-start.2 = ((f32[8,72,128]{2,1,0:T(8,128)}), f32[8,72,128]{2,1,0:T(8,128)S(1)}, u32[]{:S(2)}, u32[]{:S(2)}) async-start(f32[8,72,128]{2,1,0:T(8,128)} %get-tuple-element.42), calls=%async_computation.2 | async-start | bytes 589824 | tf_op jit(solution)/shard_map/all_to_all | solution.py:481
  55.4 7.5 %collective-permute-start.1 = (f32[2,128]{1,0:T(2,128)S(1)}, f32[2,128]{1,0:T(2,128)S(1)}, u32[]{:S(2)}, u32[]{:S(2)}) collective-permute-start(f32[2,128]{1,0:T(2,128)S(1)} %get-tuple-element.50), channel_id=1, source_target_pairs={{8,16},{16,8},{9,17},{17,9},{10,18},{18,10},{11,19},{19,11},{12,20... | collective-permute-start | bytes 3080 | tf_op jit(solution)/shard_map/ppermute | solution.py:529

commit v11 on v10

--- a/solution.py
+++ b/solution.py
@@ -174,6 +174,11 @@
     return [field(obs_ref, y, rel, kk, f) for rel in range(2)]
 
 
+def unrolled(count, step):
+    for i in range(count):
+        step(i, 0)
+
+
 def edge_rows(flat):
     return jnp.concatenate([flat[0:1], flat[8:9], flat[7:8], flat[15:16]], axis=0)
 
@@ -216,7 +221,7 @@
         add_sums(tiles, kk, *totals)
         return carry
 
-    lax.fori_loop(0, 2, sums, 0)
+    unrolled(2, sums)
     diag = df_ref[...] + (4.0 * SMOOTH + RIDGE)
     g0f = g0f_ref[...] / diag
     df_ref[...] = diag
@@ -251,7 +256,7 @@
         fit_ref[step] = fit
         return carry
 
-    lax.fori_loop(0, 4, couple, 0)
+    unrolled(4, couple)
     y = lax.axis_index("y")
     total = jnp.zeros((HI, HALF), F32)
     for kk in range(2):
@@ -331,7 +336,7 @@
         cs_ref[step // 2] += added
         return carry
 
-    lax.fori_loop(0, 4, apply, 0)
+    unrolled(4, apply)
     x, c, y = lax.axis_index("x"), lax.axis_index("c"), lax.axis_index("y")
     chip = expo_ref[2 * x + 1 - c, 64:68]
     above = jnp.where(c == 1, chip[2:4], hop_ref[...])

time: 108 us -> 106 us (0.981)
  Pallas kernels: 17 us -> 14.5 us
    pallas_call x7, Pallas kernels: 17 us -> 14.5 us  [call(): pl.pallas_call(kernel, out_shape=tuple(out) if many else out[0], in_specs...]
  transfers between devices with their start and end apart: 4 -> 4, of which waited for: 1 -> 2; matrix products, arithmetic and copies ran while one was open for 0% -> 0% of each run, Pallas kernels for 5% -> 4%
where the time goes in v11:
time: 106 us; the launch traced here: 105 us
  blocking collectives  48.6 us (46%)
  starting transfers between devices  38 us (36%)
  Pallas kernels  14.5 us (14%)
  waiting for transfers between devices  3.28 us (3%)
    all_to_all x3, blocking collectives, exchange(): return lax.all_to_all(blocks, axes, 0, 0, tiled=True)  48.6 us
    all_to_all x2, starting transfers between devices, exchange(): return lax.all_to_all(blocks, axes, 0, 0, tiled=True)  23.5 us
    pallas_call x7, Pallas kernels, call(): pl.pallas_call(kernel, out_shape=tuple(out) if many else out[0], in_specs...  14.5 us
    ppermute x1, starting transfers between devices, on_device(): partner = lax.ppermute(obs, 'zh', [(0, 1), (1, 0)])  12 us
    ppermute x1, waiting for transfers between devices, on_device(): partner = lax.ppermute(obs, 'zh', [(0, 1), (1, 0)])  2.86 us
    ppermute x1, starting transfers between devices, on_device(): by_hop = lax.ppermute(hop_row, ALL, hop)  2.56 us
  transfers between devices with their start and end apart: 4, of which 2 were waited for; matrix products, arithmetic and copies ran while one was open for 0% of the time, Pallas kernels for 4%

profile of v11, /device:TPU:1, one launch (start us, length us, event | category | flops | bytes accessed | tf_op | source)
XLA Modules:
  0.0 105.1 jit_solution(2907623513825556257)
XLA Ops:
  0.6 2.5 %shard_map.85 = (f32[80,128]{1,0:T(8,128)}, f32[16,8,128]{2,1,0:T(8,128)}) custom-call(s32[1,16]{1,0:T(1,128)} %block_ref.1, s32[16,128]{1,0:T(8,128)} %bitcast.11, s32[16,128]{1,0:T(8,128)} %bitcast.12, s32[16,128]{1,0:T(8,128)} %bitcast.13, f32[16,128]{1,0:T(8,128)} %bitcast.14, f32[16,128]{1,0:T(8,128)} %bitcast.15), custom_call_target="tpu_custom_call" | custom-call | flops 1048576 | bytes 1048576 | tf_op jit(solution)/shard_map/pallas_call | solution.py:474
  3.1 0.0 copy-start
  3.1 15.7 %all-to-all-start = ((f32[16,8,128]{2,1,0:T(8,128)}), f32[16,8,128]{2,1,0:T(8,128)S(1)}, u32[]{:S(2)}, u32[]{:S(2)}) async-start(f32[16,8,128]{2,1,0:T(8,128)} %get-tuple-element.37), calls=%async_computation | async-start | bytes 131072 | tf_op jit(solution)/shard_map/all_to_all | solution.py:486
  18.9 0.0 copy-done
  18.9 12.0 %collective-permute-start = (f32[80,128]{1,0:T(8,128)S(1)}, f32[80,128]{1,0:T(8,128)S(1)}, u32[]{:S(2)}, u32[]{:S(2)}) collective-permute-start(f32[80,128]{1,0:T(8,128)S(1)} %copy-done), channel_id=1, source_target_pairs={{0,1},{1,0},{2,3},{3,2},{4,5},{5,4},{6,7},{7,6},{8,9},{9,8},{10,11... | collective-permute-start | bytes 122888 | tf_op jit(solution)/shard_map/ppermute | solution.py:521
  30.9 2.9 %collective-permute-done = f32[80,128]{1,0:T(8,128)S(1)} collective-permute-done((f32[80,128]{1,0:T(8,128)S(1)}, f32[80,128]{1,0:T(8,128)S(1)}, u32[]{:S(2)}, u32[]{:S(2)}) %collective-permute-start) | collective-permute-done | bytes 40992 | tf_op jit(solution)/shard_map/ppermute | solution.py:521
  33.7 0.7 shard_map.86
  34.5 0.0 all-to-all-done
  34.6 10.0 %all_to_all.25.obs_ref = f32[4,176,128]{2,1,0:T(8,128)S(1)} all-to-all(f32[4,176,128]{2,1,0:T(8,128)S(1)} %broadcast_in_dim.2), channel_id=1, replica_groups=mesh['x'=4,'zl'=8,'c'=2,'y'=4,'zh'=2] {'y'}, dimensions={0} | all-to-all | bytes 720896 | tf_op jit(solution)/shard_map/all_to_all | solution.py:486
  44.6 2.6 %shard_map.87 = (f32[2,16,128]{2,1,0:T(8,128)S(1)}, f32[2,16,128]{2,1,0:T(8,128)S(1)}, f32[16,128]{1,0:T(8,128)S(1)}, f32[16,128]{1,0:T(8,128)S(1)}, f32[2,128]{1,0:T(2,128)S(1)}, /*index=5*/f32[8,72,128]{2,1,0:T(8,128)}) custom-call(f32[4,176,128]{2,1,0:T(8,128)S(1)} %all_to_all.25.obs_ref, f32[2,16,128]{2,1,0:T(8,128)S(1)} %get-tuple-element.38.star_in, ...), custom_call_target="tpu_custom_call" | custom-call | flops 536870912 | bytes 1048576 | tf_op jit(solution)/shard_map/pallas_call | solution.py:474
  47.2 7.7 %all-to-all-start.2 = ((f32[8,72,128]{2,1,0:T(8,128)}), f32[8,72,128]{2,1,0:T(8,128)S(1)}, u32[]{:S(2)}, u32[]{:S(2)}) async-start(f32[8,72,128]{2,1,0:T(8,128)} %get-tuple-element.42), calls=%async_computation.2 | async-start | bytes 589824 | tf_op jit(solution)/shard_map/all_to_all | solution.py:486
  54.9 2.6 %collective-permute-start.1 = (f32[2,128]{1,0:T(2,128)S(1)}, f32[2,128]{1,0:T(2,128)S(1)}, u32[]{:S(2)}, u32[]{:S(2)}) collective-permute-start(f32[2,128]{1,0:T(2,128)S(1)} %get-tuple-element.50), channel_id=1, source_target_pairs={{8,16},{16,8},{9,17},{17,9},{10,18},{18,10},{11,19},{19,11},{12,20... | collective-permute-start | bytes 3080 | tf_op jit(solution)/shard_map/ppermute | solution.py:534
  57.5 3.8 %shard_map.88 = (f32[2,16,128]{2,1,0:T(8,128)S(1)}, f32[16,128]{1,0:T(8,128)S(1)}, f32[16,64]{1,0:T(8,128)S(1)}) custom-call(f32[4,176,128]{2,1,0:T(8,128)S(1)} %all_to_all.25.obs_ref, f32[2,16,128]{2,1,0:T(8,128)S(1)} %get-tuple-element.43.g0s_ref, f32[16,128]{1,0:T(8,128)S(1)} %get-tuple-element.45.g0f_ref), custom_call_target="tpu_custom_call" | custom-call | flops 1073741824 | bytes 1048576 | tf_op jit(solution)/shard_map/pallas_call | solution.py:474
  61.3 0.0 collective-permute-done.1.hop_ref
  61.3 0.4 all-to-all-done.2.expo_ref
  61.7 3.9 %shard_map.89 = (f32[2,16,128]{2,1,0:T(8,128)S(1)}, f32[16,128]{1,0:T(8,128)S(1)}, f32[4,16,64]{2,1,0:T(8,128)S(1)}, f32[4,16,64]{2,1,0:T(8,128)S(1)}, f32[16,16,128]{2,1,0:T(8,128)S(1)}) custom-call(f32[4,176,128]{2,1,0:T(8,128)S(1)} %all_to_all.25.obs_ref, f32[8,72,128]{2,1,0:T(8,128)S(1)} %all-to-all-done.2.expo_ref, ...), custom_call_target="tpu_custom_call" | custom-call | flops 1073741824 | bytes 1048576 | tf_op jit(solution)/shard_map/pallas_call | solution.py:474
  65.6 25.0 %all_to_all.26.parts_ref = f32[16,16,128]{2,1,0:T(8,128)S(1)} all-to-all(f32[16,16,128]{2,1,0:T(8,128)S(1)} %get-tuple-element.51), channel_id=1, replica_groups=mesh['x'=4,'zl'=8,'c'=2,'y'=4,'zh'=2] {'zl','c'}, dimensions={0} | all-to-all | bytes 262144 | tf_op jit(solution)/shard_map/all_to_all | solution.py:486
  90.6 13.6 %all_to_all.27.sums_ref = f32[32,16,128]{2,1,0:T(8,128)S(1)} all-to-all(f32[32,16,128]{2,1,0:T(8,128)S(1)} %shard_map.90), channel_id=1, replica_groups=mesh['x'=4,'zl'=8,'c'=2,'y'=4,'zh'=2] {'x','c','y'}, dimensions={0} | all-to-all | bytes 524288 | tf_op jit(solution)/shard_map/all_to_all | solution.py:486
  104.2 1.0 shard_map.91
  (6 shorter events, 0.1 us)
Async XLA Ops:
  3.1 15.8 %copy-start = (f32[80,128]{1,0:T(8,128)S(1)}, f32[80,128]{1,0:T(8,128)}, u32[]{:S(2)}) copy-start(f32[80,128]{1,0:T(8,128)} %get-tuple-element.31) | copy-start | bytes 122884
  3.1 31.4 %all-to-all-start = ((f32[16,8,128]{2,1,0:T(8,128)}), f32[16,8,128]{2,1,0:T(8,128)S(1)}, u32[]{:S(2)}, u32[]{:S(2)}) async-start(f32[16,8,128]{2,1,0:T(8,128)} %get-tuple-element.37), calls=%async_computation | async-start | bytes 131072 | tf_op jit(solution)/shard_map/all_to_all | solution.py:486
  18.9 14.9 %collective-permute-start = (f32[80,128]{1,0:T(8,128)S(1)}, f32[80,128]{1,0:T(8,128)S(1)}, u32[]{:S(2)}, u32[]{:S(2)}) collective-permute-start(f32[80,128]{1,0:T(8,128)S(1)} %copy-done), channel_id=1, source_target_pairs={{0,1},{1,0},{2,3},{3,2},{4,5},{5,4},{6,7},{7,6},{8,9},{9,8},{10,11... | collective-permute-start | bytes 122888 | tf_op jit(solution)/shard_map/ppermute | solution.py:521
  47.2 14.5 %all-to-all-start.2 = ((f32[8,72,128]{2,1,0:T(8,128)}), f32[8,72,128]{2,1,0:T(8,128)S(1)}, u32[]{:S(2)}, u32[]{:S(2)}) async-start(f32[8,72,128]{2,1,0:T(8,128)} %get-tuple-element.42), calls=%async_computation.2 | async-start | bytes 589824 | tf_op jit(solution)/shard_map/all_to_all | solution.py:486
  54.9 6.4 %collective-permute-start.1 = (f32[2,128]{1,0:T(2,128)S(1)}, f32[2,128]{1,0:T(2,128)S(1)}, u32[]{:S(2)}, u32[]{:S(2)}) collective-permute-start(f32[2,128]{1,0:T(2,128)S(1)} %get-tuple-element.50), channel_id=1, source_target_pairs={{8,16},{16,8},{9,17},{17,9},{10,18},{18,10},{11,19},{19,11},{12,20... | collective-permute-start | bytes 3080 | tf_op jit(solution)/shard_map/ppermute | solution.py:534
